TPU v7x, 32 devices: a whole 2x2x4 slice. The times are simulated.
32 devices in a mesh: seq: 4 (over y, core), fsdp: 8 (over z, x).
Axes of the slice: x: 2, y: 2, z: 4, core: 2. Of those that a mesh axis runs over, the one named last changes fastest.
Arguments:
- latents: bfloat16 [8, 512, 1152], P('fsdp', 'seq'), may hold values from -6 to 6
- conditioning: float32 [8, 1152], P('fsdp'), may hold values from -6 to 6
- modulation_weight: bfloat16 [1, 1152, 6912], P(None, 'fsdp'), may hold values from -0.1875 to 0.1875
- modulation_bias: bfloat16 [1, 6912], P(None, 'fsdp'), may hold values from -3 to 3
- qkv_weight: bfloat16 [1, 1152, 3456], P(None, 'fsdp'), may hold values from -1 to 1
- qkv_bias: bfloat16 [1, 2304], P(None, 'fsdp'), may hold values from -3 to 3
- proj_weight: bfloat16 [1, 1152, 1152], P(None, 'fsdp'), may hold values from -4 to 4
- proj_bias: bfloat16 [1, 1152], P(None, 'fsdp'), may hold values from -3 to 3
- fc1_weight: bfloat16 [1, 1152, 4608], P(None, 'fsdp'), may hold values from -0.1875 to 0.1875
- fc1_bias: bfloat16 [1, 4608], P(None, 'fsdp'), may hold values from -3 to 3
- fc2_weight: bfloat16 [1, 4608, 1152], P(None, 'fsdp'), may hold values from -0.09375 to 0.09375
- fc2_bias: bfloat16 [1, 1152], P(None, 'fsdp'), may hold values from -3 to 3
- cotangent: float32 [8, 512, 1152], P('fsdp', 'seq'), may hold values from -6 to 6
Outputs:
- block_output: float32 [8, 512, 1152], P('fsdp', 'seq')
- latents_grad: float32 [8, 512, 1152], P('fsdp', 'seq')
- conditioning_grad: float32 [8, 1152], P('fsdp')
- modulation_weight_grad: float32 [1, 1152, 6912], P(None, 'fsdp')
- modulation_bias_grad: float32 [1, 6912], P(None, 'fsdp')
- qkv_weight_grad: float32 [1, 1152, 3456], P(None, 'fsdp')
- qkv_bias_grad: float32 [1, 2304], P(None, 'fsdp')
- proj_weight_grad: float32 [1, 1152, 1152], P(None, 'fsdp')
- proj_bias_grad: float32 [1, 1152], P(None, 'fsdp')
- fc1_weight_grad: float32 [1, 1152, 4608], P(None, 'fsdp')
- fc1_bias_grad: float32 [1, 4608], P(None, 'fsdp')
- fc2_weight_grad: float32 [1, 4608, 1152], P(None, 'fsdp')
- fc2_bias_grad: float32 [1, 1152], P(None, 'fsdp')
All inputs are finite; a program needn't handle non-finite values.
Results may differ from a plain program's by a relative error of at most 0.019.
Values may be sent and summed in bfloat16 or wider, within the bound.
No kernel may reach another device: no remote copies, remote signals or barrier semaphores. Data moves between devices by JAX's collectives and lax.ppermute only.
A program may use at most 256 MiB of HBM per device.

v0:
```python
import jax
import jax.numpy as jnp
from jax import lax
from jax.sharding import PartitionSpec as P

HEADS = 16
BLOCKS = 1


NORM_EPS = 1e-06


def layer_norm(hidden):
    center = hidden - jnp.mean(hidden, axis=-1, keepdims=True)
    inverse = lax.rsqrt(jnp.mean(center * center, axis=-1, keepdims=True) + NORM_EPS)
    return (center * inverse, inverse)


def norm_back(upstream, normed, inverse):
    return inverse * (
        upstream
        - jnp.mean(upstream, axis=-1, keepdims=True)
        - normed * jnp.mean(upstream * normed, axis=-1, keepdims=True)
    )


def gelu_tanh(before):
    return jax.nn.gelu(before, approximate=True)


def dot_back(left_side, weight):
    return lax.dot_general(
        left_side,
        weight,
        (((left_side.ndim - 1,), (1,)), ((), ())),
        preferred_element_type=jnp.float32,
    )


def dot_rows(left_side, right_side):
    return lax.dot_general(
        left_side, right_side, (((0, 1), (0, 1)), ((), ())), preferred_element_type=jnp.float32
    )


def split_blocks(blocked, block_count):
    shaped = blocked.reshape(
        (blocked.shape[0], block_count, blocked.shape[1] // block_count) + blocked.shape[2:]
    )
    return jnp.moveaxis(shaped, 1, 0)


def join_blocks(blocked):
    reordered = jnp.moveaxis(blocked, 0, 1)
    return reordered.reshape(
        (reordered.shape[0], reordered.shape[1] * reordered.shape[2]) + reordered.shape[3:]
    )


def attend_forward(queries, key_rows, value_rows, score_scale):
    length = queries.shape[1]
    block_count = length // min(512, length)

    def one_block(query_part):
        scores = (
            jnp.einsum("bqhd,bkhd->bhqk", query_part, key_rows, preferred_element_type=jnp.float32)
            * score_scale
        )
        row_peak = jnp.max(scores, axis=-1, keepdims=True)
        log_total = jnp.log(jnp.sum(jnp.exp(scores - row_peak), axis=-1, keepdims=True)) + row_peak
        probabilities = jnp.exp(scores - log_total).astype(jnp.bfloat16)
        mixture = jnp.einsum(
            "bhqk,bkhd->bqhd", probabilities, value_rows, preferred_element_type=jnp.float32
        )
        return (mixture.astype(jnp.bfloat16), log_total[..., 0])

    mixture, totals = lax.map(one_block, split_blocks(queries, block_count))
    return (join_blocks(mixture), totals)


def attend_backward(queries, key_rows, value_rows, attended, totals, upstream, score_scale):
    length = queries.shape[1]
    block_count = length // min(512, length)

    def one_block(running, inputs):
        key_sum, value_sum = running
        query_part, out_part, grad_part, log_total = inputs
        scores = (
            jnp.einsum("bqhd,bkhd->bhqk", query_part, key_rows, preferred_element_type=jnp.float32)
            * score_scale
        )
        probabilities = jnp.exp(scores - log_total[..., None])
        prob_low = probabilities.astype(jnp.bfloat16)
        d_probs = jnp.einsum(
            "bqhd,bkhd->bhqk", grad_part, value_rows, preferred_element_type=jnp.float32
        )
        delta = jnp.swapaxes(
            jnp.sum(grad_part.astype(jnp.float32) * out_part.astype(jnp.float32), axis=-1), 1, 2
        )
        d_scores = (probabilities * (d_probs - delta[..., None]) * score_scale).astype(jnp.bfloat16)
        d_queries = jnp.einsum(
            "bhqk,bkhd->bqhd", d_scores, key_rows, preferred_element_type=jnp.float32
        )
        key_sum = key_sum + jnp.einsum(
            "bhqk,bqhd->bkhd", d_scores, query_part, preferred_element_type=jnp.float32
        )
        value_sum = value_sum + jnp.einsum(
            "bhqk,bqhd->bkhd", prob_low, grad_part, preferred_element_type=jnp.float32
        )
        return ((key_sum, value_sum), d_queries.astype(jnp.bfloat16))

    zero_sums = jnp.zeros(key_rows.shape, jnp.float32)
    inputs = (
        split_blocks(queries, block_count),
        split_blocks(attended, block_count),
        split_blocks(upstream, block_count),
        totals,
    )
    (key_sum, value_sum), d_queries = lax.scan(one_block, (zero_sums, zero_sums), inputs)
    return (join_blocks(d_queries), key_sum.astype(jnp.bfloat16), value_sum.astype(jnp.bfloat16))


def forward_block(hidden, silu_cond, weights):
    (
        modulation_weight,
        modulation_bias,
        qkv_weight,
        qkv_bias,
        proj_weight,
        proj_bias,
        fc1_weight,
        fc1_bias,
        fc2_weight,
        fc2_bias,
    ) = weights
    images, tokens, feature_width = hidden.shape
    modulation = jnp.dot(silu_cond, modulation_weight, preferred_element_type=jnp.float32)
    modulation = modulation + modulation_bias.astype(jnp.float32)
    pieces = [
        modulation[:, None, piece_index * feature_width : (piece_index + 1) * feature_width]
        for piece_index in range(6)
    ]
    shift_attn, scale_attn, gate_attn, shift_mlp, scale_mlp, gate_mlp = pieces
    norm_attn, inv_attn = layer_norm(hidden)
    input_attn = (norm_attn * (1.0 + scale_attn) + shift_attn).astype(jnp.bfloat16)
    bias_row = qkv_bias.astype(jnp.float32)
    offsets = jnp.concatenate(
        [
            bias_row[:feature_width],
            jnp.zeros((feature_width,), jnp.float32),
            bias_row[feature_width:],
        ]
    )
    projected = jnp.dot(input_attn, qkv_weight, preferred_element_type=jnp.float32)
    packed = (projected + offsets).astype(jnp.bfloat16).reshape(images, tokens, 3, feature_width)
    spread = lax.all_to_all(packed, "seq", split_axis=3, concat_axis=1, tiled=True)
    length, group_width = (spread.shape[1], spread.shape[3])
    head_width = feature_width // HEADS
    local_heads = group_width // head_width
    score_scale = head_width ** (-0.5)
    queries = spread[:, :, 0].reshape(images, length, local_heads, head_width)
    key_rows = spread[:, :, 1].reshape(images, length, local_heads, head_width)
    value_rows = spread[:, :, 2].reshape(images, length, local_heads, head_width)
    attended, totals = attend_forward(queries, key_rows, value_rows, score_scale)
    returned = lax.all_to_all(
        attended.reshape(images, length, group_width),
        "seq",
        split_axis=1,
        concat_axis=2,
        tiled=True,
    )
    branch = jnp.dot(returned, proj_weight, preferred_element_type=jnp.float32) + proj_bias.astype(
        jnp.float32
    )
    middle = hidden + gate_attn * branch
    norm_mlp, inv_mlp = layer_norm(middle)
    input_mlp = (norm_mlp * (1.0 + scale_mlp) + shift_mlp).astype(jnp.bfloat16)
    before = jnp.dot(input_mlp, fc1_weight, preferred_element_type=jnp.float32) + fc1_bias.astype(
        jnp.float32
    )
    activated, pullback = jax.vjp(gelu_tanh, before)
    act_low = activated.astype(jnp.bfloat16)
    result = jnp.dot(act_low, fc2_weight, preferred_element_type=jnp.float32) + fc2_bias.astype(
        jnp.float32
    )
    output = middle + gate_mlp * result
    records = (
        pieces,
        norm_attn,
        inv_attn,
        input_attn,
        queries,
        key_rows,
        value_rows,
        attended,
        totals,
        returned,
        branch,
        norm_mlp,
        inv_mlp,
        input_mlp,
        pullback,
        act_low,
        result,
        score_scale,
    )
    return (output, records)


def backward_block(upstream, records, weights):
    (
        modulation_weight,
        modulation_bias,
        qkv_weight,
        qkv_bias,
        proj_weight,
        proj_bias,
        fc1_weight,
        fc1_bias,
        fc2_weight,
        fc2_bias,
    ) = weights
    (
        pieces,
        norm_attn,
        inv_attn,
        input_attn,
        queries,
        key_rows,
        value_rows,
        attended,
        totals,
        returned,
        branch,
        norm_mlp,
        inv_mlp,
        input_mlp,
        pullback,
        act_low,
        result,
        score_scale,
    ) = records
    shift_attn, scale_attn, gate_attn, shift_mlp, scale_mlp, gate_mlp = pieces
    images, tokens, feature_width = upstream.shape
    d_result = upstream * gate_mlp
    d_gate_mlp = jnp.sum(upstream * result, axis=1)
    d_result_low = d_result.astype(jnp.bfloat16)
    fc2_weight_grad = dot_rows(act_low, d_result_low)
    fc2_bias_grad = jnp.sum(d_result, axis=(0, 1))
    d_before = pullback(dot_back(d_result_low, fc2_weight))[0]
    d_before_low = d_before.astype(jnp.bfloat16)
    fc1_weight_grad = dot_rows(input_mlp, d_before_low)
    fc1_bias_grad = jnp.sum(d_before, axis=(0, 1))
    d_input_mlp = dot_back(d_before_low, fc1_weight)
    d_scale_mlp = jnp.sum(d_input_mlp * norm_mlp, axis=1)
    d_shift_mlp = jnp.sum(d_input_mlp, axis=1)
    d_middle = upstream + norm_back(d_input_mlp * (1.0 + scale_mlp), norm_mlp, inv_mlp)
    d_branch = d_middle * gate_attn
    d_gate_attn = jnp.sum(d_middle * branch, axis=1)
    d_branch_low = d_branch.astype(jnp.bfloat16)
    proj_weight_grad = dot_rows(returned, d_branch_low)
    proj_bias_grad = jnp.sum(d_branch, axis=(0, 1))
    d_attended = dot_back(d_branch_low, proj_weight).astype(jnp.bfloat16)
    head_grads = lax.all_to_all(d_attended, "seq", split_axis=2, concat_axis=1, tiled=True)
    head_grads = head_grads.reshape(queries.shape)
    d_queries, d_keys, d_values = attend_backward(
        queries, key_rows, value_rows, attended, totals, head_grads, score_scale
    )
    length = queries.shape[1]
    stacked = jnp.stack([d_queries, d_keys, d_values], axis=2).reshape(
        images, length, 3, feature_width // lax.axis_size("seq")
    )
    d_packed = lax.all_to_all(stacked, "seq", split_axis=1, concat_axis=3, tiled=True).reshape(
        images, tokens, 3 * feature_width
    )
    qkv_weight_grad = dot_rows(input_attn, d_packed)
    qkv_bias_grad = jnp.concatenate(
        [
            jnp.sum(d_packed[..., :feature_width].astype(jnp.float32), axis=(0, 1)),
            jnp.sum(d_packed[..., 2 * feature_width :].astype(jnp.float32), axis=(0, 1)),
        ]
    )
    d_input_attn = dot_back(d_packed, qkv_weight)
    d_scale_attn = jnp.sum(d_input_attn * norm_attn, axis=1)
    d_shift_attn = jnp.sum(d_input_attn, axis=1)
    d_hidden = d_middle + norm_back(d_input_attn * (1.0 + scale_attn), norm_attn, inv_attn)
    d_modulation = jnp.concatenate(
        [d_shift_attn, d_scale_attn, d_gate_attn, d_shift_mlp, d_scale_mlp, d_gate_mlp], axis=-1
    )
    cond_part = lax.dot_general(
        d_modulation,
        modulation_weight.astype(jnp.float32),
        (((1,), (1,)), ((), ())),
        precision=lax.Precision.HIGHEST,
    )
    grads = (
        qkv_weight_grad,
        qkv_bias_grad,
        proj_weight_grad,
        proj_bias_grad,
        fc1_weight_grad,
        fc1_bias_grad,
        fc2_weight_grad,
        fc2_bias_grad,
    )
    return (d_hidden, grads, d_modulation, cond_part)


def reduce_grads(grads):
    qkv_weight, qkv_bias, proj_weight, proj_bias, fc1_weight, fc1_bias, fc2_weight, fc2_bias = grads
    shares = (
        lax.psum_scatter(
            qkv_weight.astype(jnp.bfloat16), "fsdp", scatter_dimension=0, tiled=True
        ).astype(jnp.float32),
        lax.psum_scatter(
            qkv_bias.astype(jnp.bfloat16), "fsdp", scatter_dimension=0, tiled=True
        ).astype(jnp.float32),
        lax.psum_scatter(
            proj_weight.astype(jnp.bfloat16), "fsdp", scatter_dimension=0, tiled=True
        ).astype(jnp.float32),
        lax.psum_scatter(
            proj_bias.astype(jnp.bfloat16), "fsdp", scatter_dimension=0, tiled=True
        ).astype(jnp.float32),
        lax.psum_scatter(
            fc1_weight.astype(jnp.bfloat16), "fsdp", scatter_dimension=0, tiled=True
        ).astype(jnp.float32),
        lax.psum_scatter(
            fc1_bias.astype(jnp.bfloat16), "fsdp", scatter_dimension=0, tiled=True
        ).astype(jnp.float32),
        lax.psum_scatter(
            fc2_weight.astype(jnp.bfloat16), "fsdp", scatter_dimension=0, tiled=True
        ).astype(jnp.float32),
        lax.psum_scatter(
            fc2_bias.astype(jnp.bfloat16), "fsdp", scatter_dimension=0, tiled=True
        ).astype(jnp.float32),
    )
    qkv_weight, qkv_bias, proj_weight, proj_bias, fc1_weight, fc1_bias, fc2_weight, fc2_bias = (
        shares
    )
    return (
        lax.psum(qkv_weight.astype(jnp.bfloat16), "seq").astype(jnp.float32),
        lax.psum(qkv_bias.astype(jnp.bfloat16), "seq").astype(jnp.float32),
        lax.psum(proj_weight.astype(jnp.bfloat16), "seq").astype(jnp.float32),
        lax.psum(proj_bias.astype(jnp.bfloat16), "seq").astype(jnp.float32),
        lax.psum(fc1_weight.astype(jnp.bfloat16), "seq").astype(jnp.float32),
        lax.psum(fc1_bias.astype(jnp.bfloat16), "seq").astype(jnp.float32),
        lax.psum(fc2_weight.astype(jnp.bfloat16), "seq").astype(jnp.float32),
        lax.psum(fc2_bias.astype(jnp.bfloat16), "seq").astype(jnp.float32),
    )


def modulation_grads(d_modulation, silu_cond, own_rows, own_columns):
    silu_wide = silu_cond.astype(jnp.float32)
    d_all, silu_all = (
        lax.all_gather(d_modulation, ("seq", "fsdp"), axis=0, tiled=True),
        lax.all_gather(silu_wide, ("seq", "fsdp"), axis=0, tiled=True),
    )
    owner = lax.axis_index("fsdp")
    silu_own = lax.dynamic_slice_in_dim(silu_all, owner * own_rows, own_rows, 1)
    weight_grad = lax.dot_general(
        silu_own, d_all, (((0,), (0,)), ((), ())), precision=lax.Precision.HIGHEST
    )
    bias_whole = jnp.sum(d_all, axis=0)
    bias_grad = lax.dynamic_slice_in_dim(bias_whole, owner * own_columns, own_columns, 0)
    return (weight_grad, bias_grad)


def shards(
    latents,
    conditioning,
    modulation_weight,
    modulation_bias,
    qkv_weight,
    qkv_bias,
    proj_weight,
    proj_bias,
    fc1_weight,
    fc1_bias,
    fc2_weight,
    fc2_bias,
    cotangent,
):
    silu_cond = jax.nn.silu(conditioning).astype(jnp.bfloat16)
    hidden = latents.astype(jnp.float32)
    own_rows = modulation_weight.shape[1]
    own_columns = modulation_bias.shape[1]
    section_index = 0
    gathered = (
        lax.all_gather(modulation_weight[section_index], "fsdp", axis=0, tiled=True),
        lax.all_gather(modulation_bias[section_index], "fsdp", axis=0, tiled=True),
        lax.all_gather(qkv_weight[section_index], "fsdp", axis=0, tiled=True),
        lax.all_gather(qkv_bias[section_index], "fsdp", axis=0, tiled=True),
        lax.all_gather(proj_weight[section_index], "fsdp", axis=0, tiled=True),
        lax.all_gather(proj_bias[section_index], "fsdp", axis=0, tiled=True),
        lax.all_gather(fc1_weight[section_index], "fsdp", axis=0, tiled=True),
        lax.all_gather(fc1_bias[section_index], "fsdp", axis=0, tiled=True),
        lax.all_gather(fc2_weight[section_index], "fsdp", axis=0, tiled=True),
        lax.all_gather(fc2_bias[section_index], "fsdp", axis=0, tiled=True),
    )
    hidden, records = forward_block(hidden, silu_cond, gathered)
    stored = [(gathered, records)]
    gradient = cotangent
    cond_sum = jnp.zeros(conditioning.shape, jnp.float32)
    reduced = [None] * BLOCKS
    modulated = [None] * BLOCKS
    for section_index in reversed(range(BLOCKS)):
        gathered, records = stored[section_index]
        gradient, grads_full, d_modulation, cond_part = backward_block(gradient, records, gathered)
        reduced[section_index] = reduce_grads(grads_full)
        modulated[section_index] = modulation_grads(d_modulation, silu_cond, own_rows, own_columns)
        cond_sum = cond_part
    cond_sum = lax.psum(cond_sum, "seq")
    silu_pull = jax.vjp(jax.nn.silu, conditioning)[1]
    conditioning_grad = silu_pull(cond_sum)[0]
    modulation_weight_grad = jnp.stack([modulated[0][0]])
    modulation_bias_grad = jnp.stack([modulated[0][1]])
    stacked = [jnp.stack([reduced[0][piece_index]]) for piece_index in range(8)]
    (
        qkv_weight_grad,
        qkv_bias_grad,
        proj_weight_grad,
        proj_bias_grad,
        fc1_weight_grad,
        fc1_bias_grad,
        fc2_weight_grad,
        fc2_bias_grad,
    ) = stacked
    return (
        hidden,
        gradient,
        conditioning_grad,
        modulation_weight_grad,
        modulation_bias_grad,
        qkv_weight_grad,
        qkv_bias_grad,
        proj_weight_grad,
        proj_bias_grad,
        fc1_weight_grad,
        fc1_bias_grad,
        fc2_weight_grad,
        fc2_bias_grad,
    )


def solution(mesh):
    return jax.shard_map(
        shards,
        mesh=mesh,
        in_specs=(
            P("fsdp", "seq", None),
            P("fsdp", None),
            P(None, "fsdp", None),
            P(None, "fsdp"),
            P(None, "fsdp", None),
            P(None, "fsdp"),
            P(None, "fsdp", None),
            P(None, "fsdp"),
            P(None, "fsdp", None),
            P(None, "fsdp"),
            P(None, "fsdp", None),
            P(None, "fsdp"),
            P("fsdp", "seq", None),
        ),
        out_specs=(
            P("fsdp", "seq", None),
            P("fsdp", "seq", None),
            P("fsdp", None),
            P(None, "fsdp", None),
            P(None, "fsdp"),
            P(None, "fsdp", None),
            P(None, "fsdp"),
            P(None, "fsdp", None),
            P(None, "fsdp"),
            P(None, "fsdp", None),
            P(None, "fsdp"),
            P(None, "fsdp", None),
            P(None, "fsdp"),
        ),
        check_vma=False,
    )
```

profile of v0, /device:TPU:0, one launch (start us, length us, event | category | flops | bytes accessed | tf_op | source)
XLA Modules:
  0.0 1463.0 jit_solution(10484554921530424143)
XLA Ops:
  15.2 41.9 %all-reduce.10 = (bf16[2304]{0:T(1024)(128)(2,1)S(1)}, bf16[6912]{0:T(1024)(128)(2,1)S(1)}, bf16[1152]{0:T(1024)(128)(2,1)S(1)}, bf16[1152]{0:T(1024)(128)(2,1)S(1)}, bf16[4608]{0:T(1024)(128)(2,1)S(1)}) all-reduce(bf16[2304]{0:T(1024)(128)(2,1)S(1)} %dynamic-update-slice.1, ...), channel_id=5, replica_groups=mesh['seq'=4,'fsdp'=8] {'fsdp'}, use_global_device_ids=true, to_apply=%add.1 | all-reduce | flops 16128 | bytes 64512
  58.2 172.7 %all-gather.18.cloned.1.call-done = bf16[1,1152,6912]{2,1,0:T(8,128)(2,1)} async-done(((bf16[1,144,6912]{2,1,0:T(8,128)(2,1)}), bf16[1,1152,6912]{2,1,0:T(8,128)(2,1)}) %all-gather.18.cloned.1.call-update) | async-done | bytes 15925264 | tf_op jit(solution)/shard_map/all_gather | solution.py:389
  230.9 7.7 fusion.50
  238.8 111.6 %all-gather.20.cloned.1.call-done = bf16[1,1152,3456]{2,1,0:T(8,128)(2,1)} async-done(((bf16[1,144,3456]{2,1,0:T(8,128)(2,1)}), bf16[1,1152,3456]{2,1,0:T(8,128)(2,1)}) %all-gather.20.cloned.1.call-update) | async-done | bytes 7962640 | tf_op jit(solution)/shard_map/all_gather | solution.py:391
  350.4 4.7 fusion.22
  356.2 5.5 copy.56
  361.7 18.7 %all_to_all.63 = bf16[1,128,3,1152]{1,2,0,3:T(4,128)(2,1)S(1)} all-to-all(bf16[1,128,3,1152]{1,2,0,3:T(4,128)(2,1)S(1)} %copy.56), channel_id=1, replica_groups=mesh['seq'=4,'fsdp'=8] {'seq'}, dimensions={3} | all-to-all | bytes 1769472 | tf_op jit(solution)/shard_map/all_to_all | solution.py:156
  385.2 3.2 reduce.53
  389.6 3.5 all-to-all-start.1
  393.7 5.7 all-to-all-done.1
  401.4 4.3 all-gather.22.cloned.1.call-done
  405.8 3.2 fusion.106
  409.2 149.3 %all-gather.24.cloned.1.call-done = bf16[1,1152,4608]{2,1,0:T(8,128)(2,1)} async-done(((bf16[1,144,4608]{2,1,0:T(8,128)(2,1)}), bf16[1,1152,4608]{2,1,0:T(8,128)(2,1)}) %all-gather.24.cloned.1.call-update) | async-done | bytes 10616848 | tf_op jit(solution)/shard_map/all_gather | solution.py:395
  558.6 5.8 fusion.16
  564.4 146.6 %all-gather.26.cloned.1.call-done = bf16[1,4608,1152]{2,1,0:T(8,128)(2,1)} async-done(((bf16[1,576,1152]{2,1,0:T(8,128)(2,1)}), bf16[1,4608,1152]{2,1,0:T(8,128)(2,1)}) %all-gather.26.cloned.1.call-update) | async-done | bytes 10616848 | tf_op jit(solution)/shard_map/all_gather | solution.py:397
  710.9 8.9 fusion.109
  719.8 4.0 fusion.70
  724.5 7.9 multiply_reduce_fusion.4
  732.5 3.6 convolution_convert_fusion.3
  736.3 2.7 fusion.47
  740.5 6.8 reduce.54
  747.4 8.9 all_to_all.64
  757.1 3.3 convolution_convert_fusion.4
  760.4 1.8 copy.72
  762.6 3.6 multiply_convert_fusion
  767.7 2.8 copy.71
  771.7 2.4 copy.70
  774.0 4.0 pad_maximum_fusion
  778.0 22.7 %all_to_all.65 = bf16[1,512,3,288]{3,2,0,1:T(4,128)(2,1)S(1)} all-to-all(bf16[1,512,3,288]{3,2,0,1:T(4,128)(2,1)S(1)} %pad_maximum_fusion), channel_id=1, replica_groups=mesh['seq'=4,'fsdp'=8] {'seq'}, dimensions={1} | all-to-all | bytes 1769472 | tf_op jit(solution)/shard_map/all_to_all | solution.py:273
  800.7 2.3 copy.81
  804.4 5.6 convolution_convert_fusion.2
  811.2 5.9 convolution_convert_fusion.1
  818.8 6.7 convolution_convert_fusion
  827.6 69.1 %all-gather.10 = f32[32,1,1152]{2,1,0:T(1,128)S(1)} all-gather(f32[1,1,1152]{2,1,0:T(1,128)S(1)} %copy-done.42), channel_id=1, replica_groups=mesh['seq'=4,'fsdp'=8] {'seq','fsdp'}, dimensions={0}, use_global_device_ids=true | all-gather | bytes 152064 | tf_op jit(solution)/shard_map/all_gather | solution.py:356
  896.9 6.0 fusion.67
  903.1 15.2 %fusion = f32[1,1152]{1,0:T(1,128)S(1)} fusion(bf16[1,1152,6912]{2,1,0:T(8,128)(2,1)} %all-gather.18.cloned.1.call-done, f32[1,6912]{1,0:T(1,128)S(1)} %constant_dynamic-update-slice_fusion), kind=kOutput, calls=%fused_computation.2 | convolution fusion | flops 95551488 | bytes 15957504 | tf_op jit(solution)/shard_map/dot_general | solution.py:290
  918.3 35.2 %reduce-scatter.5.cloned.1.call-done = bf16[144,3456]{1,0:T(8,128)(2,1)} async-done(((bf16[1152,3456]{1,0:T(8,128)(2,1)}), bf16[144,3456]{1,0:T(8,128)(2,1)}) %reduce-scatter.5.cloned.1.call-update) | async-done | bytes 995344 | tf_op jit(solution)/shard_map/reduce_scatter | solution.py:312
  953.5 182.8 %reduce-scatter.9.cloned.1.call-done = bf16[144,4608]{1,0:T(8,128)(2,1)} async-done(((bf16[1152,4608]{1,0:T(8,128)(2,1)}), bf16[144,4608]{1,0:T(8,128)(2,1)}) %reduce-scatter.9.cloned.1.call-update) | async-done | bytes 1327120 | tf_op jit(solution)/shard_map/reduce_scatter | solution.py:324
  1136.3 182.8 %reduce-scatter.11.cloned.1.call-done = bf16[576,1152]{1,0:T(8,128)(2,1)} async-done(((bf16[4608,1152]{1,0:T(8,128)(2,1)}), bf16[576,1152]{1,0:T(8,128)(2,1)}) %reduce-scatter.11.cloned.1.call-update) | async-done | bytes 1327120 | tf_op jit(solution)/shard_map/reduce_scatter | solution.py:330
  1319.1 72.6 %all-gather.11 = f32[32,1,6912]{2,1,0:T(1,128)S(1)} all-gather(f32[1,1,6912]{2,1,0:T(1,128)S(1)} %bitcast.237), channel_id=1, replica_groups=mesh['seq'=4,'fsdp'=8] {'seq','fsdp'}, dimensions={0}, use_global_device_ids=true | all-gather | bytes 912384 | tf_op jit(solution)/shard_map/all_gather | solution.py:355
  1393.2 33.3 %all-reduce.9 = (bf16[2304]{0:T(1024)(128)(2,1)S(1)}, bf16[1152]{0:T(1024)(128)(2,1)S(1)}, bf16[4608]{0:T(1024)(128)(2,1)S(1)}, bf16[1152]{0:T(1024)(128)(2,1)S(1)}) all-reduce(bf16[2304]{0:T(1024)(128)(2,1)S(1)} %pad_maximum_fusion.2, bf16[1152]{0:T(1024)(128)(2,1)S(1)} %copy-done.54, ...), channel_id=13, replica_groups=mesh['seq'=4,'fsdp'=8] {'fsdp'}, use_global_device_ids=true, to_apply=%region_23.24.clone | all-reduce | flops 9216 | bytes 36864
  1426.9 5.8 all-reduce.11
  1435.0 5.8 psum.63
  1440.8 5.2 convolution_bitcast_fusion
  1446.7 2.1 fusion.66
  1448.8 2.7 stack.72
  1452.5 1.8 stack.80
  1454.2 1.7 stack.84
  (236 shorter events, 32.7 us)
Async XLA Ops:
  7.2 223.7 %all-gather.18.cloned.1.call-start = ((), (), s32[]{:S(2)}) async-start(), calls=%async_computation.12 | async-start | bytes 17915904 | tf_op jit(solution)/shard_map/all_gather | solution.py:389
  7.9 4.7 copy-start.59
  8.0 5.4 copy-start.60
  8.0 5.4 copy-start.56
  8.0 49.2 %copy-start.2 = (bf16[1,128,1152]{2,1,0:T(8,128)(2,1)S(1)}, bf16[1,128,1152]{2,1,0:T(8,128)(2,1)}, u32[]{:S(2)}) copy-start(bf16[1,128,1152]{2,1,0:T(8,128)(2,1)} %param.13) | copy-start | bytes 884740
  8.0 49.6 %copy-start.31 = (f32[1,1152]{1,0:T(1,128)S(1)}, f32[1,1152]{1,0:T(1,128)}, u32[]{:S(2)}) copy-start(f32[1,1152]{1,0:T(1,128)} %param.14) | copy-start | bytes 13828
  8.0 342.4 %all-gather.20.cloned.1.call-start = ((), (), s32[]{:S(2)}) async-start(), calls=%async_computation.13 | async-start | bytes 8957952 | tf_op jit(solution)/shard_map/all_gather | solution.py:391
  8.7 397.0 %all-gather.22.cloned.1.call-start = ((), (), s32[]{:S(2)}) async-start(), calls=%async_computation.14 | async-start | bytes 2985984 | tf_op jit(solution)/shard_map/all_gather | solution.py:393
  9.5 549.1 %all-gather.24.cloned.1.call-start = ((), (), s32[]{:S(2)}) async-start(), calls=%async_computation.15 | async-start | bytes 11943936 | tf_op jit(solution)/shard_map/all_gather | solution.py:395
  10.1 700.8 %all-gather.26.cloned.1.call-start = ((), (), s32[]{:S(2)}) async-start(), calls=%async_computation.16 | async-start | bytes 11943936 | tf_op jit(solution)/shard_map/all_gather | solution.py:397
  57.3 293.1 %copy-start.39 = (f32[128]{0:T(128)}, f32[128]{0:T(128)S(1)}, u32[]{:S(2)}) copy-start(f32[128]{0:T(128)S(1)} %broadcast_multiply_fusion.5) | copy-start | bytes 1540
  57.6 292.8 %copy-start.43 = (f32[128]{0:T(128)}, f32[128]{0:T(128)S(1)}, u32[]{:S(2)}) copy-start(f32[128]{0:T(128)S(1)} %add_rsqrt_fusion.1) | copy-start | bytes 1540
  58.2 180.4 %copy-start.33 = (f32[1,1152]{1,0:T(1,128)}, f32[1,1152]{1,0:T(1,128)S(1)}, u32[]{:S(2)}) copy-start(f32[1,1152]{1,0:T(1,128)S(1)} %get-tuple-element.101) | copy-start | bytes 13828
  238.8 116.4 %copy-start.26 = (f32[1152]{0:T(1024)}, f32[1152]{0:T(1024)S(1)}, u32[]{:S(2)}) copy-start(f32[1152]{0:T(1024)S(1)} %get-tuple-element.78) | copy-start | bytes 13828
  238.8 319.8 %copy-start.24 = (f32[1152]{0:T(1024)}, f32[1152]{0:T(1024)S(1)}, u32[]{:S(2)}) copy-start(f32[1152]{0:T(1024)S(1)} %get-tuple-element.76) | copy-start | bytes 13828
  238.8 485.7 %copy-start.28 = (f32[1152]{0:T(1024)}, f32[1152]{0:T(1024)S(1)}, u32[]{:S(2)}) copy-start(f32[1152]{0:T(1024)S(1)} %get-tuple-element.80) | copy-start | bytes 13828
  238.8 485.7 %copy-start.35 = (f32[1152]{0:T(1024)}, f32[1152]{0:T(1024)S(1)}, u32[]{:S(2)}) copy-start(f32[1152]{0:T(1024)S(1)} %get-tuple-element.75) | copy-start | bytes 13828
  383.5 17.8 %copy-start.14 = (bf16[4,72,512]{2,1,0:T(8,128)(2,1)}, bf16[4,72,512]{2,1,0:T(8,128)(2,1)S(1)}, u32[]{:S(2)}) copy-start(bf16[4,72,512]{2,1,0:T(8,128)(2,1)S(1)} %convolution_convert_fusion.7) | copy-start | bytes 884740
  389.6 9.8 all-to-all-start.1
  393.1 525.2 %reduce-scatter.7.cloned.1.call-start = ((), (), s32[]{:S(2)}) async-start(), calls=%async_computation.9 | async-start | bytes 2985984 | tf_op jit(solution)/shard_map/reduce_scatter | solution.py:318
  401.4 7.8 copy-start.8
  409.0 315.5 %copy-start.46 = (f32[128]{0:T(128)}, f32[128]{0:T(128)S(1)}, u32[]{:S(2)}) copy-start(f32[128]{0:T(128)S(1)} %broadcast_multiply_fusion.4) | copy-start | bytes 1540
  409.2 315.3 %copy-start.48 = (f32[128]{0:T(128)}, f32[128]{0:T(128)S(1)}, u32[]{:S(2)}) copy-start(f32[128]{0:T(128)S(1)} %add_rsqrt_fusion) | copy-start | bytes 1540
  564.3 160.2 %copy-start.3 = (f32[128,4608]{1,0:T(8,128)}, f32[128,4608]{1,0:T(8,128)S(1)}, u32[]{:S(2)}) copy-start(f32[128,4608]{1,0:T(8,128)S(1)} %fusion.16) | copy-start | bytes 7077892
  710.9 8.9 copy-start.1
  719.8 4.0 copy-start.6
  719.8 4.7 copy-start.21
  719.8 4.7 copy-start.22
  724.5 8.0 copy-start.9
  732.5 3.8 copy-start.5
  736.1 217.4 %reduce-scatter.5.cloned.1.call-start = ((), (), s32[]{:S(2)}) async-start(), calls=%async_computation.8 | async-start | bytes 8957952 | tf_op jit(solution)/shard_map/reduce_scatter | solution.py:312
  747.4 9.7 copy-start.30
  757.1 5.3 copy-start.15
  766.2 4.2 copy-start.11
  810.0 326.3 %reduce-scatter.9.cloned.1.call-start = ((), (), s32[]{:S(2)}) async-start(), calls=%async_computation.10 | async-start | bytes 11943936 | tf_op jit(solution)/shard_map/reduce_scatter | solution.py:324
  817.1 502.0 %reduce-scatter.11.cloned.1.call-start = ((), (), s32[]{:S(2)}) async-start(), calls=%async_computation.11 | async-start | bytes 11943936 | tf_op jit(solution)/shard_map/reduce_scatter | solution.py:330
  825.5 71.3 %copy-start.41 = (f32[128]{0:T(128)S(1)}, f32[128]{0:T(128)}, u32[]{:S(2)}) copy-start(f32[128]{0:T(128)} %copy-done.39) | copy-start | bytes 1540
  825.5 71.3 %copy-start.45 = (f32[128]{0:T(128)S(1)}, f32[128]{0:T(128)}, u32[]{:S(2)}) copy-start(f32[128]{0:T(128)} %copy-done.43) | copy-start | bytes 1540
  825.6 623.3 %all-reduce.15.cloned.1.call-start = ((), (), s32[]{:S(2)}) async-start(), calls=%async_computation.17 | async-start | bytes 7962624 | tf_op jit(solution)/shard_map/psum | solution.py:341
  896.8 6.2 copy-start.52
  896.8 6.2 copy-start.37
  896.8 6.2 copy-start.38
  896.8 6.2 copy-start.51
  1319.1 74.1 %copy-start.50 = (bf16[4608]{0:T(1024)(128)(2,1)S(1)}, bf16[4608]{0:T(1024)(128)(2,1)}, u32[]{:S(2)}) copy-start(bf16[4608]{0:T(1024)(128)(2,1)} %get-tuple-element.119) | copy-start | bytes 27652
  1319.1 74.1 %copy-start.53 = (bf16[1152]{0:T(1024)(128)(2,1)S(1)}, bf16[1152]{0:T(1024)(128)(2,1)}, u32[]{:S(2)}) copy-start(bf16[1152]{0:T(1024)(128)(2,1)} %get-tuple-element.67) | copy-start | bytes 6916
  1319.1 74.1 %copy-start.54 = (bf16[1152]{0:T(1024)(128)(2,1)S(1)}, bf16[1152]{0:T(1024)(128)(2,1)}, u32[]{:S(2)}) copy-start(bf16[1152]{0:T(1024)(128)(2,1)} %get-tuple-element.110) | copy-start | bytes 6916
  1440.8 5.3 copy-start.32
  1440.8 5.3 copy-start.34
  (24 other events, 54.3 us)
Sparse Core Ops, SparseCore 0:
  10.2 220.6 all-gather.17
  233.1 117.2 all-gather.19
  352.6 53.1 all-gather.21
  407.8 150.6 all-gather.23
  560.6 150.2 all-gather.25
  736.2 69.9 reduce-scatter.6
  810.1 143.3 reduce-scatter.4
  957.1 179.1 reduce-scatter.8
  1139.9 179.1 reduce-scatter.10
  1321.6 85.2 all-reduce.14
where the time goes:
time: 1470 us; the launch traced here: 1460 us
  waiting for transfers between devices  994 us (68%)
  blocking collectives  279 us (19%)
  matrix products  104 us (7%)
  local copies, waits for them, and re-layouts  31.4 us (2%)
  other arithmetic  29.8 us (2%)
  between operations  20 us (1%)
    reduce_scatter x1, waiting for transfers between devices, reduce_grads(): lax.psum_scatter(fc2_weight.astype(jnp.bfloat16), 'fsdp', scatter_dimensi...  183 us
    reduce_scatter x1, waiting for transfers between devices, reduce_grads(): lax.psum_scatter(fc1_weight.astype(jnp.bfloat16), 'fsdp', scatter_dimensi...  183 us
    all_gather x1, waiting for transfers between devices, shards(): lax.all_gather(modulation_weight[section_index], 'fsdp', axis=0, tiled=True)  173 us
    all_gather x1, waiting for transfers between devices, shards(): lax.all_gather(fc1_weight[section_index], 'fsdp', axis=0, tiled=True)  149 us
    all_gather x1, waiting for transfers between devices, shards(): lax.all_gather(fc2_weight[section_index], 'fsdp', axis=0, tiled=True)  147 us
    all_gather x1, waiting for transfers between devices, shards(): lax.all_gather(qkv_weight[section_index], 'fsdp', axis=0, tiled=True)  112 us
    unnamed x2, blocking collectives  75.2 us
    all_gather x1, blocking collectives, modulation_grads(): lax.all_gather(d_modulation, ('seq', 'fsdp'), axis=0, tiled=True)  72.6 us
  transfers between devices with their start and end apart: 11, of which 9 were waited for; matrix products, arithmetic and copies ran while one was open for 9% of the time, Pallas kernels for 0%

commit v1 on v0

v1 whole, which is shorter than its diff:
```python
import jax
import jax.numpy as jnp
from jax import lax
from jax.experimental import pallas as pl
from jax.experimental.pallas import tpu as pltpu
from jax.sharding import PartitionSpec as P


HEADS = 16
NORM_EPS = 1e-06


def layer_norm(hidden):
    center = hidden - jnp.mean(hidden, axis=-1, keepdims=True)
    inverse = lax.rsqrt(jnp.mean(center * center, axis=-1, keepdims=True) + NORM_EPS)
    return (center * inverse, inverse)


def norm_back(upstream, normed, inverse):
    return inverse * (
        upstream
        - jnp.mean(upstream, axis=-1, keepdims=True)
        - normed * jnp.mean(upstream * normed, axis=-1, keepdims=True)
    )


def gelu_tanh(before):
    return jax.nn.gelu(before, approximate=True)


def dot(left, right):
    return jnp.dot(left, right, preferred_element_type=jnp.float32)


def dot_back(left, weight):
    return lax.dot_general(
        left, weight, (((left.ndim - 1,), (1,)), ((), ())), preferred_element_type=jnp.float32
    )


def dot_rows(left, right):
    return lax.dot_general(left, right, (((0,), (0,)), ((), ())), preferred_element_type=jnp.float32)


def swap(value, axis, mask):
    pairs = [(i, i ^ mask) for i in range(lax.axis_size(axis))]
    return lax.ppermute(value, axis, pairs)


def bits_of(size):
    bits = []
    step = 1
    while step < size:
        bits.append(step)
        step *= 2
    return bits


def seq_gather(value):
    near = swap(value, "seq", 1)
    far = swap(value, "seq", 2)
    both = swap(far, "seq", 1)
    return jnp.concatenate([value, near, far, both], axis=0)


def seq_blocks(block):
    low = block.astype(jnp.bfloat16)
    return seq_gather(low).reshape((-1,) + low.shape)


def seq_exchange(blocks):
    if blocks.shape[0] == 1:
        return blocks
    pairs = blocks.reshape((-1, 2) + blocks.shape[1:])
    near = swap(pairs[:, 1], "seq", 1)
    kept = jnp.stack([pairs[:, 0], near], axis=1)
    far = swap(kept[1], "seq", 2)
    return jnp.concatenate([kept[0], far], axis=0)


def seq_reduce(partial):
    size = lax.axis_size("seq")
    rows = partial.shape[0] // size
    for mask in bits_of(size):
        count = partial.shape[0] // rows
        blocks = partial.reshape((count // 2, 2) + (rows,) + partial.shape[1:])
        kept, sent = blocks[:, 0], blocks[:, 1]
        received = swap(sent.astype(jnp.bfloat16), "seq", mask)
        partial = (kept + received.astype(jnp.float32)).reshape((-1,) + partial.shape[1:])
    return partial


def tie(*values):
    return lax.optimization_barrier(values)


def reduce_near(partial):
    size = lax.axis_size("fsdp")
    near = lax.axis_index("fsdp") % 2
    rows = partial.shape[0] // size
    blocks = partial.astype(jnp.bfloat16).reshape((size // 2, 2, rows) + partial.shape[1:])
    kept = lax.dynamic_index_in_dim(blocks, near, 1, keepdims=False)
    sent = lax.dynamic_index_in_dim(blocks, 1 - near, 1, keepdims=False)
    return (kept, swap(sent, "fsdp", 1))


def reduce_far(kept, received):
    far = lax.axis_index("fsdp") // 2
    pair = kept.astype(jnp.float32) + received.astype(jnp.float32)
    total = lax.dynamic_index_in_dim(pair, far, 0, keepdims=False)
    low = pair.astype(jnp.bfloat16)
    for k in range(1, pair.shape[0]):
        piece = lax.dynamic_index_in_dim(low, far ^ k, 0, keepdims=False)
        total = total + swap(piece, "fsdp", 2 * k).astype(jnp.float32)
    return total


def lanes(columns):
    return -(-columns // 128) * 128


def in_vmem(count):
    return [pl.BlockSpec(memory_space=pltpu.VMEM) for _ in range(count)]


def own_columns_of(whole, part, groups, parts):
    span = whole.shape[1] // (groups * parts)
    starts = [(group * parts + part) * span for group in range(groups)]
    return [whole[:, start : start + span] for start in starts]


def take_attention(qkv, proj, index, parts):
    rows = qkv.shape[0]
    used = qkv.shape[1] // parts
    columns = lanes(used) + proj.shape[1] // parts

    def kernel(at_ref, qkv_ref, proj_ref, target):
        for part in range(parts):

            @pl.when(at_ref[0] == part)
            def _():
                pieces = own_columns_of(qkv_ref[...], part, 3, parts)
                pieces.append(jnp.zeros((rows, lanes(used) - used), qkv.dtype))
                pieces += own_columns_of(proj_ref[...], part, 1, parts)
                target[...] = jnp.concatenate(pieces, axis=1)

    return pl.pallas_call(
        kernel,
        out_shape=jax.ShapeDtypeStruct((rows, columns), qkv.dtype),
        in_specs=[pl.BlockSpec(memory_space=pltpu.SMEM)] + in_vmem(2),
        out_specs=in_vmem(1)[0],
        name="take_attention",
    )(index.reshape(1), qkv, proj)


def take_feed_forward(fc1, fc2, index, groups, parts):
    rows, width = fc1.shape[0], fc2.shape[1]
    quarter = fc2.shape[0] // parts

    def kernel(at_ref, fc1_ref, fc2_ref, target):
        for part in range(parts):

            @pl.when(at_ref[0] == part)
            def _():
                pieces = own_columns_of(fc1_ref[...], part, groups, parts)
                target[0] = jnp.concatenate(pieces, axis=1)
                target[1] = fc2_ref[part * quarter : (part + 1) * quarter]

    return pl.pallas_call(
        kernel,
        out_shape=jax.ShapeDtypeStruct((2, rows, width), fc1.dtype),
        in_specs=[pl.BlockSpec(memory_space=pltpu.SMEM)] + in_vmem(2),
        out_specs=in_vmem(1)[0],
        name="take_feed_forward",
    )(index.reshape(1), fc1, fc2)


def pack_near(grad, blocks, index, near, devices):
    group = blocks.shape[1]
    rows, used = grad.shape[0] // devices, grad.shape[1]
    shape = (devices // 2, rows, used + blocks.shape[2])

    def kernel(at_ref, grad_ref, blocks_ref, kept_ref, sent_ref):
        for side in range(2):

            @pl.when(at_ref[1] == side)
            def _():
                for owner in range(devices):
                    target = kept_ref if owner % 2 == side else sent_ref
                    part, start = divmod(owner * rows, group)
                    target[owner // 2, :, :used] = grad_ref[owner * rows : (owner + 1) * rows]
                    target[owner // 2, :, used:] = blocks_ref[at_ref[0] ^ part][start : start + rows]

    return pl.pallas_call(
        kernel,
        out_shape=[jax.ShapeDtypeStruct(shape, grad.dtype)] * 2,
        in_specs=[pl.BlockSpec(memory_space=pltpu.SMEM)] + in_vmem(2),
        out_specs=in_vmem(2),
        name="pack_near",
    )(jnp.stack([index, near]), grad, blocks)


def split_columns(whole, index, parts):
    rows, columns = whole.shape
    span = columns // parts

    def kernel(at_ref, source, target):
        for own in range(parts):

            @pl.when(at_ref[0] == own)
            def _():
                values = source[...]
                for part in range(parts):
                    start = (own ^ part) * span
                    target[part] = values[:, start : start + span]

    return pl.pallas_call(
        kernel,
        out_shape=jax.ShapeDtypeStruct((parts, rows, span), whole.dtype),
        in_specs=[pl.BlockSpec(memory_space=pltpu.SMEM)] + in_vmem(1),
        out_specs=in_vmem(1)[0],
        name="split_columns",
    )(index.reshape(1), whole)


def join_columns(blocks, index, groups, dtype):
    parts, rows, columns = blocks.shape
    span = columns // groups

    def kernel(at_ref, source, target):
        own = at_ref[0]
        wholes = [source[own ^ part].astype(dtype) for part in range(parts)]
        pieces = []
        for group in range(groups):
            for part in range(parts):
                pieces.append(wholes[part][:, group * span : (group + 1) * span])
        target[...] = jnp.concatenate(pieces, axis=1)

    return pl.pallas_call(
        kernel,
        out_shape=jax.ShapeDtypeStruct((rows, parts * columns), dtype),
        in_specs=[pl.BlockSpec(memory_space=pltpu.SMEM)] + in_vmem(1),
        out_specs=in_vmem(1)[0],
        name="join_columns",
    )(index.reshape(1), blocks)


def join_attention(blocks, index, span):
    parts, rows, columns = blocks.shape
    starts = [0, span, 2 * span, columns - span]

    def kernel(at_ref, source, qkv_ref, proj_ref):
        own = at_ref[0]
        wholes = [source[own ^ part].astype(jnp.float32) for part in range(parts)]
        pieces = []
        for start in starts:
            for part in range(parts):
                pieces.append(wholes[part][:, start : start + span])
        qkv_ref[...] = jnp.concatenate(pieces[: 3 * parts], axis=1)
        proj_ref[...] = jnp.concatenate(pieces[3 * parts :], axis=1)

    return pl.pallas_call(
        kernel,
        out_shape=[
            jax.ShapeDtypeStruct((rows, 3 * parts * span), jnp.float32),
            jax.ShapeDtypeStruct((rows, parts * span), jnp.float32),
        ],
        in_specs=[pl.BlockSpec(memory_space=pltpu.SMEM)] + in_vmem(1),
        out_specs=in_vmem(2),
        name="join_attention",
    )(index.reshape(1), blocks)


def join_rows(blocks, index, dtype):
    parts, rows, columns = blocks.shape

    def kernel(at_ref, source, target):
        for part in range(parts):
            target[part * rows : (part + 1) * rows] = source[at_ref[0] ^ part].astype(dtype)

    return pl.pallas_call(
        kernel,
        out_shape=jax.ShapeDtypeStruct((parts * rows, columns), dtype),
        in_specs=[pl.BlockSpec(memory_space=pltpu.SMEM)] + in_vmem(1),
        out_specs=in_vmem(1)[0],
        name="join_rows",
    )(index.reshape(1), blocks)


def small_gather(row, axis):
    own = lax.axis_index(axis)
    rows = row
    for mask in bits_of(lax.axis_size(axis)):
        other = swap(rows, axis, mask)
        upper = (own & mask) != 0
        rows = jnp.concatenate(
            [jnp.where(upper, other, rows), jnp.where(upper, rows, other)], axis=0
        )
    return rows


def small_reduce(rows, axis):
    own = lax.axis_index(axis)
    for mask in reversed(bits_of(lax.axis_size(axis))):
        half = rows.shape[0] // 2
        upper = (own & mask) != 0
        kept = jnp.where(upper, rows[half:], rows[:half])
        sent = jnp.where(upper, rows[:half], rows[half:])
        rows = kept + swap(sent, axis, mask)
    return rows


def seq_sum(value):
    for mask in bits_of(lax.axis_size("seq")):
        value = value + swap(value, "seq", mask)
    return value


def shards(
    latents,
    conditioning,
    modulation_weight,
    modulation_bias,
    qkv_weight,
    qkv_bias,
    proj_weight,
    proj_bias,
    fc1_weight,
    fc1_bias,
    fc2_weight,
    fc2_bias,
    cotangent,
):
    f32, bf16 = jnp.float32, jnp.bfloat16
    seq, fsdp = lax.axis_size("seq"), lax.axis_size("fsdp")
    s, f = lax.axis_index("seq"), lax.axis_index("fsdp")
    hidden = latents[0].astype(f32)
    upstream = cotangent[0]
    width = hidden.shape[1]
    group = width // seq
    head_width = width // HEADS
    local_heads = HEADS // seq
    rows = qkv_weight.shape[1]
    unit_rows = fc2_weight.shape[1]
    quarter = unit_rows // seq
    units = quarter * fsdp
    score_scale = head_width ** (-0.5)

    silu_cond = jax.nn.silu(conditioning).astype(bf16)
    shorts = [silu_cond, qkv_bias, proj_bias, fc1_bias, fc2_bias]
    gathered = small_gather(jnp.concatenate(shorts, axis=1), "fsdp")
    split = []
    at = 0
    for short in shorts:
        split.append(gathered[:, at : at + short.shape[1]])
        at += short.shape[1]
    silu_all = split[0]
    qkv_offset, proj_offset, fc1_offset, fc2_offset = [
        part.astype(f32).reshape(1, -1) for part in split[1:]
    ]

    attention_own = take_attention(qkv_weight[0], proj_weight[0], s, seq)
    attention_full = lax.all_gather(attention_own, "fsdp", axis=0, tiled=True)
    padded = lanes(3 * group)
    qkv_full = attention_full[:, :padded]
    proj_blocks = attention_full[:, padded:].reshape(seq, group, group)
    proj_blocks = jnp.stack(
        [lax.dynamic_index_in_dim(proj_blocks, s ^ k, 0, keepdims=False) for k in range(seq)]
    )
    proj_full = join_columns(seq_exchange(proj_blocks), s, 1, bf16)
    forward_own = take_feed_forward(fc1_weight[0], fc2_weight[0], s, fsdp, seq)

    silu_own = lax.dynamic_slice_in_dim(silu_all, f * rows, rows, 1)
    partial = dot(silu_own, modulation_weight[0])
    bias_row = lax.dynamic_update_slice_in_dim(
        jnp.zeros((1, 6 * width), f32),
        modulation_bias.astype(f32),
        f * modulation_bias.shape[1],
        1,
    )
    modulation = small_reduce(partial + bias_row, "fsdp")
    shift_attn, scale_attn, gate_attn, shift_mlp, scale_mlp, gate_mlp = [
        modulation[:, at * width : (at + 1) * width] for at in range(6)
    ]

    norm_attn, inv_attn = layer_norm(hidden)
    low_attn = (norm_attn * (1.0 + scale_attn) + shift_attn).astype(bf16)
    low_attn, forward_own = tie(low_attn, forward_own)
    input_attn = seq_gather(low_attn)
    forward_full = lax.all_gather(forward_own, "fsdp", axis=1, tiled=True)
    fc1_full, fc2_full = forward_full[0], forward_full[1]
    d_result = upstream * gate_mlp
    low_result, packed_weight = tie(d_result.astype(bf16), qkv_full)
    d_result_low = seq_gather(low_result)

    query_bias = lax.dynamic_slice_in_dim(qkv_offset[:, :width], s * group, group, 1)
    value_bias = lax.dynamic_slice_in_dim(qkv_offset[:, width:], s * group, group, 1)
    zeros = jnp.zeros((1, group), f32)
    offsets = jnp.concatenate(
        [query_bias, zeros, value_bias, zeros[:, : padded - 3 * group]], axis=1
    )
    packed = (dot(input_attn, packed_weight) + offsets).astype(bf16)
    length = packed.shape[0]
    heads = packed[:, : 3 * group].reshape(length, 3, local_heads, head_width)
    queries, key_rows, value_rows = heads[:, 0], heads[:, 1], heads[:, 2]
    scores = (
        jnp.einsum("qhd,khd->hqk", queries, key_rows, preferred_element_type=f32) * score_scale
    )
    row_peak = jnp.max(scores, axis=-1, keepdims=True)
    log_total = jnp.log(jnp.sum(jnp.exp(scores - row_peak), axis=-1, keepdims=True)) + row_peak
    probabilities = jnp.exp(scores - log_total)
    prob_low = probabilities.astype(bf16)
    attended = jnp.einsum("hqk,khd->qhd", prob_low, value_rows, preferred_element_type=f32).astype(
        bf16
    )
    attended_flat = attended.reshape(length, group)
    branch_part = dot(attended_flat, proj_full)
    branch = seq_reduce(branch_part) + proj_offset
    middle = hidden + gate_attn * branch

    norm_mlp, inv_mlp = layer_norm(middle)
    low_mlp = (norm_mlp * (1.0 + scale_mlp) + shift_mlp).astype(bf16)
    low_mlp, d_result_low = tie(low_mlp, d_result_low)
    input_mlp = seq_gather(low_mlp)
    fc1_offset_own = lax.dynamic_index_in_dim(
        fc1_offset.reshape(fsdp, seq, quarter), s, 1, keepdims=False
    ).reshape(1, units)
    before = dot(input_mlp, fc1_full) + fc1_offset_own
    activated, pullback = jax.vjp(gelu_tanh, before)
    act_low = activated.astype(bf16)
    d_before = pullback(dot_back(d_result_low, fc2_full))[0]
    d_before_low = d_before.astype(bf16)
    fc2_near = reduce_near(dot_rows(act_low, d_result_low))
    d_input_part = dot_back(d_before_low, fc1_full)
    fc1_near = reduce_near(dot_rows(input_mlp, d_before_low))
    d_input_part, act_late = tie(d_input_part, act_low)
    d_input_mlp = seq_reduce(d_input_part)
    result = seq_reduce(dot(act_late, fc2_full)) + fc2_offset
    output = middle + gate_mlp * result
    d_gate_mlp = jnp.sum(upstream * result, axis=0, keepdims=True)
    fc2_bias_part = jnp.sum(d_result, axis=0, keepdims=True)
    fc1_bias_part = jnp.sum(d_before, axis=0, keepdims=True)
    d_scale_mlp = jnp.sum(d_input_mlp * norm_mlp, axis=0, keepdims=True)
    d_shift_mlp = jnp.sum(d_input_mlp, axis=0, keepdims=True)
    d_middle = upstream + norm_back(d_input_mlp * (1.0 + scale_mlp), norm_mlp, inv_mlp)

    d_branch = d_middle * gate_attn
    d_gate_attn = jnp.sum(d_middle * branch, axis=0, keepdims=True)
    proj_bias_part = jnp.sum(d_branch, axis=0, keepdims=True)
    low_branch = d_branch.astype(bf16)
    d_branch_low = seq_gather(low_branch)
    fc2_grad = reduce_far(*fc2_near)
    proj_grad = split_columns(dot_rows(attended_flat, d_branch_low).astype(bf16), s, seq)
    proj_grad, d_branch_low = tie(proj_grad, d_branch_low)
    proj_grad = seq_exchange(proj_grad)
    d_attended = dot_back(d_branch_low, proj_full).astype(bf16).reshape(attended.shape)
    d_probs = jnp.einsum("qhd,khd->hqk", d_attended, value_rows, preferred_element_type=f32)
    delta = jnp.sum(d_attended.astype(f32) * attended.astype(f32), axis=-1).T
    d_scores = (probabilities * (d_probs - delta[..., None]) * score_scale).astype(bf16)
    d_queries = jnp.einsum("hqk,khd->qhd", d_scores, key_rows, preferred_element_type=f32)
    d_keys = jnp.einsum("hqk,qhd->khd", d_scores, queries, preferred_element_type=f32)
    d_values = jnp.einsum("hqk,qhd->khd", prob_low, d_attended, preferred_element_type=f32)
    d_packed = jnp.concatenate(
        [grad.astype(bf16).reshape(length, group) for grad in (d_queries, d_keys, d_values)]
        + [jnp.zeros((length, padded - 3 * group), bf16)],
        axis=1,
    )
    d_input_part = dot_back(d_packed, qkv_full)
    d_input_attn = seq_reduce(d_input_part)
    fc1_grad = reduce_far(*fc1_near)
    qkv_grad = dot_rows(input_attn, d_packed).astype(bf16)
    kept, sent = pack_near(qkv_grad, proj_grad, s, f % 2, fsdp)
    attention_near = (kept, swap(sent, "fsdp", 1))
    qkv_sum = jnp.sum(d_packed.astype(f32), axis=0, keepdims=True)
    d_scale_attn = jnp.sum(d_input_attn * norm_attn, axis=0, keepdims=True)
    d_shift_attn = jnp.sum(d_input_attn, axis=0, keepdims=True)
    latents_grad = d_middle + norm_back(d_input_attn * (1.0 + scale_attn), norm_attn, inv_attn)

    sums = seq_sum(
        jnp.concatenate(
            [
                d_shift_attn,
                d_scale_attn,
                d_gate_attn,
                d_shift_mlp,
                d_scale_mlp,
                d_gate_mlp,
                proj_bias_part,
                fc2_bias_part,
            ],
            axis=1,
        )
    )
    own_columns = jnp.concatenate(
        [qkv_sum[:, :group], qkv_sum[:, 2 * group : 3 * group], fc1_bias_part], axis=1
    )
    columns = small_gather(own_columns, "seq")
    query_sum = columns[:, :group].reshape(1, -1)
    value_sum = columns[:, group : 2 * group].reshape(1, -1)
    fc1_sum = jnp.moveaxis(columns[:, 2 * group :].reshape(seq, fsdp, quarter), 0, 1).reshape(1, -1)
    every = small_gather(
        jnp.concatenate([sums, query_sum, value_sum, fc1_sum], axis=1), "fsdp"
    )
    every, kept, received = tie(every, *attention_near)
    d_modulation = every[:, : 6 * width]
    weight_grad = lax.dot_general(
        silu_own.astype(f32),
        d_modulation,
        (((0,), (0,)), ((), ())),
        precision=lax.Precision.HIGHEST,
    )
    totals = jnp.sum(every, axis=0, keepdims=True)

    def own_part(start, count):
        part = count // fsdp
        return lax.dynamic_slice_in_dim(totals[:, start : start + count], f * part, part, 1)

    modulation_bias_grad = own_part(0, 6 * width)
    proj_bias_grad = own_part(6 * width, width)
    fc2_bias_grad = own_part(7 * width, width)
    qkv_bias_grad = own_part(8 * width, 2 * width)
    fc1_bias_grad = own_part(10 * width, fc1_offset.shape[1])

    cond_rows = lax.dot_general(
        d_modulation,
        modulation_weight[0].astype(f32),
        (((1,), (1,)), ((), ())),
        precision=lax.Precision.HIGHEST,
    )
    cond_all = small_gather(cond_rows.reshape(1, -1), "fsdp").reshape(fsdp, fsdp, rows)
    cond_sum = lax.dynamic_index_in_dim(cond_all, f, 1, keepdims=False).reshape(1, width)
    conditioning_grad = jax.vjp(jax.nn.silu, conditioning)[1](cond_sum)[0]

    fc2_out = join_rows(seq_blocks(fc2_grad), s, f32)
    fc1_out = join_columns(seq_blocks(fc1_grad), s, fsdp, f32)
    attention_grad = reduce_far(kept, received)
    qkv_out, proj_out = join_attention(seq_blocks(attention_grad), s, group)
    return (
        output[None],
        latents_grad[None],
        conditioning_grad,
        weight_grad[None],
        modulation_bias_grad,
        qkv_out[None],
        qkv_bias_grad,
        proj_out[None],
        proj_bias_grad,
        fc1_out[None],
        fc1_bias_grad,
        fc2_out[None],
        fc2_bias_grad,
    )


def solution(mesh):
    tokens = P("fsdp", "seq", None)
    matrix = P(None, "fsdp", None)
    vector = P(None, "fsdp")
    cond = P("fsdp", None)
    weights = (matrix, vector) * 5

    return jax.shard_map(
        shards,
        mesh=mesh,
        in_specs=(tokens, cond) + weights + (tokens,),
        out_specs=(tokens, tokens, cond) + weights,
        check_vma=False,
    )
```

time: 1470 us -> 444 us (0.30)
  waiting for transfers between devices: 994 us -> 213 us
  blocking collectives: 279 us -> 0 us
  matrix products: 104 us -> 41.2 us
  starting transfers between devices: 4.55 us -> 53.3 us
  Pallas kernels: 0 us -> 23.6 us
  other arithmetic: 29.8 us -> 52.2 us
    all_gather x5 -> x2, waiting for transfers between devices: 585 us -> 37.9 us  [the longest x1 23.1 us: shards(): forward_full = lax.all_gather(forward_own, 'fsdp', axis=1, tiled=True)]
    reduce_scatter x4 -> x0, waiting for transfers between devices: 401 us -> none  [the longest x1 183 us: reduce_grads(): lax.psum_scatter(fc2_weight.astype(jnp.bfloat16), 'fsdp', scatter_dimensi...]
    ppermute x0 -> x61, waiting for transfers between devices: none -> 175 us  [swap(): return lax.ppermute(value, axis, pairs)]
    all_gather x2 -> x0, blocking collectives: 142 us -> none  [the longest x1 72.6 us: modulation_grads(): lax.all_gather(d_modulation, ('seq', 'fsdp'), axis=0, tiled=True)]
    unnamed x2 -> x0, blocking collectives: 75.2 us -> none
    dot_general x21, matrix products: 104 us -> 41.2 us  [the longest x5 11.2 us: dot(): return jnp.dot(left, right, preferred_element_type=jnp.float32)]
    ppermute x0 -> x61, starting transfers between devices: none -> 53.2 us  [swap(): return lax.ppermute(value, axis, pairs)]
    all_to_all x3 -> x0, blocking collectives: 50.3 us -> none  [the longest x1 22.7 us: backward_block(): lax.all_to_all(stacked, 'seq', split_axis=1, concat_axis=3, tiled=True)]
  transfers between devices with their start and end apart: 11 -> 63, of which waited for: 9 -> 27; matrix products, arithmetic and copies ran while one was open for 9% -> 23% of each run, Pallas kernels for 0% -> 5%
where the time goes in v1:
time: 444 us; the launch traced here: 440 us
  waiting for transfers between devices  213 us (48%)
  starting transfers between devices  53.3 us (12%)
  other arithmetic  52.2 us (12%)
  matrix products  41.2 us (9%)
  local copies, waits for them, and re-layouts  40.4 us (9%)
  Pallas kernels  23.6 us (5%)
  between operations  15.6 us (4%)
    ppermute x61, waiting for transfers between devices, swap(): return lax.ppermute(value, axis, pairs)  175 us
    ppermute x61, starting transfers between devices, swap(): return lax.ppermute(value, axis, pairs)  53.2 us
    all_gather x1, waiting for transfers between devices, shards(): forward_full = lax.all_gather(forward_own, 'fsdp', axis=1, tiled=True)  23.1 us
    unnamed x129, local copies, waits for them, and re-layouts  16.4 us
    all_gather x1, waiting for transfers between devices, shards(): attention_full = lax.all_gather(attention_own, 'fsdp', axis=0, tiled=True)  14.8 us
    dot_general x5, matrix products, dot(): return jnp.dot(left, right, preferred_element_type=jnp.float32)  11.2 us
    dot_general x4, matrix products, dot_rows(): lax.dot_general(left, right, (((0,), (0,)), ((), ())), preferred_element_...  10.6 us
    concatenate x5, other arithmetic, seq_gather(): return jnp.concatenate([value, near, far, both], axis=0)  9.83 us
  transfers between devices with their start and end apart: 63, of which 27 were waited for; matrix products, arithmetic and copies ran while one was open for 23% of the time, Pallas kernels for 5%

profile of v1, /device:TPU:0, one launch (start us, length us, event | category | flops | bytes accessed | tf_op | source)
XLA Modules:
  0.0 439.5 jit_solution(10574913581378253287)
XLA Ops:
  9.5 3.0 collective-permute-start
  12.6 2.2 take_attention.1
  19.1 2.7 collective-permute-start.2
  21.9 2.9 take_feed_forward.1
  27.2 12.6 %collective-permute-done.3 = f32[4,6912]{1,0:T(4,128)S(1)} collective-permute-done((f32[4,6912]{1,0:T(4,128)S(1)}, f32[4,6912]{1,0:T(4,128)S(1)}, u32[]{:S(2)}, u32[]{:S(2)}) %collective-permute-start.3) | collective-permute-done | bytes 110624 | tf_op jit(solution)/shard_map/ppermute | solution.py:47
  40.0 4.2 collective-permute-done.4
  45.8 2.5 collective-permute-done.5
  52.6 6.5 %collective-permute-done.7 = bf16[128,1152]{1,0:T(8,128)(2,1)} collective-permute-done((bf16[128,1152]{1,0:T(8,128)(2,1)}, bf16[128,1152]{1,0:T(8,128)(2,1)}, u32[]{:S(2)}, u32[]{:S(2)}) %collective-permute-start.7) | collective-permute-done | bytes 294944 | tf_op jit(solution)/shard_map/ppermute | solution.py:47
  63.3 14.8 %all-gather.3.cloned.1.call-done = bf16[1152,1184]{1,0:T(8,128)(2,1)} async-done(((bf16[144,1184]{1,0:T(8,128)(2,1)}), bf16[1152,1184]{1,0:T(8,128)(2,1)}) %all-gather.3.cloned.1.call-update) | async-done | bytes 2727952 | tf_op jit(solution)/shard_map/all_gather | solution.py:363
  81.3 2.7 fusion.125
  90.2 8.3 %collective-permute-done.10 = bf16[2,288,288]{2,1,0:T(8,128)(2,1)} collective-permute-done((bf16[2,288,288]{2,1,0:T(8,128)(2,1)}, bf16[2,288,288]{2,1,0:T(8,128)(2,1)}, u32[]{:S(2)}, u32[]{:S(2)}) %collective-permute-start.10) | collective-permute-done | bytes 331808 | tf_op jit(solution)/shard_map/ppermute | solution.py:47
  100.5 2.3 join_columns.2
  110.1 6.5 %collective-permute-done.14 = bf16[128,1152]{1,0:T(8,128)(2,1)} collective-permute-done((bf16[128,1152]{1,0:T(8,128)(2,1)S(1)}, bf16[128,1152]{1,0:T(8,128)(2,1)}, u32[]{:S(2)}, u32[]{:S(2)}) %collective-permute-start.14) | collective-permute-done | bytes 294944 | tf_op jit(solution)/shard_map/ppermute | solution.py:47
  121.5 2.3 pad_maximum_fusion.3
  123.8 5.0 %collective-permute-done.12 = bf16[1,128,1152]{2,1,0:T(8,128)(2,1)S(1)} collective-permute-done((bf16[1,128,1152]{2,1,0:T(8,128)(2,1)S(1)}, bf16[1,128,1152]{2,1,0:T(8,128)(2,1)S(1)}, u32[]{:S(2)}, u32[]{:S(2)}) %collective-permute-start.12) | collective-permute-done | bytes 294944 | tf_op jit(solution)/shard_map/ppermute | solution.py:47
  134.0 5.0 %collective-permute-done.17 = bf16[128,1152]{1,0:T(8,128)(2,1)} collective-permute-done((bf16[128,1152]{1,0:T(8,128)(2,1)S(1)}, bf16[128,1152]{1,0:T(8,128)(2,1)}, u32[]{:S(2)}, u32[]{:S(2)}) %collective-permute-start.17) | collective-permute-done | bytes 294944 | tf_op jit(solution)/shard_map/ppermute | solution.py:47
  143.2 23.1 %all-gather.5.cloned.1.call-done = bf16[2,1152,1152]{2,1,0:T(8,128)(2,1)} async-done(((bf16[2,144,1152]{2,1,0:T(8,128)(2,1)}), bf16[2,1152,1152]{2,1,0:T(8,128)(2,1)}) %all-gather.5.cloned.1.call-update) | async-done | bytes 5308432 | tf_op jit(solution)/shard_map/all_gather | solution.py:390
  166.3 4.2 multiply_convert_fusion.1
  170.5 2.9 fusion.124
  173.4 3.0 convolution_convert_fusion.1
  187.6 7.6 %collective-permute-done.22 = bf16[1,128,1152]{2,1,0:T(8,128)(2,1)S(1)} collective-permute-done((bf16[1,128,1152]{2,1,0:T(8,128)(2,1)S(1)}, bf16[1,128,1152]{2,1,0:T(8,128)(2,1)S(1)}, u32[]{:S(2)}, u32[]{:S(2)}) %collective-permute-start.22) | collective-permute-done | bytes 294944 | tf_op jit(solution)/shard_map/ppermute | solution.py:47
  196.7 3.3 collective-permute-done.20
  204.0 5.0 %collective-permute-done.24 = bf16[128,1152]{1,0:T(8,128)(2,1)S(1)} collective-permute-done((bf16[128,1152]{1,0:T(8,128)(2,1)S(1)}, bf16[128,1152]{1,0:T(8,128)(2,1)S(1)}, u32[]{:S(2)}, u32[]{:S(2)}) %collective-permute-start.24) | collective-permute-done | bytes 294944 | tf_op jit(solution)/shard_map/ppermute | solution.py:47
  209.0 4.1 collective-permute-done.47
  218.0 22.5 %collective-permute-done.54 = bf16[4,144,1152]{2,1,0:T(8,128)(2,1)S(1)} collective-permute-done((bf16[4,144,1152]{2,1,0:T(8,128)(2,1)S(1)}, bf16[4,144,1152]{2,1,0:T(8,128)(2,1)S(1)}, u32[]{:S(2)}, u32[]{:S(2)}) %collective-permute-start.54) | collective-permute-done | bytes 1327136 | tf_op jit(solution)/shard_map/ppermute | solution.py:47
  244.1 2.3 collective-permute-start.57
  248.5 2.5 split_columns.1
  263.9 4.4 %convolution_convert_fusion.2.grad_ref = bf16[1152,896]{1,0:T(8,128)(2,1)} fusion(bf16[512,1152]{1,0:T(8,128)(2,1)} %constant_dynamic-update-slice_fusion, bf16[512,288]{0,1:T(8,128)(2,1)S(1)} %bitcast.360, bf16[512,288]{0,1:T(8,128)(2,1)S(1)} %bitcast.366, bf16[512,288]{0,1:T(8,128)(2,1)} %bitcast.369, bf16[896]{0:T(1024)(128)(2,1)S(1)} %copy-done.50), kind=kOutput, calls=%fused_computation.8 | convolution fusion | flops 1061666816 | bytes 4130560 | tf_op jit(solution)/shard_map/dot_general | solution.py:42
  277.9 10.3 %collective-permute-done.56 = bf16[144,1152]{1,0:T(8,128)(2,1)S(1)} collective-permute-done((bf16[144,1152]{1,0:T(8,128)(2,1)S(1)}, bf16[144,1152]{1,0:T(8,128)(2,1)S(1)}, u32[]{:S(2)}, u32[]{:S(2)}) %collective-permute-start.56) | collective-permute-done | bytes 331808 | tf_op jit(solution)/shard_map/ppermute | solution.py:47
  304.9 6.2 %collective-permute-done.36 = bf16[2,288,288]{2,1,0:T(8,128)(2,1)} collective-permute-done((bf16[2,288,288]{2,1,0:T(8,128)(2,1)}, bf16[2,288,288]{2,1,0:T(8,128)(2,1)}, u32[]{:S(2)}, u32[]{:S(2)}) %collective-permute-start.36) | collective-permute-done | bytes 331808 | tf_op jit(solution)/shard_map/ppermute | solution.py:47
  311.1 2.2 pad_maximum_fusion.7.blocks_ref
  313.3 3.9 pack_near.1
  321.4 2.3 pad_maximum_fusion.1
  325.4 2.5 pad_maximum_fusion.2
  327.9 3.5 join_columns.3
  331.3 3.1 join_rows.1
  338.3 15.3 %collective-permute-done.32 = f32[1,16128]{1,0:T(1,128)S(1)} collective-permute-done((f32[1,16128]{1,0:T(1,128)S(1)}, f32[1,16128]{1,0:T(1,128)S(1)}, u32[]{:S(2)}, u32[]{:S(2)}) %collective-permute-start.32) | collective-permute-done | bytes 64544 | tf_op jit(solution)/shard_map/ppermute | solution.py:47
  355.5 4.2 collective-permute-done.33
  361.0 2.7 fusion.56
  363.7 9.5 %collective-permute-done.34 = f32[4,16128]{1,0:T(4,128)S(1)} collective-permute-done((f32[4,16128]{1,0:T(4,128)S(1)}, f32[4,16128]{1,0:T(4,128)S(1)}, u32[]{:S(2)}, u32[]{:S(2)}) %collective-permute-start.34) | collective-permute-done | bytes 258080 | tf_op jit(solution)/shard_map/ppermute | solution.py:47
  375.1 4.5 %convolution_bitcast_fusion = f32[1,144,6912]{2,1,0:T(8,128)} fusion(f32[8,16128]{1,0:T(8,128)S(1)} %pad_maximum_fusion.8, bf16[8,1152]{1,0:T(8,128)(2,1)} %copy-done.36, s32[]{:T(128)S(6)} %select_n.268, bf16[8,1152]{1,0:T(8,128)(2,1)} %copy-done.37), kind=kOutput, calls=%fused_computation | convolution fusion | flops 95556096 | bytes 4210692 | tf_op jit(solution)/shard_map/dot_general | solution.py:506
  381.2 2.2 convert_add_fusion
  383.5 2.4 collective-permute-start.43
  390.7 19.0 %collective-permute-done.39 = f32[2,1152]{1,0:T(2,128)S(1)} collective-permute-done((f32[2,1152]{1,0:T(2,128)S(1)}, f32[2,1152]{1,0:T(2,128)S(1)}, u32[]{:S(2)}, u32[]{:S(2)}) %collective-permute-start.39) | collective-permute-done | bytes 9248 | tf_op jit(solution)/shard_map/ppermute | solution.py:47
  409.7 2.6 collective-permute-start.40
  412.4 4.7 %collective-permute-done.42 = bf16[144,1184]{1,0:T(8,128)(2,1)S(1)} collective-permute-done((bf16[144,1184]{1,0:T(8,128)(2,1)S(1)}, bf16[144,1184]{1,0:T(8,128)(2,1)S(1)}, u32[]{:S(2)}, u32[]{:S(2)}) %collective-permute-start.42) | collective-permute-done | bytes 341024 | tf_op jit(solution)/shard_map/ppermute | solution.py:47
  419.1 7.2 %collective-permute-done.45 = bf16[144,1184]{1,0:T(8,128)(2,1)S(1)} collective-permute-done((bf16[144,1184]{1,0:T(8,128)(2,1)S(1)}, bf16[144,1184]{1,0:T(8,128)(2,1)S(1)}, u32[]{:S(2)}, u32[]{:S(2)}) %collective-permute-start.45) | collective-permute-done | bytes 341024 | tf_op jit(solution)/shard_map/ppermute | solution.py:47
  429.2 3.2 join_attention.1
  (394 shorter events, 143.9 us)
Async XLA Ops:
  7.2 70.9 %all-gather.3.cloned.1.call-start = ((), (), s32[]{:S(2)}) async-start(), calls=%async_computation | async-start | bytes 3317760 | tf_op jit(solution)/shard_map/all_gather | solution.py:363
  14.7 151.6 %all-gather.5.cloned.1.call-start = ((), (), s32[]{:S(2)}) async-start(), calls=%async_computation.1 | async-start | bytes 5971968 | tf_op jit(solution)/shard_map/all_gather | solution.py:390
  26.3 13.6 %collective-permute-start.3 = (f32[4,6912]{1,0:T(4,128)S(1)}, f32[4,6912]{1,0:T(4,128)S(1)}, u32[]{:S(2)}, u32[]{:S(2)}) collective-permute-start(f32[4,6912]{1,0:T(4,128)S(1)} %slice_select_fusion), channel_id=1, source_target_pairs={{0,4},{1,5},{2,6},{3,7},{4,0},{5,1},{6,2},{7,3},{8,12},{9,13},{10,... | collective-permute-start | bytes 331784 | tf_op jit(solution)/shard_map/ppermute | solution.py:47
  49.4 9.7 %collective-permute-start.6 = (bf16[128,1152]{1,0:T(8,128)(2,1)}, bf16[128,1152]{1,0:T(8,128)(2,1)}, u32[]{:S(2)}, u32[]{:S(2)}) collective-permute-start(bf16[128,1152]{1,0:T(8,128)(2,1)} %fusion.48), channel_id=1, source_target_pairs={{0,8},{8,0},{16,24},{24,16},{1,9},{9,1},{17,25},{25,17},{2,10},{10... | collective-permute-start | bytes 884744 | tf_op jit(solution)/shard_map/ppermute | solution.py:47
  49.4 9.7 %collective-permute-start.7 = (bf16[128,1152]{1,0:T(8,128)(2,1)}, bf16[128,1152]{1,0:T(8,128)(2,1)}, u32[]{:S(2)}, u32[]{:S(2)}) collective-permute-start(bf16[128,1152]{1,0:T(8,128)(2,1)} %fusion.48), channel_id=1, source_target_pairs={{0,16},{8,24},{16,0},{24,8},{1,17},{9,25},{17,1},{25,9},{2,18},{10... | collective-permute-start | bytes 884744 | tf_op jit(solution)/shard_map/ppermute | solution.py:47
  87.0 11.4 %collective-permute-start.10 = (bf16[2,288,288]{2,1,0:T(8,128)(2,1)}, bf16[2,288,288]{2,1,0:T(8,128)(2,1)}, u32[]{:S(2)}, u32[]{:S(2)}) collective-permute-start(bf16[2,288,288]{2,1,0:T(8,128)(2,1)} %get-tuple-element.90), channel_id=1, source_target_pairs={{0,16},{8,24},{16,0},{24,8},{1,17},{9,25},{17,1},{25,9},{2,18},{10... | collective-permute-start | bytes 995336 | tf_op jit(solution)/shard_map/ppermute | solution.py:47
  107.1 9.5 %collective-permute-start.11 = (bf16[2,128,1152]{2,1,0:T(8,128)(2,1)}, bf16[2,128,1152]{2,1,0:T(8,128)(2,1)S(1)}, u32[]{:S(2)}, u32[]{:S(2)}) collective-permute-start(bf16[2,128,1152]{2,1,0:T(8,128)(2,1)} %fusion.57), channel_id=1, source_target_pairs={{0,8},{8,0},{16,24},{24,16},{1,9},{9,1},{17,25},{25,17},{2,10},{10... | collective-permute-start | bytes 1769480 | tf_op jit(solution)/shard_map/ppermute | solution.py:47
  107.1 9.5 %collective-permute-start.14 = (bf16[128,1152]{1,0:T(8,128)(2,1)S(1)}, bf16[128,1152]{1,0:T(8,128)(2,1)}, u32[]{:S(2)}, u32[]{:S(2)}) collective-permute-start(bf16[128,1152]{1,0:T(8,128)(2,1)S(1)} %fusion.71), channel_id=1, source_target_pairs={{0,16},{8,24},{16,0},{24,8},{1,17},{9,25},{17,1},{25,9},{2,18},{10... | collective-permute-start | bytes 884744 | tf_op jit(solution)/shard_map/ppermute | solution.py:47
  109.9 11.5 %collective-permute-start.13 = (bf16[128,1152]{1,0:T(8,128)(2,1)S(1)}, bf16[128,1152]{1,0:T(8,128)(2,1)}, u32[]{:S(2)}, u32[]{:S(2)}) collective-permute-start(bf16[128,1152]{1,0:T(8,128)(2,1)S(1)} %fusion.71), channel_id=1, source_target_pairs={{0,8},{8,0},{16,24},{24,16},{1,9},{9,1},{17,25},{25,17},{2,10},{10... | collective-permute-start | bytes 884744 | tf_op jit(solution)/shard_map/ppermute | solution.py:47
  119.1 9.6 %collective-permute-start.12 = (bf16[1,128,1152]{2,1,0:T(8,128)(2,1)S(1)}, bf16[1,128,1152]{2,1,0:T(8,128)(2,1)S(1)}, u32[]{:S(2)}, u32[]{:S(2)}) collective-permute-start(bf16[1,128,1152]{2,1,0:T(8,128)(2,1)S(1)} %fusion.82), channel_id=1, source_target_pairs={{0,16},{8,24},{16,0},{24,8},{1,17},{9,25},{17,1},{25,9},{2,18},{10... | collective-permute-start | bytes 884744 | tf_op jit(solution)/shard_map/ppermute | solution.py:47
  129.4 9.6 %collective-permute-start.16 = (bf16[128,1152]{1,0:T(8,128)(2,1)S(1)}, bf16[128,1152]{1,0:T(8,128)(2,1)}, u32[]{:S(2)}, u32[]{:S(2)}) collective-permute-start(bf16[128,1152]{1,0:T(8,128)(2,1)S(1)} %add_convert_fusion), channel_id=1, source_target_pairs={{0,8},{8,0},{16,24},{24,16},{1,9},{9,1},{17,25},{25,17},{2,10},{10... | collective-permute-start | bytes 884744 | tf_op jit(solution)/shard_map/ppermute | solution.py:47
  129.5 9.5 %collective-permute-start.17 = (bf16[128,1152]{1,0:T(8,128)(2,1)S(1)}, bf16[128,1152]{1,0:T(8,128)(2,1)}, u32[]{:S(2)}, u32[]{:S(2)}) collective-permute-start(bf16[128,1152]{1,0:T(8,128)(2,1)S(1)} %add_convert_fusion), channel_id=1, source_target_pairs={{0,16},{8,24},{16,0},{24,8},{1,17},{9,25},{17,1},{25,9},{2,18},{10... | collective-permute-start | bytes 884744 | tf_op jit(solution)/shard_map/ppermute | solution.py:47
  180.2 6.6 %collective-permute-start.19 = (bf16[2,128,1152]{2,1,0:T(8,128)(2,1)S(1)}, bf16[2,128,1152]{2,1,0:T(8,128)(2,1)S(1)}, u32[]{:S(2)}, u32[]{:S(2)}) collective-permute-start(bf16[2,128,1152]{2,1,0:T(8,128)(2,1)S(1)} %fusion.58), channel_id=1, source_target_pairs={{0,8},{8,0},{16,24},{24,16},{1,9},{9,1},{17,25},{25,17},{2,10},{10... | collective-permute-start | bytes 1769480 | tf_op jit(solution)/shard_map/ppermute | solution.py:47
  181.0 32.1 %collective-permute-start.47 = (bf16[4,144,1152]{2,1,0:T(8,128)(2,1)S(1)}, bf16[4,144,1152]{2,1,0:T(8,128)(2,1)S(1)}, u32[]{:S(2)}, u32[]{:S(2)}) collective-permute-start(bf16[4,144,1152]{2,1,0:T(8,128)(2,1)S(1)} %dynamic-slice_bitcast_fusion.1), channel_id=1, source_target_pairs={{0,1},{1,0},{2,3},{3,2},{4,5},{5,4},{6,7},{7,6},{8,9},{9,8},{10,11... | collective-permute-start | bytes 3981320 | tf_op jit(solution)/shard_map/ppermute | solution.py:47
  183.5 57.1 %collective-permute-start.54 = (bf16[4,144,1152]{2,1,0:T(8,128)(2,1)S(1)}, bf16[4,144,1152]{2,1,0:T(8,128)(2,1)S(1)}, u32[]{:S(2)}, u32[]{:S(2)}) collective-permute-start(bf16[4,144,1152]{2,1,0:T(8,128)(2,1)S(1)} %dynamic-slice_bitcast_fusion), channel_id=1, source_target_pairs={{0,1},{1,0},{2,3},{3,2},{4,5},{5,4},{6,7},{7,6},{8,9},{9,8},{10,11... | collective-permute-start | bytes 3981320 | tf_op jit(solution)/shard_map/ppermute | solution.py:47
  185.2 9.9 %collective-permute-start.22 = (bf16[1,128,1152]{2,1,0:T(8,128)(2,1)S(1)}, bf16[1,128,1152]{2,1,0:T(8,128)(2,1)S(1)}, u32[]{:S(2)}, u32[]{:S(2)}) collective-permute-start(bf16[1,128,1152]{2,1,0:T(8,128)(2,1)S(1)} %fusion.84), channel_id=1, source_target_pairs={{0,16},{8,24},{16,0},{24,8},{1,17},{9,25},{17,1},{25,9},{2,18},{10... | collective-permute-start | bytes 884744 | tf_op jit(solution)/shard_map/ppermute | solution.py:47
  187.0 13.0 %collective-permute-start.20 = (bf16[1,128,1152]{2,1,0:T(8,128)(2,1)S(1)}, bf16[1,128,1152]{2,1,0:T(8,128)(2,1)S(1)}, u32[]{:S(2)}, u32[]{:S(2)}) collective-permute-start(bf16[1,128,1152]{2,1,0:T(8,128)(2,1)S(1)} %fusion.83), channel_id=1, source_target_pairs={{0,16},{8,24},{16,0},{24,8},{1,17},{9,25},{17,1},{25,9},{2,18},{10... | collective-permute-start | bytes 884744 | tf_op jit(solution)/shard_map/ppermute | solution.py:47
  201.4 7.6 %collective-permute-start.24 = (bf16[128,1152]{1,0:T(8,128)(2,1)S(1)}, bf16[128,1152]{1,0:T(8,128)(2,1)S(1)}, u32[]{:S(2)}, u32[]{:S(2)}) collective-permute-start(bf16[128,1152]{1,0:T(8,128)(2,1)S(1)} %multiply_convert_fusion.2), channel_id=1, source_target_pairs={{0,16},{8,24},{16,0},{24,8},{1,17},{9,25},{17,1},{25,9},{2,18},{10... | collective-permute-start | bytes 884744 | tf_op jit(solution)/shard_map/ppermute | solution.py:47
  202.9 41.1 %collective-permute-start.23 = (bf16[128,1152]{1,0:T(8,128)(2,1)S(1)}, bf16[128,1152]{1,0:T(8,128)(2,1)S(1)}, u32[]{:S(2)}, u32[]{:S(2)}) collective-permute-start(bf16[128,1152]{1,0:T(8,128)(2,1)S(1)} %multiply_convert_fusion.2), channel_id=1, source_target_pairs={{0,8},{8,0},{16,24},{24,16},{1,9},{9,1},{17,25},{25,17},{2,10},{10... | collective-permute-start | bytes 884744 | tf_op jit(solution)/shard_map/ppermute | solution.py:47
  209.0 37.4 %collective-permute-start.25 = (bf16[128,1152]{1,0:T(8,128)(2,1)S(1)}, bf16[128,1152]{1,0:T(8,128)(2,1)S(1)}, u32[]{:S(2)}, u32[]{:S(2)}) collective-permute-start(bf16[128,1152]{1,0:T(8,128)(2,1)S(1)} %collective-permute-done.24), channel_id=1, source_target_pairs={{0,8},{8,0},{16,24},{24,16},{1,9},{9,1},{17,25},{25,17},{2,10},{10... | collective-permute-start | bytes 884744 | tf_op jit(solution)/shard_map/ppermute | solution.py:47
  215.9 56.7 %collective-permute-start.50 = (bf16[144,1152]{1,0:T(8,128)(2,1)}, bf16[144,1152]{1,0:T(8,128)(2,1)}, u32[]{:S(2)}, u32[]{:S(2)}) collective-permute-start(bf16[144,1152]{1,0:T(8,128)(2,1)} %get-tuple-element.83), channel_id=1, source_target_pairs={{0,6},{1,7},{2,4},{3,5},{4,2},{5,3},{6,0},{7,1},{8,14},{9,15},{10,... | collective-permute-start | bytes 995336 | tf_op jit(solution)/shard_map/ppermute | solution.py:47
  217.5 56.9 %collective-permute-start.49 = (bf16[144,1152]{1,0:T(8,128)(2,1)}, bf16[144,1152]{1,0:T(8,128)(2,1)}, u32[]{:S(2)}, u32[]{:S(2)}) collective-permute-start(bf16[144,1152]{1,0:T(8,128)(2,1)} %get-tuple-element.84), channel_id=1, source_target_pairs={{0,4},{1,5},{2,6},{3,7},{4,0},{5,1},{6,2},{7,3},{8,12},{9,13},{10,... | collective-permute-start | bytes 995336 | tf_op jit(solution)/shard_map/ppermute | solution.py:47
  240.6 33.7 %collective-permute-start.48 = (bf16[144,1152]{1,0:T(8,128)(2,1)}, bf16[144,1152]{1,0:T(8,128)(2,1)}, u32[]{:S(2)}, u32[]{:S(2)}) collective-permute-start(bf16[144,1152]{1,0:T(8,128)(2,1)} %get-tuple-element.82), channel_id=1, source_target_pairs={{0,2},{1,3},{2,0},{3,1},{4,6},{5,7},{6,4},{7,5},{8,10},{9,11},{10,... | collective-permute-start | bytes 995336 | tf_op jit(solution)/shard_map/ppermute | solution.py:47
  244.1 32.3 %collective-permute-start.57 = (bf16[144,1152]{1,0:T(8,128)(2,1)}, bf16[144,1152]{1,0:T(8,128)(2,1)}, u32[]{:S(2)}, u32[]{:S(2)}) collective-permute-start(bf16[144,1152]{1,0:T(8,128)(2,1)} %get-tuple-element.80), channel_id=1, source_target_pairs={{0,6},{1,7},{2,4},{3,5},{4,2},{5,3},{6,0},{7,1},{8,14},{9,15},{10,... | collective-permute-start | bytes 995336 | tf_op jit(solution)/shard_map/ppermute | solution.py:47
  272.1 16.1 %collective-permute-start.56 = (bf16[144,1152]{1,0:T(8,128)(2,1)S(1)}, bf16[144,1152]{1,0:T(8,128)(2,1)S(1)}, u32[]{:S(2)}, u32[]{:S(2)}) collective-permute-start(bf16[144,1152]{1,0:T(8,128)(2,1)S(1)} %copy-done.28), channel_id=1, source_target_pairs={{0,4},{1,5},{2,6},{3,7},{4,0},{5,1},{6,2},{7,3},{8,12},{9,13},{10,... | collective-permute-start | bytes 995336 | tf_op jit(solution)/shard_map/ppermute | solution.py:47
  272.7 15.8 %collective-permute-start.55 = (bf16[144,1152]{1,0:T(8,128)(2,1)S(1)}, bf16[144,1152]{1,0:T(8,128)(2,1)S(1)}, u32[]{:S(2)}, u32[]{:S(2)}) collective-permute-start(bf16[144,1152]{1,0:T(8,128)(2,1)S(1)} %copy-done.27), channel_id=1, source_target_pairs={{0,2},{1,3},{2,0},{3,1},{4,6},{5,7},{6,4},{7,5},{8,10},{9,11},{10,... | collective-permute-start | bytes 995336 | tf_op jit(solution)/shard_map/ppermute | solution.py:47
  274.3 19.4 %collective-permute-start.26 = (bf16[2,128,1152]{2,1,0:T(8,128)(2,1)S(1)}, bf16[2,128,1152]{2,1,0:T(8,128)(2,1)S(1)}, u32[]{:S(2)}, u32[]{:S(2)}) collective-permute-start(bf16[2,128,1152]{2,1,0:T(8,128)(2,1)S(1)} %copy-done.26), channel_id=1, source_target_pairs={{0,8},{8,0},{16,24},{24,16},{1,9},{9,1},{17,25},{25,17},{2,10},{10... | collective-permute-start | bytes 1769480 | tf_op jit(solution)/shard_map/ppermute | solution.py:47
  274.3 17.8 %collective-permute-start.35 = (bf16[2,288,288]{2,1,0:T(8,128)(2,1)S(1)}, bf16[2,288,288]{2,1,0:T(8,128)(2,1)S(1)}, u32[]{:S(2)}, u32[]{:S(2)}) collective-permute-start(bf16[2,288,288]{2,1,0:T(8,128)(2,1)S(1)} %get-tuple-element.88), channel_id=1, source_target_pairs={{0,8},{8,0},{16,24},{24,16},{1,9},{9,1},{17,25},{25,17},{2,10},{10... | collective-permute-start | bytes 995336 | tf_op jit(solution)/shard_map/ppermute | solution.py:47
  276.4 27.9 %collective-permute-start.52 = (bf16[144,1152]{1,0:T(8,128)(2,1)S(1)}, bf16[144,1152]{1,0:T(8,128)(2,1)}, u32[]{:S(2)}, u32[]{:S(2)}) collective-permute-start(bf16[144,1152]{1,0:T(8,128)(2,1)S(1)} %fusion.46), channel_id=1, source_target_pairs={{0,16},{8,24},{16,0},{24,8},{1,17},{9,25},{17,1},{25,9},{2,18},{10... | collective-permute-start | bytes 995336 | tf_op jit(solution)/shard_map/ppermute | solution.py:47
  290.6 14.2 %collective-permute-start.59 = (bf16[144,1152]{1,0:T(8,128)(2,1)}, bf16[144,1152]{1,0:T(8,128)(2,1)}, u32[]{:S(2)}, u32[]{:S(2)}) collective-permute-start(bf16[144,1152]{1,0:T(8,128)(2,1)} %fusion.43), channel_id=1, source_target_pairs={{0,16},{8,24},{16,0},{24,8},{1,17},{9,25},{17,1},{25,9},{2,18},{10... | collective-permute-start | bytes 995336 | tf_op jit(solution)/shard_map/ppermute | solution.py:47
  293.2 17.9 %collective-permute-start.36 = (bf16[2,288,288]{2,1,0:T(8,128)(2,1)}, bf16[2,288,288]{2,1,0:T(8,128)(2,1)}, u32[]{:S(2)}, u32[]{:S(2)}) collective-permute-start(bf16[2,288,288]{2,1,0:T(8,128)(2,1)} %get-tuple-element.86), channel_id=1, source_target_pairs={{0,16},{8,24},{16,0},{24,8},{1,17},{9,25},{17,1},{25,9},{2,18},{10... | collective-permute-start | bytes 995336 | tf_op jit(solution)/shard_map/ppermute | solution.py:47
  295.6 21.6 %collective-permute-start.27 = (bf16[1,128,1152]{2,1,0:T(8,128)(2,1)}, bf16[1,128,1152]{2,1,0:T(8,128)(2,1)S(1)}, u32[]{:S(2)}, u32[]{:S(2)}) collective-permute-start(bf16[1,128,1152]{2,1,0:T(8,128)(2,1)} %fusion.85), channel_id=1, source_target_pairs={{0,16},{8,24},{16,0},{24,8},{1,17},{9,25},{17,1},{25,9},{2,18},{10... | collective-permute-start | bytes 884744 | tf_op jit(solution)/shard_map/ppermute | solution.py:47
  304.3 16.8 %collective-permute-start.51 = (bf16[144,1152]{1,0:T(8,128)(2,1)S(1)}, bf16[144,1152]{1,0:T(8,128)(2,1)}, u32[]{:S(2)}, u32[]{:S(2)}) collective-permute-start(bf16[144,1152]{1,0:T(8,128)(2,1)S(1)} %fusion.46), channel_id=1, source_target_pairs={{0,8},{8,0},{16,24},{24,16},{1,9},{9,1},{17,25},{25,17},{2,10},{10... | collective-permute-start | bytes 995336 | tf_op jit(solution)/shard_map/ppermute | solution.py:47
  304.3 21.1 %collective-permute-start.58 = (bf16[144,1152]{1,0:T(8,128)(2,1)}, bf16[144,1152]{1,0:T(8,128)(2,1)}, u32[]{:S(2)}, u32[]{:S(2)}) collective-permute-start(bf16[144,1152]{1,0:T(8,128)(2,1)} %fusion.43), channel_id=1, source_target_pairs={{0,8},{8,0},{16,24},{24,16},{1,9},{9,1},{17,25},{25,17},{2,10},{10... | collective-permute-start | bytes 995336 | tf_op jit(solution)/shard_map/ppermute | solution.py:47
  304.8 16.6 %collective-permute-start.53 = (bf16[144,1152]{1,0:T(8,128)(2,1)}, bf16[144,1152]{1,0:T(8,128)(2,1)}, u32[]{:S(2)}, u32[]{:S(2)}) collective-permute-start(bf16[144,1152]{1,0:T(8,128)(2,1)} %collective-permute-done.52), channel_id=1, source_target_pairs={{0,8},{8,0},{16,24},{24,16},{1,9},{9,1},{17,25},{25,17},{2,10},{10... | collective-permute-start | bytes 995336 | tf_op jit(solution)/shard_map/ppermute | solution.py:47
  311.1 14.3 %collective-permute-start.60 = (bf16[144,1152]{1,0:T(8,128)(2,1)}, bf16[144,1152]{1,0:T(8,128)(2,1)}, u32[]{:S(2)}, u32[]{:S(2)}) collective-permute-start(bf16[144,1152]{1,0:T(8,128)(2,1)} %collective-permute-done.59), channel_id=1, source_target_pairs={{0,8},{8,0},{16,24},{24,16},{1,9},{9,1},{17,25},{25,17},{2,10},{10... | collective-permute-start | bytes 995336 | tf_op jit(solution)/shard_map/ppermute | solution.py:47
  317.3 56.2 %collective-permute-start.37 = (bf16[4,144,1184]{2,1,0:T(8,128)(2,1)}, bf16[4,144,1184]{2,1,0:T(8,128)(2,1)}, u32[]{:S(2)}, u32[]{:S(2)}) collective-permute-start(bf16[4,144,1184]{2,1,0:T(8,128)(2,1)} %get-tuple-element.41), channel_id=1, source_target_pairs={{0,1},{1,0},{2,3},{3,2},{4,5},{5,4},{6,7},{7,6},{8,9},{9,8},{10,11... | collective-permute-start | bytes 4091912 | tf_op jit(solution)/shard_map/ppermute | solution.py:47
  323.8 10.6 %collective-permute-start.29 = (f32[1,9216]{1,0:T(1,128)S(1)}, f32[1,9216]{1,0:T(1,128)}, u32[]{:S(2)}, u32[]{:S(2)}) collective-permute-start(f32[1,9216]{1,0:T(1,128)S(1)} %add.370), channel_id=1, source_target_pairs={{0,16},{8,24},{16,0},{24,8},{1,17},{9,25},{17,1},{25,9},{2,18},{10... | collective-permute-start | bytes 110600 | tf_op jit(solution)/shard_map/ppermute | solution.py:47
  336.1 17.5 %collective-permute-start.32 = (f32[1,16128]{1,0:T(1,128)S(1)}, f32[1,16128]{1,0:T(1,128)S(1)}, u32[]{:S(2)}, u32[]{:S(2)}) collective-permute-start(f32[1,16128]{1,0:T(1,128)S(1)} %pad_maximum_fusion.13), channel_id=1, source_target_pairs={{0,1},{1,0},{2,3},{3,2},{4,5},{5,4},{6,7},{7,6},{8,9},{9,8},{10,11... | collective-permute-start | bytes 193544 | tf_op jit(solution)/shard_map/ppermute | solution.py:47
  359.9 13.2 %collective-permute-start.34 = (f32[4,16128]{1,0:T(4,128)S(1)}, f32[4,16128]{1,0:T(4,128)S(1)}, u32[]{:S(2)}, u32[]{:S(2)}) collective-permute-start(f32[4,16128]{1,0:T(4,128)S(1)} %pad_maximum_fusion.11), channel_id=1, source_target_pairs={{0,4},{1,5},{2,6},{3,7},{4,0},{5,1},{6,2},{7,3},{8,12},{9,13},{10,... | collective-permute-start | bytes 774152 | tf_op jit(solution)/shard_map/ppermute | solution.py:47
  379.9 10.0 %collective-permute-start.38 = (f32[1,1152]{1,0:T(1,128)S(1)}, f32[1,1152]{1,0:T(1,128)S(1)}, u32[]{:S(2)}, u32[]{:S(2)}) collective-permute-start(f32[1,1152]{1,0:T(1,128)S(1)} %reshape.391), channel_id=1, source_target_pairs={{0,1},{1,0},{2,3},{3,2},{4,5},{5,4},{6,7},{7,6},{8,9},{9,8},{10,11... | collective-permute-start | bytes 13832 | tf_op jit(solution)/shard_map/ppermute | solution.py:47
  383.5 28.9 %collective-permute-start.43 = (bf16[144,1184]{1,0:T(8,128)(2,1)S(1)}, bf16[144,1184]{1,0:T(8,128)(2,1)S(1)}, u32[]{:S(2)}, u32[]{:S(2)}) collective-permute-start(bf16[144,1184]{1,0:T(8,128)(2,1)S(1)} %get-tuple-element.77), channel_id=1, source_target_pairs={{0,6},{1,7},{2,4},{3,5},{4,2},{5,3},{6,0},{7,1},{8,14},{9,15},{10,... | collective-permute-start | bytes 1022984 | tf_op jit(solution)/shard_map/ppermute | solution.py:47
  385.9 31.2 %collective-permute-start.42 = (bf16[144,1184]{1,0:T(8,128)(2,1)S(1)}, bf16[144,1184]{1,0:T(8,128)(2,1)S(1)}, u32[]{:S(2)}, u32[]{:S(2)}) collective-permute-start(bf16[144,1184]{1,0:T(8,128)(2,1)S(1)} %get-tuple-element.78), channel_id=1, source_target_pairs={{0,4},{1,5},{2,6},{3,7},{4,0},{5,1},{6,2},{7,3},{8,12},{9,13},{10,... | collective-permute-start | bytes 1022984 | tf_op jit(solution)/shard_map/ppermute | solution.py:47
  385.9 31.2 %collective-permute-start.41 = (bf16[144,1184]{1,0:T(8,128)(2,1)S(1)}, bf16[144,1184]{1,0:T(8,128)(2,1)S(1)}, u32[]{:S(2)}, u32[]{:S(2)}) collective-permute-start(bf16[144,1184]{1,0:T(8,128)(2,1)S(1)} %get-tuple-element.76), channel_id=1, source_target_pairs={{0,2},{1,3},{2,0},{3,1},{4,6},{5,7},{6,4},{7,5},{8,10},{9,11},{10,... | collective-permute-start | bytes 1022984 | tf_op jit(solution)/shard_map/ppermute | solution.py:47
  389.9 19.8 %collective-permute-start.39 = (f32[2,1152]{1,0:T(2,128)S(1)}, f32[2,1152]{1,0:T(2,128)S(1)}, u32[]{:S(2)}, u32[]{:S(2)}) collective-permute-start(f32[2,1152]{1,0:T(2,128)S(1)} %pad_maximum_fusion.20), channel_id=1, source_target_pairs={{0,2},{1,3},{2,0},{3,1},{4,6},{5,7},{6,4},{7,5},{8,10},{9,11},{10,... | collective-permute-start | bytes 27656 | tf_op jit(solution)/shard_map/ppermute | solution.py:47
  409.7 9.0 %collective-permute-start.40 = (f32[4,1152]{1,0:T(4,128)S(1)}, f32[4,1152]{1,0:T(4,128)S(1)}, u32[]{:S(2)}, u32[]{:S(2)}) collective-permute-start(f32[4,1152]{1,0:T(4,128)S(1)} %pad_maximum_fusion.17), channel_id=1, source_target_pairs={{0,4},{1,5},{2,6},{3,7},{4,0},{5,1},{6,2},{7,3},{8,12},{9,13},{10,... | collective-permute-start | bytes 55304 | tf_op jit(solution)/shard_map/ppermute | solution.py:47
  417.2 9.0 %collective-permute-start.45 = (bf16[144,1184]{1,0:T(8,128)(2,1)S(1)}, bf16[144,1184]{1,0:T(8,128)(2,1)S(1)}, u32[]{:S(2)}, u32[]{:S(2)}) collective-permute-start(bf16[144,1184]{1,0:T(8,128)(2,1)S(1)} %fusion.33), channel_id=1, source_target_pairs={{0,16},{8,24},{16,0},{24,8},{1,17},{9,25},{17,1},{25,9},{2,18},{10... | collective-permute-start | bytes 1022984 | tf_op jit(solution)/shard_map/ppermute | solution.py:47
  419.0 7.9 %collective-permute-start.44 = (bf16[144,1184]{1,0:T(8,128)(2,1)S(1)}, bf16[144,1184]{1,0:T(8,128)(2,1)S(1)}, u32[]{:S(2)}, u32[]{:S(2)}) collective-permute-start(bf16[144,1184]{1,0:T(8,128)(2,1)S(1)} %fusion.33), channel_id=1, source_target_pairs={{0,8},{8,0},{16,24},{24,16},{1,9},{9,1},{17,25},{25,17},{2,10},{10... | collective-permute-start | bytes 1022984 | tf_op jit(solution)/shard_map/ppermute | solution.py:47
  (77 other events, 691.6 us)
Sparse Core Ops, SparseCore 0:
  14.9 63.1 all-gather.2
  80.9 85.3 all-gather.4

commit v2 on v1

--- a/solution.py
+++ b/solution.py
@@ -57,25 +57,26 @@
 
 
 def seq_gather(value):
-    near = swap(value, "seq", 1)
-    far = swap(value, "seq", 2)
-    both = swap(far, "seq", 1)
-    return jnp.concatenate([value, near, far, both], axis=0)
-
-
-def seq_blocks(block):
-    low = block.astype(jnp.bfloat16)
-    return seq_gather(low).reshape((-1,) + low.shape)
+    return jnp.concatenate(seq_blocks(value), axis=0)
+
+
+def seq_blocks(value):
+    blocks = {0: value}
+    for mask in reversed(bits_of(lax.axis_size("seq"))):
+        for tag in list(blocks):
+            blocks[tag ^ mask] = swap(blocks[tag], "seq", mask)
+    return [blocks[tag] for tag in range(len(blocks))]
 
 
 def seq_exchange(blocks):
-    if blocks.shape[0] == 1:
-        return blocks
-    pairs = blocks.reshape((-1, 2) + blocks.shape[1:])
-    near = swap(pairs[:, 1], "seq", 1)
-    kept = jnp.stack([pairs[:, 0], near], axis=1)
-    far = swap(kept[1], "seq", 2)
-    return jnp.concatenate([kept[0], far], axis=0)
+    count = len(blocks)
+    blocks = list(blocks)
+    for mask in bits_of(count):
+        kept = [tag for tag in range(count) if not tag & mask]
+        received = swap(jnp.stack([blocks[tag | mask] for tag in kept]), "seq", mask)
+        moved = {tag | mask: received[at] for at, tag in enumerate(kept)}
+        blocks = [moved.get(tag, blocks[tag]) for tag in range(count)]
+    return blocks
 
 
 def seq_reduce(partial):
@@ -175,29 +176,11 @@
     )(index.reshape(1), fc1, fc2)
 
 
-def pack_near(grad, blocks, index, near, devices):
-    group = blocks.shape[1]
-    rows, used = grad.shape[0] // devices, grad.shape[1]
-    shape = (devices // 2, rows, used + blocks.shape[2])
-
-    def kernel(at_ref, grad_ref, blocks_ref, kept_ref, sent_ref):
-        for side in range(2):
-
-            @pl.when(at_ref[1] == side)
-            def _():
-                for owner in range(devices):
-                    target = kept_ref if owner % 2 == side else sent_ref
-                    part, start = divmod(owner * rows, group)
-                    target[owner // 2, :, :used] = grad_ref[owner * rows : (owner + 1) * rows]
-                    target[owner // 2, :, used:] = blocks_ref[at_ref[0] ^ part][start : start + rows]
-
-    return pl.pallas_call(
-        kernel,
-        out_shape=[jax.ShapeDtypeStruct(shape, grad.dtype)] * 2,
-        in_specs=[pl.BlockSpec(memory_space=pltpu.SMEM)] + in_vmem(2),
-        out_specs=in_vmem(2),
-        name="pack_near",
-    )(jnp.stack([index, near]), grad, blocks)
+def pick(refs, index, dtype):
+    value = refs[0][...]
+    for at in range(1, len(refs)):
+        value = jnp.where(index == at, refs[at][...], value)
+    return value.astype(dtype)
 
 
 def split_columns(whole, index, parts):
@@ -223,13 +206,12 @@
     )(index.reshape(1), whole)
 
 
-def join_columns(blocks, index, groups, dtype):
-    parts, rows, columns = blocks.shape
-    span = columns // groups
-
-    def kernel(at_ref, source, target):
-        own = at_ref[0]
-        wholes = [source[own ^ part].astype(dtype) for part in range(parts)]
+def join_columns(blocks, index, groups, span, dtype):
+    parts, rows = len(blocks), blocks[0].shape[0]
+
+    def kernel(at_ref, *refs):
+        target = refs[-1]
+        wholes = [pick(refs[:-1], at_ref[0] ^ part, dtype) for part in range(parts)]
         pieces = []
         for group in range(groups):
             for part in range(parts):
@@ -238,53 +220,30 @@
 
     return pl.pallas_call(
         kernel,
-        out_shape=jax.ShapeDtypeStruct((rows, parts * columns), dtype),
-        in_specs=[pl.BlockSpec(memory_space=pltpu.SMEM)] + in_vmem(1),
+        out_shape=jax.ShapeDtypeStruct((rows, parts * groups * span), dtype),
+        in_specs=[pl.BlockSpec(memory_space=pltpu.SMEM)] + in_vmem(parts),
         out_specs=in_vmem(1)[0],
         name="join_columns",
-    )(index.reshape(1), blocks)
-
-
-def join_attention(blocks, index, span):
-    parts, rows, columns = blocks.shape
-    starts = [0, span, 2 * span, columns - span]
-
-    def kernel(at_ref, source, qkv_ref, proj_ref):
-        own = at_ref[0]
-        wholes = [source[own ^ part].astype(jnp.float32) for part in range(parts)]
-        pieces = []
-        for start in starts:
-            for part in range(parts):
-                pieces.append(wholes[part][:, start : start + span])
-        qkv_ref[...] = jnp.concatenate(pieces[: 3 * parts], axis=1)
-        proj_ref[...] = jnp.concatenate(pieces[3 * parts :], axis=1)
-
-    return pl.pallas_call(
-        kernel,
-        out_shape=[
-            jax.ShapeDtypeStruct((rows, 3 * parts * span), jnp.float32),
-            jax.ShapeDtypeStruct((rows, parts * span), jnp.float32),
-        ],
-        in_specs=[pl.BlockSpec(memory_space=pltpu.SMEM)] + in_vmem(1),
-        out_specs=in_vmem(2),
-        name="join_attention",
-    )(index.reshape(1), blocks)
+    )(index.reshape(1), *blocks)
 
 
 def join_rows(blocks, index, dtype):
-    parts, rows, columns = blocks.shape
-
-    def kernel(at_ref, source, target):
+    parts = len(blocks)
+    rows, columns = blocks[0].shape
+
+    def kernel(at_ref, *refs):
+        target = refs[-1]
         for part in range(parts):
-            target[part * rows : (part + 1) * rows] = source[at_ref[0] ^ part].astype(dtype)
+            value = pick(refs[:-1], at_ref[0] ^ part, dtype)
+            target[part * rows : (part + 1) * rows] = value
 
     return pl.pallas_call(
         kernel,
         out_shape=jax.ShapeDtypeStruct((parts * rows, columns), dtype),
-        in_specs=[pl.BlockSpec(memory_space=pltpu.SMEM)] + in_vmem(1),
+        in_specs=[pl.BlockSpec(memory_space=pltpu.SMEM)] + in_vmem(parts),
         out_specs=in_vmem(1)[0],
         name="join_rows",
-    )(index.reshape(1), blocks)
+    )(index.reshape(1), *blocks)
 
 
 def small_gather(row, axis):
@@ -301,11 +260,11 @@
 
 def small_reduce(rows, axis):
     own = lax.axis_index(axis)
-    for mask in reversed(bits_of(lax.axis_size(axis))):
-        half = rows.shape[0] // 2
+    for mask in bits_of(lax.axis_size(axis)):
+        pairs = rows.reshape(rows.shape[0] // 2, 2, rows.shape[1])
         upper = (own & mask) != 0
-        kept = jnp.where(upper, rows[half:], rows[:half])
-        sent = jnp.where(upper, rows[:half], rows[half:])
+        kept = jnp.where(upper, pairs[:, 1], pairs[:, 0])
+        sent = jnp.where(upper, pairs[:, 0], pairs[:, 1])
         rows = kept + swap(sent, axis, mask)
     return rows
 
@@ -346,7 +305,9 @@
     units = quarter * fsdp
     score_scale = head_width ** (-0.5)
 
-    silu_cond = jax.nn.silu(conditioning).astype(bf16)
+    attention_own = take_attention(qkv_weight[0], proj_weight[0], s, seq)
+    attention_own, vector = tie(attention_own, conditioning)
+    silu_cond = jax.nn.silu(vector).astype(bf16)
     shorts = [silu_cond, qkv_bias, proj_bias, fc1_bias, fc2_bias]
     gathered = small_gather(jnp.concatenate(shorts, axis=1), "fsdp")
     split = []
@@ -359,15 +320,14 @@
         part.astype(f32).reshape(1, -1) for part in split[1:]
     ]
 
-    attention_own = take_attention(qkv_weight[0], proj_weight[0], s, seq)
     attention_full = lax.all_gather(attention_own, "fsdp", axis=0, tiled=True)
     padded = lanes(3 * group)
     qkv_full = attention_full[:, :padded]
     proj_blocks = attention_full[:, padded:].reshape(seq, group, group)
-    proj_blocks = jnp.stack(
-        [lax.dynamic_index_in_dim(proj_blocks, s ^ k, 0, keepdims=False) for k in range(seq)]
-    )
-    proj_full = join_columns(seq_exchange(proj_blocks), s, 1, bf16)
+    proj_blocks = [
+        lax.dynamic_index_in_dim(proj_blocks, s ^ k, 0, keepdims=False) for k in range(seq)
+    ]
+    proj_full = join_columns(seq_exchange(proj_blocks), s, 1, group, bf16)
     forward_own = take_feed_forward(fc1_weight[0], fc2_weight[0], s, fsdp, seq)
 
     silu_own = lax.dynamic_slice_in_dim(silu_all, f * rows, rows, 1)
@@ -452,7 +412,7 @@
     fc2_grad = reduce_far(*fc2_near)
     proj_grad = split_columns(dot_rows(attended_flat, d_branch_low).astype(bf16), s, seq)
     proj_grad, d_branch_low = tie(proj_grad, d_branch_low)
-    proj_grad = seq_exchange(proj_grad)
+    proj_grad = seq_exchange([proj_grad[k] for k in range(seq)])
     d_attended = dot_back(d_branch_low, proj_full).astype(bf16).reshape(attended.shape)
     d_probs = jnp.einsum("qhd,khd->hqk", d_attended, value_rows, preferred_element_type=f32)
     delta = jnp.sum(d_attended.astype(f32) * attended.astype(f32), axis=-1).T
@@ -469,8 +429,8 @@
     d_input_attn = seq_reduce(d_input_part)
     fc1_grad = reduce_far(*fc1_near)
     qkv_grad = dot_rows(input_attn, d_packed).astype(bf16)
-    kept, sent = pack_near(qkv_grad, proj_grad, s, f % 2, fsdp)
-    attention_near = (kept, swap(sent, "fsdp", 1))
+    qkv_near = reduce_near(qkv_grad)
+    proj_near = reduce_near(join_rows(proj_grad, s, bf16))
     qkv_sum = jnp.sum(d_packed.astype(f32), axis=0, keepdims=True)
     d_scale_attn = jnp.sum(d_input_attn * norm_attn, axis=0, keepdims=True)
     d_shift_attn = jnp.sum(d_input_attn, axis=0, keepdims=True)
@@ -501,7 +461,7 @@
     every = small_gather(
         jnp.concatenate([sums, query_sum, value_sum, fc1_sum], axis=1), "fsdp"
     )
-    every, kept, received = tie(every, *attention_near)
+    every, *qkv_near = tie(every, *qkv_near)
     d_modulation = every[:, : 6 * width]
     weight_grad = lax.dot_general(
         silu_own.astype(f32),
@@ -531,10 +491,12 @@
     cond_sum = lax.dynamic_index_in_dim(cond_all, f, 1, keepdims=False).reshape(1, width)
     conditioning_grad = jax.vjp(jax.nn.silu, conditioning)[1](cond_sum)[0]
 
-    fc2_out = join_rows(seq_blocks(fc2_grad), s, f32)
-    fc1_out = join_columns(seq_blocks(fc1_grad), s, fsdp, f32)
-    attention_grad = reduce_far(kept, received)
-    qkv_out, proj_out = join_attention(seq_blocks(attention_grad), s, group)
+    fc2_out = join_rows(seq_blocks(fc2_grad.astype(bf16)), s, f32)
+    fc1_out = join_columns(seq_blocks(fc1_grad.astype(bf16)), s, fsdp, quarter, f32)
+    proj_grad = reduce_far(*proj_near)
+    qkv_grad = reduce_far(*qkv_near)
+    proj_out = join_columns(seq_blocks(proj_grad.astype(bf16)), s, 1, group, f32)
+    qkv_out = join_columns(seq_blocks(qkv_grad.astype(bf16)), s, 3, group, f32)
     return (
         output[None],
         latents_grad[None],

time: 444 us -> 440 us (level)
  other arithmetic: 52.2 us -> 37.1 us
  starting transfers between devices: 53.3 us -> 61.8 us
  local copies, waits for them, and re-layouts: 40.4 us -> 47.5 us
    concatenate x7 -> x2, other arithmetic: 14.1 us -> 3.63 us  [seq_gather(): return jnp.concatenate(seq_blocks(value), axis=0)]
    ppermute x61 -> x68, starting transfers between devices: 53.2 us -> 61.7 us  [swap(): return lax.ppermute(value, axis, pairs)]
    squeeze x2 -> x4, local copies, waits for them, and re-layouts: 0.21 us -> 5.05 us  [reduce_near(): sent = lax.dynamic_index_in_dim(blocks, 1 - near, 1, keepdims=False)]
    ppermute x61 -> x68, waiting for transfers between devices: 175 us -> 173 us  [swap(): return lax.ppermute(value, axis, pairs)]
    unnamed x129 -> x157, local copies, waits for them, and re-layouts: 16.4 us -> 16.4 us
  transfers between devices with their start and end apart: 63 -> 70, of which waited for: 27 -> 35; matrix products, arithmetic and copies ran while one was open for 23% -> 21% of each run, Pallas kernels for 5% -> 4%
where the time goes in v2:
time: 440 us; the launch traced here: 436 us
  waiting for transfers between devices  209 us (48%)
  starting transfers between devices  61.8 us (14%)
  local copies, waits for them, and re-layouts  47.5 us (11%)
  matrix products  41.1 us (9%)
  other arithmetic  37.1 us (8%)
  Pallas kernels  24.2 us (6%)
  between operations  15.9 us (4%)
    ppermute x68, waiting for transfers between devices, swap(): return lax.ppermute(value, axis, pairs)  173 us
    ppermute x68, starting transfers between devices, swap(): return lax.ppermute(value, axis, pairs)  61.7 us
    all_gather x1, waiting for transfers between devices, shards(): forward_full = lax.all_gather(forward_own, 'fsdp', axis=1, tiled=True)  22.2 us
    unnamed x157, local copies, waits for them, and re-layouts  16.4 us
    all_gather x1, waiting for transfers between devices, shards(): attention_full = lax.all_gather(attention_own, 'fsdp', axis=0, tiled=True)  14.1 us
    dot_general x5, matrix products, dot(): return jnp.dot(left, right, preferred_element_type=jnp.float32)  11.1 us
    pallas_call x4, Pallas kernels, join_columns(): pl.pallas_call(kernel, out_shape=jax.ShapeDtypeStruct((rows, parts * grou...  11.1 us
    dot_general x4, matrix products, dot_rows(): lax.dot_general(left, right, (((0,), (0,)), ((), ())), preferred_element_...  10.5 us
  transfers between devices with their start and end apart: 70, of which 35 were waited for; matrix products, arithmetic and copies ran while one was open for 21% of the time, Pallas kernels for 4%

profile of v2, /device:TPU:0, one launch (start us, length us, event | category | flops | bytes accessed | tf_op | source)
XLA Modules:
  0.0 436.5 jit_solution(8634144785316371267)
XLA Ops:
  7.3 2.3 take_attention.1
  11.1 3.0 collective-permute-start
  19.7 3.1 collective-permute-start.2
  23.0 2.8 take_feed_forward.1
  29.8 3.1 collective-permute-done.3
  34.9 3.9 collective-permute-done.4
  40.5 3.6 collective-permute-done.5
  47.7 7.6 %collective-permute-done.7 = bf16[128,1152]{1,0:T(8,128)(2,1)} collective-permute-done((bf16[128,1152]{1,0:T(8,128)(2,1)S(1)}, bf16[128,1152]{1,0:T(8,128)(2,1)}, u32[]{:S(2)}, u32[]{:S(2)}) %collective-permute-start.7) | collective-permute-done | bytes 294944 | tf_op jit(solution)/shard_map/ppermute | solution.py:47
  59.5 14.1 %all-gather.3.cloned.1.call-done = bf16[1152,1184]{1,0:T(8,128)(2,1)} async-done(((bf16[144,1184]{1,0:T(8,128)(2,1)}), bf16[1152,1184]{1,0:T(8,128)(2,1)}) %all-gather.3.cloned.1.call-update) | async-done | bytes 2727952 | tf_op jit(solution)/shard_map/all_gather | solution.py:323
  77.2 2.7 fusion.136
  86.1 9.0 %collective-permute-done.10 = bf16[2,288,288]{2,1,0:T(8,128)(2,1)} collective-permute-done((bf16[2,288,288]{2,1,0:T(8,128)(2,1)}, bf16[2,288,288]{2,1,0:T(8,128)(2,1)}, u32[]{:S(2)}, u32[]{:S(2)}) %collective-permute-start.10) | collective-permute-done | bytes 331808 | tf_op jit(solution)/shard_map/ppermute | solution.py:47
  96.9 2.4 join_columns.4
  105.4 7.6 %collective-permute-done.14 = bf16[128,1152]{1,0:T(8,128)(2,1)S(1)} collective-permute-done((bf16[128,1152]{1,0:T(8,128)(2,1)S(1)}, bf16[128,1152]{1,0:T(8,128)(2,1)S(1)}, u32[]{:S(2)}, u32[]{:S(2)}) %collective-permute-start.14) | collective-permute-done | bytes 294944 | tf_op jit(solution)/shard_map/ppermute | solution.py:47
  121.2 4.0 collective-permute-done.12
  130.7 4.7 %collective-permute-done.17 = bf16[128,1152]{1,0:T(8,128)(2,1)} collective-permute-done((bf16[128,1152]{1,0:T(8,128)(2,1)S(1)}, bf16[128,1152]{1,0:T(8,128)(2,1)}, u32[]{:S(2)}, u32[]{:S(2)}) %collective-permute-start.17) | collective-permute-done | bytes 294944 | tf_op jit(solution)/shard_map/ppermute | solution.py:47
  139.6 22.2 %all-gather.5.cloned.1.call-done = bf16[2,1152,1152]{2,1,0:T(8,128)(2,1)} async-done(((bf16[2,144,1152]{2,1,0:T(8,128)(2,1)}), bf16[2,1152,1152]{2,1,0:T(8,128)(2,1)}) %all-gather.5.cloned.1.call-update) | async-done | bytes 5308432 | tf_op jit(solution)/shard_map/all_gather | solution.py:350
  161.8 4.2 multiply_convert_fusion.1
  166.0 2.9 fusion.135
  168.9 3.0 convolution_convert_fusion.1
  183.0 7.6 %collective-permute-done.22 = bf16[1,128,1152]{2,1,0:T(8,128)(2,1)S(1)} collective-permute-done((bf16[1,128,1152]{2,1,0:T(8,128)(2,1)S(1)}, bf16[1,128,1152]{2,1,0:T(8,128)(2,1)S(1)}, u32[]{:S(2)}, u32[]{:S(2)}) %collective-permute-start.22) | collective-permute-done | bytes 294944 | tf_op jit(solution)/shard_map/ppermute | solution.py:47
  192.1 3.3 collective-permute-done.20
  199.4 5.0 %collective-permute-done.24 = bf16[128,1152]{1,0:T(8,128)(2,1)S(1)} collective-permute-done((bf16[128,1152]{1,0:T(8,128)(2,1)S(1)}, bf16[128,1152]{1,0:T(8,128)(2,1)S(1)}, u32[]{:S(2)}, u32[]{:S(2)}) %collective-permute-start.24) | collective-permute-done | bytes 294944 | tf_op jit(solution)/shard_map/ppermute | solution.py:47
  204.4 4.1 collective-permute-done.54
  213.5 22.5 %collective-permute-done.61 = bf16[4,144,1152]{2,1,0:T(8,128)(2,1)S(1)} collective-permute-done((bf16[4,144,1152]{2,1,0:T(8,128)(2,1)S(1)}, bf16[4,144,1152]{2,1,0:T(8,128)(2,1)S(1)}, u32[]{:S(2)}, u32[]{:S(2)}) %collective-permute-start.61) | collective-permute-done | bytes 1327136 | tf_op jit(solution)/shard_map/ppermute | solution.py:47
  239.5 2.3 collective-permute-start.64
  244.0 2.5 split_columns.1
  253.9 4.4 %convolution_convert_fusion.2 = bf16[1152,896]{1,0:T(8,128)(2,1)} fusion(bf16[512,1152]{1,0:T(8,128)(2,1)} %constant_dynamic-update-slice_fusion, bf16[512,288]{0,1:T(8,128)(2,1)S(1)} %bitcast.406, bf16[512,288]{0,1:T(8,128)(2,1)S(1)} %bitcast.412, bf16[512,288]{0,1:T(8,128)(2,1)S(1)} %bitcast.415, bf16[896]{0:T(1024)(128)(2,1)S(1)} %pad.27.clone), kind=kOutput, calls=%fused_computation.8 | convolution fusion | flops 1061666816 | bytes 4130560 | tf_op jit(solution)/shard_map/dot_general | solution.py:42
  264.8 3.0 dynamic-slice_bitcast_fusion.2
  277.2 11.0 %collective-permute-done.63 = bf16[144,1152]{1,0:T(8,128)(2,1)} collective-permute-done((bf16[144,1152]{1,0:T(8,128)(2,1)}, bf16[144,1152]{1,0:T(8,128)(2,1)}, u32[]{:S(2)}, u32[]{:S(2)}) %collective-permute-start.63) | collective-permute-done | bytes 331808 | tf_op jit(solution)/shard_map/ppermute | solution.py:47
  293.8 5.1 %collective-permute-done.59.refs_2_ = bf16[144,1152]{1,0:T(8,128)(2,1)} collective-permute-done((bf16[144,1152]{1,0:T(8,128)(2,1)S(1)}, bf16[144,1152]{1,0:T(8,128)(2,1)}, u32[]{:S(2)}, u32[]{:S(2)}) %collective-permute-start.59) | collective-permute-done | bytes 331808 | tf_op jit(solution)/shard_map/ppermute | solution.py:47
  300.4 5.7 %collective-permute-done.66.refs_2_ = bf16[144,1152]{1,0:T(8,128)(2,1)} collective-permute-done((bf16[144,1152]{1,0:T(8,128)(2,1)}, bf16[144,1152]{1,0:T(8,128)(2,1)}, u32[]{:S(2)}, u32[]{:S(2)}) %collective-permute-start.66) | collective-permute-done | bytes 331808 | tf_op jit(solution)/shard_map/ppermute | solution.py:47
  308.5 6.0 %collective-permute-done.46 = bf16[2,288,288]{2,1,0:T(8,128)(2,1)S(1)} collective-permute-done((bf16[2,288,288]{2,1,0:T(8,128)(2,1)S(1)}, bf16[2,288,288]{2,1,0:T(8,128)(2,1)S(1)}, u32[]{:S(2)}, u32[]{:S(2)}) %collective-permute-start.46) | collective-permute-done | bytes 331808 | tf_op jit(solution)/shard_map/ppermute | solution.py:47
  316.7 2.4 join_rows.2
  322.9 3.5 join_columns.7
  326.5 3.1 join_rows.3
  334.5 3.4 collective-permute-done.29
  338.7 16.2 %collective-permute-done.47 = bf16[4,144,288]{2,1,0:T(8,128)(2,1)} collective-permute-done((bf16[4,144,288]{2,1,0:T(8,128)(2,1)}, bf16[4,144,288]{2,1,0:T(8,128)(2,1)}, u32[]{:S(2)}, u32[]{:S(2)}) %collective-permute-start.47) | collective-permute-done | bytes 331808 | tf_op jit(solution)/shard_map/ppermute | solution.py:47
  356.4 2.4 collective-permute-start.50
  361.1 3.0 collective-permute-done.50
  364.1 2.3 collective-permute-done.49
  369.6 2.6 collective-permute-done.52.refs_2_
  376.5 6.9 %collective-permute-done.34 = f32[4,16128]{1,0:T(4,128)} collective-permute-done((f32[4,16128]{1,0:T(4,128)}, f32[4,16128]{1,0:T(4,128)}, u32[]{:S(2)}, u32[]{:S(2)}) %collective-permute-start.34) | collective-permute-done | bytes 258080 | tf_op jit(solution)/shard_map/ppermute | solution.py:47
  386.2 4.5 %convolution_bitcast_fusion = f32[1,144,6912]{2,1,0:T(8,128)} fusion(f32[8,16128]{1,0:T(8,128)S(1)} %pad_maximum_fusion.2, bf16[8,1152]{1,0:T(8,128)(2,1)} %copy-done.47, s32[]{:T(128)S(6)} %select_n.317, bf16[8,1152]{1,0:T(8,128)(2,1)} %copy-done.48), kind=kOutput, calls=%fused_computation | convolution fusion | flops 95556096 | bytes 4210692 | tf_op jit(solution)/shard_map/dot_general | solution.py:466
  395.8 2.9 collective-permute-start.39
  401.4 11.1 %collective-permute-done.37 = f32[2,1152]{1,0:T(2,128)S(1)} collective-permute-done((f32[2,1152]{1,0:T(2,128)S(1)}, f32[2,1152]{1,0:T(2,128)S(1)}, u32[]{:S(2)}, u32[]{:S(2)}) %collective-permute-start.37) | collective-permute-done | bytes 9248 | tf_op jit(solution)/shard_map/ppermute | solution.py:47
  412.6 3.4 collective-permute-start.38
  419.1 5.0 %collective-permute-done.43.refs_2_ = bf16[144,896]{1,0:T(8,128)(2,1)S(1)} collective-permute-done((bf16[144,896]{1,0:T(8,128)(2,1)S(1)}, bf16[144,896]{1,0:T(8,128)(2,1)S(1)}, u32[]{:S(2)}, u32[]{:S(2)}) %collective-permute-start.43) | collective-permute-done | bytes 258080 | tf_op jit(solution)/shard_map/ppermute | solution.py:47
  426.4 3.0 join_columns.5
  (440 shorter events, 155.7 us)
Async XLA Ops:
  7.2 66.3 %all-gather.3.cloned.1.call-start = ((), (), s32[]{:S(2)}) async-start(), calls=%async_computation | async-start | bytes 3317760 | tf_op jit(solution)/shard_map/all_gather | solution.py:323
  14.2 147.6 %all-gather.5.cloned.1.call-start = ((), (), s32[]{:S(2)}) async-start(), calls=%async_computation.1 | async-start | bytes 5971968 | tf_op jit(solution)/shard_map/all_gather | solution.py:350
  45.7 9.6 %collective-permute-start.6 = (bf16[128,1152]{1,0:T(8,128)(2,1)S(1)}, bf16[128,1152]{1,0:T(8,128)(2,1)}, u32[]{:S(2)}, u32[]{:S(2)}) collective-permute-start(bf16[128,1152]{1,0:T(8,128)(2,1)S(1)} %fusion.45), channel_id=1, source_target_pairs={{0,8},{8,0},{16,24},{24,16},{1,9},{9,1},{17,25},{25,17},{2,10},{10... | collective-permute-start | bytes 884744 | tf_op jit(solution)/shard_map/ppermute | solution.py:47
  45.8 9.5 %collective-permute-start.7 = (bf16[128,1152]{1,0:T(8,128)(2,1)S(1)}, bf16[128,1152]{1,0:T(8,128)(2,1)}, u32[]{:S(2)}, u32[]{:S(2)}) collective-permute-start(bf16[128,1152]{1,0:T(8,128)(2,1)S(1)} %fusion.45), channel_id=1, source_target_pairs={{0,16},{8,24},{16,0},{24,8},{1,17},{9,25},{17,1},{25,9},{2,18},{10... | collective-permute-start | bytes 884744 | tf_op jit(solution)/shard_map/ppermute | solution.py:47
  83.7 11.4 %collective-permute-start.10 = (bf16[2,288,288]{2,1,0:T(8,128)(2,1)}, bf16[2,288,288]{2,1,0:T(8,128)(2,1)}, u32[]{:S(2)}, u32[]{:S(2)}) collective-permute-start(bf16[2,288,288]{2,1,0:T(8,128)(2,1)} %pad_maximum_fusion.4), channel_id=1, source_target_pairs={{0,16},{8,24},{16,0},{24,8},{1,17},{9,25},{17,1},{25,9},{2,18},{10... | collective-permute-start | bytes 995336 | tf_op jit(solution)/shard_map/ppermute | solution.py:47
  103.6 9.4 %collective-permute-start.11 = (bf16[2,128,1152]{2,1,0:T(8,128)(2,1)}, bf16[2,128,1152]{2,1,0:T(8,128)(2,1)S(1)}, u32[]{:S(2)}, u32[]{:S(2)}) collective-permute-start(bf16[2,128,1152]{2,1,0:T(8,128)(2,1)} %fusion.54), channel_id=1, source_target_pairs={{0,8},{8,0},{16,24},{24,16},{1,9},{9,1},{17,25},{25,17},{2,10},{10... | collective-permute-start | bytes 1769480 | tf_op jit(solution)/shard_map/ppermute | solution.py:47
  103.6 9.4 %collective-permute-start.14 = (bf16[128,1152]{1,0:T(8,128)(2,1)S(1)}, bf16[128,1152]{1,0:T(8,128)(2,1)S(1)}, u32[]{:S(2)}, u32[]{:S(2)}) collective-permute-start(bf16[128,1152]{1,0:T(8,128)(2,1)S(1)} %fusion.68), channel_id=1, source_target_pairs={{0,16},{8,24},{16,0},{24,8},{1,17},{9,25},{17,1},{25,9},{2,18},{10... | collective-permute-start | bytes 884744 | tf_op jit(solution)/shard_map/ppermute | solution.py:47
  105.2 13.7 %collective-permute-start.13 = (bf16[128,1152]{1,0:T(8,128)(2,1)S(1)}, bf16[128,1152]{1,0:T(8,128)(2,1)}, u32[]{:S(2)}, u32[]{:S(2)}) collective-permute-start(bf16[128,1152]{1,0:T(8,128)(2,1)S(1)} %fusion.68), channel_id=1, source_target_pairs={{0,8},{8,0},{16,24},{24,16},{1,9},{9,1},{17,25},{25,17},{2,10},{10... | collective-permute-start | bytes 884744 | tf_op jit(solution)/shard_map/ppermute | solution.py:47
  115.7 9.4 %collective-permute-start.12 = (bf16[1,128,1152]{2,1,0:T(8,128)(2,1)S(1)}, bf16[1,128,1152]{2,1,0:T(8,128)(2,1)S(1)}, u32[]{:S(2)}, u32[]{:S(2)}) collective-permute-start(bf16[1,128,1152]{2,1,0:T(8,128)(2,1)S(1)} %fusion.76), channel_id=1, source_target_pairs={{0,16},{8,24},{16,0},{24,8},{1,17},{9,25},{17,1},{25,9},{2,18},{10... | collective-permute-start | bytes 884744 | tf_op jit(solution)/shard_map/ppermute | solution.py:47
  125.8 9.6 %collective-permute-start.16 = (bf16[128,1152]{1,0:T(8,128)(2,1)S(1)}, bf16[128,1152]{1,0:T(8,128)(2,1)}, u32[]{:S(2)}, u32[]{:S(2)}) collective-permute-start(bf16[128,1152]{1,0:T(8,128)(2,1)S(1)} %add_convert_fusion), channel_id=1, source_target_pairs={{0,8},{8,0},{16,24},{24,16},{1,9},{9,1},{17,25},{25,17},{2,10},{10... | collective-permute-start | bytes 884744 | tf_op jit(solution)/shard_map/ppermute | solution.py:47
  125.9 9.5 %collective-permute-start.17 = (bf16[128,1152]{1,0:T(8,128)(2,1)S(1)}, bf16[128,1152]{1,0:T(8,128)(2,1)}, u32[]{:S(2)}, u32[]{:S(2)}) collective-permute-start(bf16[128,1152]{1,0:T(8,128)(2,1)S(1)} %add_convert_fusion), channel_id=1, source_target_pairs={{0,16},{8,24},{16,0},{24,8},{1,17},{9,25},{17,1},{25,9},{2,18},{10... | collective-permute-start | bytes 884744 | tf_op jit(solution)/shard_map/ppermute | solution.py:47
  176.5 32.1 %collective-permute-start.54 = (bf16[4,144,1152]{2,1,0:T(8,128)(2,1)S(1)}, bf16[4,144,1152]{2,1,0:T(8,128)(2,1)S(1)}, u32[]{:S(2)}, u32[]{:S(2)}) collective-permute-start(bf16[4,144,1152]{2,1,0:T(8,128)(2,1)S(1)} %dynamic-slice_bitcast_fusion.1), channel_id=1, source_target_pairs={{0,1},{1,0},{2,3},{3,2},{4,5},{5,4},{6,7},{7,6},{8,9},{9,8},{10,11... | collective-permute-start | bytes 3981320 | tf_op jit(solution)/shard_map/ppermute | solution.py:47
  178.9 57.1 %collective-permute-start.61 = (bf16[4,144,1152]{2,1,0:T(8,128)(2,1)S(1)}, bf16[4,144,1152]{2,1,0:T(8,128)(2,1)S(1)}, u32[]{:S(2)}, u32[]{:S(2)}) collective-permute-start(bf16[4,144,1152]{2,1,0:T(8,128)(2,1)S(1)} %dynamic-slice_bitcast_fusion), channel_id=1, source_target_pairs={{0,1},{1,0},{2,3},{3,2},{4,5},{5,4},{6,7},{7,6},{8,9},{9,8},{10,11... | collective-permute-start | bytes 3981320 | tf_op jit(solution)/shard_map/ppermute | solution.py:47
  180.7 9.9 %collective-permute-start.22 = (bf16[1,128,1152]{2,1,0:T(8,128)(2,1)S(1)}, bf16[1,128,1152]{2,1,0:T(8,128)(2,1)S(1)}, u32[]{:S(2)}, u32[]{:S(2)}) collective-permute-start(bf16[1,128,1152]{2,1,0:T(8,128)(2,1)S(1)} %fusion.78), channel_id=1, source_target_pairs={{0,16},{8,24},{16,0},{24,8},{1,17},{9,25},{17,1},{25,9},{2,18},{10... | collective-permute-start | bytes 884744 | tf_op jit(solution)/shard_map/ppermute | solution.py:47
  182.4 13.0 %collective-permute-start.20 = (bf16[1,128,1152]{2,1,0:T(8,128)(2,1)S(1)}, bf16[1,128,1152]{2,1,0:T(8,128)(2,1)S(1)}, u32[]{:S(2)}, u32[]{:S(2)}) collective-permute-start(bf16[1,128,1152]{2,1,0:T(8,128)(2,1)S(1)} %fusion.77), channel_id=1, source_target_pairs={{0,16},{8,24},{16,0},{24,8},{1,17},{9,25},{17,1},{25,9},{2,18},{10... | collective-permute-start | bytes 884744 | tf_op jit(solution)/shard_map/ppermute | solution.py:47
  196.8 7.6 %collective-permute-start.24 = (bf16[128,1152]{1,0:T(8,128)(2,1)S(1)}, bf16[128,1152]{1,0:T(8,128)(2,1)S(1)}, u32[]{:S(2)}, u32[]{:S(2)}) collective-permute-start(bf16[128,1152]{1,0:T(8,128)(2,1)S(1)} %multiply_convert_fusion.2), channel_id=1, source_target_pairs={{0,16},{8,24},{16,0},{24,8},{1,17},{9,25},{17,1},{25,9},{2,18},{10... | collective-permute-start | bytes 884744 | tf_op jit(solution)/shard_map/ppermute | solution.py:47
  198.4 41.2 %collective-permute-start.23 = (bf16[128,1152]{1,0:T(8,128)(2,1)S(1)}, bf16[128,1152]{1,0:T(8,128)(2,1)S(1)}, u32[]{:S(2)}, u32[]{:S(2)}) collective-permute-start(bf16[128,1152]{1,0:T(8,128)(2,1)S(1)} %multiply_convert_fusion.2), channel_id=1, source_target_pairs={{0,8},{8,0},{16,24},{24,16},{1,9},{9,1},{17,25},{25,17},{2,10},{10... | collective-permute-start | bytes 884744 | tf_op jit(solution)/shard_map/ppermute | solution.py:47
  204.4 37.4 %collective-permute-start.25 = (bf16[128,1152]{1,0:T(8,128)(2,1)S(1)}, bf16[128,1152]{1,0:T(8,128)(2,1)S(1)}, u32[]{:S(2)}, u32[]{:S(2)}) collective-permute-start(bf16[128,1152]{1,0:T(8,128)(2,1)S(1)} %collective-permute-done.24), channel_id=1, source_target_pairs={{0,8},{8,0},{16,24},{24,16},{1,9},{9,1},{17,25},{25,17},{2,10},{10... | collective-permute-start | bytes 884744 | tf_op jit(solution)/shard_map/ppermute | solution.py:47
  211.4 61.9 %collective-permute-start.57 = (bf16[144,1152]{1,0:T(8,128)(2,1)}, bf16[144,1152]{1,0:T(8,128)(2,1)}, u32[]{:S(2)}, u32[]{:S(2)}) collective-permute-start(bf16[144,1152]{1,0:T(8,128)(2,1)} %get-tuple-element.78), channel_id=1, source_target_pairs={{0,6},{1,7},{2,4},{3,5},{4,2},{5,3},{6,0},{7,1},{8,14},{9,15},{10,... | collective-permute-start | bytes 995336 | tf_op jit(solution)/shard_map/ppermute | solution.py:47
  212.9 62.0 %collective-permute-start.56 = (bf16[144,1152]{1,0:T(8,128)(2,1)}, bf16[144,1152]{1,0:T(8,128)(2,1)}, u32[]{:S(2)}, u32[]{:S(2)}) collective-permute-start(bf16[144,1152]{1,0:T(8,128)(2,1)} %get-tuple-element.79), channel_id=1, source_target_pairs={{0,4},{1,5},{2,6},{3,7},{4,0},{5,1},{6,2},{7,3},{8,12},{9,13},{10,... | collective-permute-start | bytes 995336 | tf_op jit(solution)/shard_map/ppermute | solution.py:47
  236.0 38.9 %collective-permute-start.55 = (bf16[144,1152]{1,0:T(8,128)(2,1)}, bf16[144,1152]{1,0:T(8,128)(2,1)}, u32[]{:S(2)}, u32[]{:S(2)}) collective-permute-start(bf16[144,1152]{1,0:T(8,128)(2,1)} %get-tuple-element.77), channel_id=1, source_target_pairs={{0,2},{1,3},{2,0},{3,1},{4,6},{5,7},{6,4},{7,5},{8,10},{9,11},{10,... | collective-permute-start | bytes 995336 | tf_op jit(solution)/shard_map/ppermute | solution.py:47
  239.5 37.5 %collective-permute-start.64 = (bf16[144,1152]{1,0:T(8,128)(2,1)}, bf16[144,1152]{1,0:T(8,128)(2,1)}, u32[]{:S(2)}, u32[]{:S(2)}) collective-permute-start(bf16[144,1152]{1,0:T(8,128)(2,1)} %get-tuple-element.75), channel_id=1, source_target_pairs={{0,6},{1,7},{2,4},{3,5},{4,2},{5,3},{6,0},{7,1},{8,14},{9,15},{10,... | collective-permute-start | bytes 995336 | tf_op jit(solution)/shard_map/ppermute | solution.py:47
  271.6 16.6 %collective-permute-start.63 = (bf16[144,1152]{1,0:T(8,128)(2,1)}, bf16[144,1152]{1,0:T(8,128)(2,1)}, u32[]{:S(2)}, u32[]{:S(2)}) collective-permute-start(bf16[144,1152]{1,0:T(8,128)(2,1)} %get-tuple-element.76), channel_id=1, source_target_pairs={{0,4},{1,5},{2,6},{3,7},{4,0},{5,1},{6,2},{7,3},{8,12},{9,13},{10,... | collective-permute-start | bytes 995336 | tf_op jit(solution)/shard_map/ppermute | solution.py:47
  273.3 16.3 %collective-permute-start.62 = (bf16[144,1152]{1,0:T(8,128)(2,1)}, bf16[144,1152]{1,0:T(8,128)(2,1)S(1)}, u32[]{:S(2)}, u32[]{:S(2)}) collective-permute-start(bf16[144,1152]{1,0:T(8,128)(2,1)} %get-tuple-element.74), channel_id=1, source_target_pairs={{0,2},{1,3},{2,0},{3,1},{4,6},{5,7},{6,4},{7,5},{8,10},{9,11},{10,... | collective-permute-start | bytes 995336 | tf_op jit(solution)/shard_map/ppermute | solution.py:47
  274.9 31.2 %collective-permute-start.26 = (bf16[2,128,1152]{2,1,0:T(8,128)(2,1)}, bf16[2,128,1152]{2,1,0:T(8,128)(2,1)S(1)}, u32[]{:S(2)}, u32[]{:S(2)}) collective-permute-start(bf16[2,128,1152]{2,1,0:T(8,128)(2,1)} %fusion.57), channel_id=1, source_target_pairs={{0,8},{8,0},{16,24},{24,16},{1,9},{9,1},{17,25},{25,17},{2,10},{10... | collective-permute-start | bytes 1769480 | tf_op jit(solution)/shard_map/ppermute | solution.py:47
  274.9 16.9 %collective-permute-start.45 = (bf16[2,288,288]{2,1,0:T(8,128)(2,1)}, bf16[2,288,288]{2,1,0:T(8,128)(2,1)S(1)}, u32[]{:S(2)}, u32[]{:S(2)}) collective-permute-start(bf16[2,288,288]{2,1,0:T(8,128)(2,1)} %pad_maximum_fusion.5), channel_id=1, source_target_pairs={{0,8},{8,0},{16,24},{24,16},{1,9},{9,1},{17,25},{25,17},{2,10},{10... | collective-permute-start | bytes 995336 | tf_op jit(solution)/shard_map/ppermute | solution.py:47
  277.0 43.9 %collective-permute-start.58 = (bf16[144,1152]{1,0:T(8,128)(2,1)S(1)}, bf16[144,1152]{1,0:T(8,128)(2,1)}, u32[]{:S(2)}, u32[]{:S(2)}) collective-permute-start(bf16[144,1152]{1,0:T(8,128)(2,1)S(1)} %fusion.43.refs_0_), channel_id=1, source_target_pairs={{0,8},{8,0},{16,24},{24,16},{1,9},{9,1},{17,25},{25,17},{2,10},{10... | collective-permute-start | bytes 995336 | tf_op jit(solution)/shard_map/ppermute | solution.py:47
  288.2 10.8 %collective-permute-start.59 = (bf16[144,1152]{1,0:T(8,128)(2,1)S(1)}, bf16[144,1152]{1,0:T(8,128)(2,1)}, u32[]{:S(2)}, u32[]{:S(2)}) collective-permute-start(bf16[144,1152]{1,0:T(8,128)(2,1)S(1)} %fusion.43.refs_0_), channel_id=1, source_target_pairs={{0,16},{8,24},{16,0},{24,8},{1,17},{9,25},{17,1},{25,9},{2,18},{10... | collective-permute-start | bytes 995336 | tf_op jit(solution)/shard_map/ppermute | solution.py:47
  291.8 34.7 %collective-permute-start.65 = (bf16[144,1152]{1,0:T(8,128)(2,1)}, bf16[144,1152]{1,0:T(8,128)(2,1)}, u32[]{:S(2)}, u32[]{:S(2)}) collective-permute-start(bf16[144,1152]{1,0:T(8,128)(2,1)} %fusion.40.refs_0_), channel_id=1, source_target_pairs={{0,8},{8,0},{16,24},{24,16},{1,9},{9,1},{17,25},{25,17},{2,10},{10... | collective-permute-start | bytes 995336 | tf_op jit(solution)/shard_map/ppermute | solution.py:47
  291.8 14.2 %collective-permute-start.66 = (bf16[144,1152]{1,0:T(8,128)(2,1)}, bf16[144,1152]{1,0:T(8,128)(2,1)}, u32[]{:S(2)}, u32[]{:S(2)}) collective-permute-start(bf16[144,1152]{1,0:T(8,128)(2,1)} %fusion.40.refs_0_), channel_id=1, source_target_pairs={{0,16},{8,24},{16,0},{24,8},{1,17},{9,25},{17,1},{25,9},{2,18},{10... | collective-permute-start | bytes 995336 | tf_op jit(solution)/shard_map/ppermute | solution.py:47
  299.0 15.5 %collective-permute-start.46 = (bf16[2,288,288]{2,1,0:T(8,128)(2,1)S(1)}, bf16[2,288,288]{2,1,0:T(8,128)(2,1)S(1)}, u32[]{:S(2)}, u32[]{:S(2)}) collective-permute-start(bf16[2,288,288]{2,1,0:T(8,128)(2,1)S(1)} %pad_maximum_fusion.6), channel_id=1, source_target_pairs={{0,16},{8,24},{16,0},{24,8},{1,17},{9,25},{17,1},{25,9},{2,18},{10... | collective-permute-start | bytes 995336 | tf_op jit(solution)/shard_map/ppermute | solution.py:47
  306.1 15.4 %collective-permute-start.60 = (bf16[144,1152]{1,0:T(8,128)(2,1)}, bf16[144,1152]{1,0:T(8,128)(2,1)}, u32[]{:S(2)}, u32[]{:S(2)}) collective-permute-start(bf16[144,1152]{1,0:T(8,128)(2,1)} %collective-permute-done.59.refs_2_), channel_id=1, source_target_pairs={{0,8},{8,0},{16,24},{24,16},{1,9},{9,1},{17,25},{25,17},{2,10},{10... | collective-permute-start | bytes 995336 | tf_op jit(solution)/shard_map/ppermute | solution.py:47
  306.1 20.4 %collective-permute-start.67 = (bf16[144,1152]{1,0:T(8,128)(2,1)}, bf16[144,1152]{1,0:T(8,128)(2,1)}, u32[]{:S(2)}, u32[]{:S(2)}) collective-permute-start(bf16[144,1152]{1,0:T(8,128)(2,1)} %collective-permute-done.66.refs_2_), channel_id=1, source_target_pairs={{0,8},{8,0},{16,24},{24,16},{1,9},{9,1},{17,25},{25,17},{2,10},{10... | collective-permute-start | bytes 995336 | tf_op jit(solution)/shard_map/ppermute | solution.py:47
  314.5 15.2 %collective-permute-start.27 = (bf16[1,128,1152]{2,1,0:T(8,128)(2,1)}, bf16[1,128,1152]{2,1,0:T(8,128)(2,1)S(1)}, u32[]{:S(2)}, u32[]{:S(2)}) collective-permute-start(bf16[1,128,1152]{2,1,0:T(8,128)(2,1)} %fusion.79), channel_id=1, source_target_pairs={{0,16},{8,24},{16,0},{24,8},{1,17},{9,25},{17,1},{25,9},{2,18},{10... | collective-permute-start | bytes 884744 | tf_op jit(solution)/shard_map/ppermute | solution.py:47
  320.9 63.7 %collective-permute-start.35 = (bf16[4,144,896]{2,1,0:T(8,128)(2,1)}, bf16[4,144,896]{2,1,0:T(8,128)(2,1)}, u32[]{:S(2)}, u32[]{:S(2)}) collective-permute-start(bf16[4,144,896]{2,1,0:T(8,128)(2,1)} %get-tuple-element.72), channel_id=1, source_target_pairs={{0,1},{1,0},{2,3},{3,2},{4,5},{5,4},{6,7},{7,6},{8,9},{9,8},{10,11... | collective-permute-start | bytes 3096584 | tf_op jit(solution)/shard_map/ppermute | solution.py:47
  321.4 33.5 %collective-permute-start.47 = (bf16[4,144,288]{2,1,0:T(8,128)(2,1)}, bf16[4,144,288]{2,1,0:T(8,128)(2,1)}, u32[]{:S(2)}, u32[]{:S(2)}) collective-permute-start(bf16[4,144,288]{2,1,0:T(8,128)(2,1)} %dynamic-slice_bitcast_fusion.4), channel_id=1, source_target_pairs={{0,1},{1,0},{2,3},{3,2},{4,5},{5,4},{6,7},{7,6},{8,9},{9,8},{10,11... | collective-permute-start | bytes 995336 | tf_op jit(solution)/shard_map/ppermute | solution.py:47
  338.1 22.7 %collective-permute-start.32 = (f32[1,16128]{1,0:T(1,128)S(1)}, f32[1,16128]{1,0:T(1,128)S(1)}, u32[]{:S(2)}, u32[]{:S(2)}) collective-permute-start(f32[1,16128]{1,0:T(1,128)S(1)} %pad_maximum_fusion.9), channel_id=1, source_target_pairs={{0,1},{1,0},{2,3},{3,2},{4,5},{5,4},{6,7},{7,6},{8,9},{9,8},{10,11... | collective-permute-start | bytes 193544 | tf_op jit(solution)/shard_map/ppermute | solution.py:47
  356.4 7.8 %collective-permute-start.50 = (bf16[144,288]{1,0:T(8,128)(2,1)S(1)}, bf16[144,288]{1,0:T(8,128)(2,1)S(1)}, u32[]{:S(2)}, u32[]{:S(2)}) collective-permute-start(bf16[144,288]{1,0:T(8,128)(2,1)S(1)} %get-tuple-element.97), channel_id=1, source_target_pairs={{0,6},{1,7},{2,4},{3,5},{4,2},{5,3},{6,0},{7,1},{8,14},{9,15},{10,... | collective-permute-start | bytes 248840 | tf_op jit(solution)/shard_map/ppermute | solution.py:47
  358.7 7.7 %collective-permute-start.49 = (bf16[144,288]{1,0:T(8,128)(2,1)S(1)}, bf16[144,288]{1,0:T(8,128)(2,1)S(1)}, u32[]{:S(2)}, u32[]{:S(2)}) collective-permute-start(bf16[144,288]{1,0:T(8,128)(2,1)S(1)} %get-tuple-element.98), channel_id=1, source_target_pairs={{0,4},{1,5},{2,6},{3,7},{4,0},{5,1},{6,2},{7,3},{8,12},{9,13},{10,... | collective-permute-start | bytes 248840 | tf_op jit(solution)/shard_map/ppermute | solution.py:47
  358.7 7.8 %collective-permute-start.48 = (bf16[144,288]{1,0:T(8,128)(2,1)S(1)}, bf16[144,288]{1,0:T(8,128)(2,1)S(1)}, u32[]{:S(2)}, u32[]{:S(2)}) collective-permute-start(bf16[144,288]{1,0:T(8,128)(2,1)S(1)} %get-tuple-element.96), channel_id=1, source_target_pairs={{0,2},{1,3},{2,0},{3,1},{4,6},{5,7},{6,4},{7,5},{8,10},{9,11},{10,... | collective-permute-start | bytes 248840 | tf_op jit(solution)/shard_map/ppermute | solution.py:47
  361.1 6.9 %collective-permute-start.33 = (f32[2,16128]{1,0:T(2,128)S(1)}, f32[2,16128]{1,0:T(2,128)S(1)}, u32[]{:S(2)}, u32[]{:S(2)}) collective-permute-start(f32[2,16128]{1,0:T(2,128)S(1)} %pad_maximum_fusion.8), channel_id=1, source_target_pairs={{0,2},{1,3},{2,0},{3,1},{4,6},{5,7},{6,4},{7,5},{8,10},{9,11},{10,... | collective-permute-start | bytes 387080 | tf_op jit(solution)/shard_map/ppermute | solution.py:47
  366.7 7.1 %collective-permute-start.51 = (bf16[144,288]{1,0:T(8,128)(2,1)S(1)}, bf16[144,288]{1,0:T(8,128)(2,1)S(1)}, u32[]{:S(2)}, u32[]{:S(2)}) collective-permute-start(bf16[144,288]{1,0:T(8,128)(2,1)S(1)} %fusion.84.refs_0_), channel_id=1, source_target_pairs={{0,8},{8,0},{16,24},{24,16},{1,9},{9,1},{17,25},{25,17},{2,10},{10... | collective-permute-start | bytes 248840 | tf_op jit(solution)/shard_map/ppermute | solution.py:47
  369.0 14.4 %collective-permute-start.34 = (f32[4,16128]{1,0:T(4,128)}, f32[4,16128]{1,0:T(4,128)}, u32[]{:S(2)}, u32[]{:S(2)}) collective-permute-start(f32[4,16128]{1,0:T(4,128)} %pad_maximum_fusion.7), channel_id=1, source_target_pairs={{0,4},{1,5},{2,6},{3,7},{4,0},{5,1},{6,2},{7,3},{8,12},{9,13},{10,... | collective-permute-start | bytes 774152 | tf_op jit(solution)/shard_map/ppermute | solution.py:47
  391.1 9.5 %collective-permute-start.36 = (f32[1,1152]{1,0:T(1,128)S(1)}, f32[1,1152]{1,0:T(1,128)S(1)}, u32[]{:S(2)}, u32[]{:S(2)}) collective-permute-start(f32[1,1152]{1,0:T(1,128)S(1)} %reshape.449), channel_id=1, source_target_pairs={{0,1},{1,0},{2,3},{3,2},{4,5},{5,4},{6,7},{7,6},{8,9},{9,8},{10,11... | collective-permute-start | bytes 13832 | tf_op jit(solution)/shard_map/ppermute | solution.py:47
  394.3 21.7 %collective-permute-start.41 = (bf16[144,896]{1,0:T(8,128)(2,1)S(1)}, bf16[144,896]{1,0:T(8,128)(2,1)S(1)}, u32[]{:S(2)}, u32[]{:S(2)}) collective-permute-start(bf16[144,896]{1,0:T(8,128)(2,1)S(1)} %get-tuple-element.81), channel_id=1, source_target_pairs={{0,6},{1,7},{2,4},{3,5},{4,2},{5,3},{6,0},{7,1},{8,14},{9,15},{10,... | collective-permute-start | bytes 774152 | tf_op jit(solution)/shard_map/ppermute | solution.py:47
  395.8 21.5 %collective-permute-start.40 = (bf16[144,896]{1,0:T(8,128)(2,1)S(1)}, bf16[144,896]{1,0:T(8,128)(2,1)S(1)}, u32[]{:S(2)}, u32[]{:S(2)}) collective-permute-start(bf16[144,896]{1,0:T(8,128)(2,1)S(1)} %get-tuple-element.82), channel_id=1, source_target_pairs={{0,4},{1,5},{2,6},{3,7},{4,0},{5,1},{6,2},{7,3},{8,12},{9,13},{10,... | collective-permute-start | bytes 774152 | tf_op jit(solution)/shard_map/ppermute | solution.py:47
  395.8 21.5 %collective-permute-start.39 = (bf16[144,896]{1,0:T(8,128)(2,1)S(1)}, bf16[144,896]{1,0:T(8,128)(2,1)S(1)}, u32[]{:S(2)}, u32[]{:S(2)}) collective-permute-start(bf16[144,896]{1,0:T(8,128)(2,1)S(1)} %get-tuple-element.80), channel_id=1, source_target_pairs={{0,2},{1,3},{2,0},{3,1},{4,6},{5,7},{6,4},{7,5},{8,10},{9,11},{10,... | collective-permute-start | bytes 774152 | tf_op jit(solution)/shard_map/ppermute | solution.py:47
  400.7 11.9 %collective-permute-start.37 = (f32[2,1152]{1,0:T(2,128)S(1)}, f32[2,1152]{1,0:T(2,128)S(1)}, u32[]{:S(2)}, u32[]{:S(2)}) collective-permute-start(f32[2,1152]{1,0:T(2,128)S(1)} %pad_maximum_fusion.16), channel_id=1, source_target_pairs={{0,2},{1,3},{2,0},{3,1},{4,6},{5,7},{6,4},{7,5},{8,10},{9,11},{10,... | collective-permute-start | bytes 27656 | tf_op jit(solution)/shard_map/ppermute | solution.py:47
  (95 other events, 1507.9 us)
Sparse Core Ops, SparseCore 0:
  14.3 59.2 all-gather.2
  76.4 85.3 all-gather.4

commit v3 on v2

--- a/solution.py
+++ b/solution.py
@@ -95,6 +95,20 @@
     return lax.optimization_barrier(values)
 
 
+def fsdp_gather(block):
+    own = lax.axis_index("fsdp")
+    count = lax.axis_size("fsdp") // 2
+    stack = jnp.zeros((count,) + block.shape, block.dtype)
+    for k in range(count):
+        part = swap(block, "fsdp", 2 * k) if k else block
+        stack = lax.dynamic_update_slice_in_dim(stack, part[None], (own // 2) ^ k, 0)
+    other = swap(stack, "fsdp", 1)
+    upper = own % 2 == 1
+    first = jnp.where(upper, other, stack)
+    second = jnp.where(upper, stack, other)
+    return jnp.stack([first, second], axis=1).reshape((-1,) + block.shape[1:])
+
+
 def reduce_near(partial):
     size = lax.axis_size("fsdp")
     near = lax.axis_index("fsdp") % 2
@@ -110,10 +124,13 @@
     pair = kept.astype(jnp.float32) + received.astype(jnp.float32)
     total = lax.dynamic_index_in_dim(pair, far, 0, keepdims=False)
     low = pair.astype(jnp.bfloat16)
+    received = []
     for k in range(1, pair.shape[0]):
         piece = lax.dynamic_index_in_dim(low, far ^ k, 0, keepdims=False)
-        total = total + swap(piece, "fsdp", 2 * k).astype(jnp.float32)
-    return total
+        received.append(swap(piece, "fsdp", 2 * k))
+    for part in received:
+        total = total + part.astype(jnp.float32)
+    return total.astype(jnp.bfloat16)
 
 
 def lanes(columns):
@@ -133,24 +150,25 @@
 def take_attention(qkv, proj, index, parts):
     rows = qkv.shape[0]
     used = qkv.shape[1] // parts
-    columns = lanes(used) + proj.shape[1] // parts
-
-    def kernel(at_ref, qkv_ref, proj_ref, target):
+
+    def kernel(at_ref, qkv_ref, proj_ref, target, proj_target):
         for part in range(parts):
 
             @pl.when(at_ref[0] == part)
             def _():
                 pieces = own_columns_of(qkv_ref[...], part, 3, parts)
                 pieces.append(jnp.zeros((rows, lanes(used) - used), qkv.dtype))
-                pieces += own_columns_of(proj_ref[...], part, 1, parts)
                 target[...] = jnp.concatenate(pieces, axis=1)
+                proj_target[...] = own_columns_of(proj_ref[...], part, 1, parts)[0]
 
     return pl.pallas_call(
         kernel,
-        out_shape=jax.ShapeDtypeStruct((rows, columns), qkv.dtype),
+        out_shape=[
+            jax.ShapeDtypeStruct((rows, lanes(used)), qkv.dtype),
+            jax.ShapeDtypeStruct((rows, proj.shape[1] // parts), proj.dtype),
+        ],
         in_specs=[pl.BlockSpec(memory_space=pltpu.SMEM)] + in_vmem(2),
-        out_specs=in_vmem(1)[0],
-        name="take_attention",
+        out_specs=in_vmem(2),
     )(index.reshape(1), qkv, proj)
 
 
@@ -172,7 +190,6 @@
         out_shape=jax.ShapeDtypeStruct((2, rows, width), fc1.dtype),
         in_specs=[pl.BlockSpec(memory_space=pltpu.SMEM)] + in_vmem(2),
         out_specs=in_vmem(1)[0],
-        name="take_feed_forward",
     )(index.reshape(1), fc1, fc2)
 
 
@@ -202,7 +219,6 @@
         out_shape=jax.ShapeDtypeStruct((parts, rows, span), whole.dtype),
         in_specs=[pl.BlockSpec(memory_space=pltpu.SMEM)] + in_vmem(1),
         out_specs=in_vmem(1)[0],
-        name="split_columns",
     )(index.reshape(1), whole)
 
 
@@ -223,7 +239,6 @@
         out_shape=jax.ShapeDtypeStruct((rows, parts * groups * span), dtype),
         in_specs=[pl.BlockSpec(memory_space=pltpu.SMEM)] + in_vmem(parts),
         out_specs=in_vmem(1)[0],
-        name="join_columns",
     )(index.reshape(1), *blocks)
 
 
@@ -242,7 +257,6 @@
         out_shape=jax.ShapeDtypeStruct((parts * rows, columns), dtype),
         in_specs=[pl.BlockSpec(memory_space=pltpu.SMEM)] + in_vmem(parts),
         out_specs=in_vmem(1)[0],
-        name="join_rows",
     )(index.reshape(1), *blocks)
 
 
@@ -305,7 +319,7 @@
     units = quarter * fsdp
     score_scale = head_width ** (-0.5)
 
-    attention_own = take_attention(qkv_weight[0], proj_weight[0], s, seq)
+    attention_own, proj_own = take_attention(qkv_weight[0], proj_weight[0], s, seq)
     attention_own, vector = tie(attention_own, conditioning)
     silu_cond = jax.nn.silu(vector).astype(bf16)
     shorts = [silu_cond, qkv_bias, proj_bias, fc1_bias, fc2_bias]
@@ -320,14 +334,8 @@
         part.astype(f32).reshape(1, -1) for part in split[1:]
     ]
 
-    attention_full = lax.all_gather(attention_own, "fsdp", axis=0, tiled=True)
+    qkv_full = lax.all_gather(attention_own, "fsdp", axis=0, tiled=True)
     padded = lanes(3 * group)
-    qkv_full = attention_full[:, :padded]
-    proj_blocks = attention_full[:, padded:].reshape(seq, group, group)
-    proj_blocks = [
-        lax.dynamic_index_in_dim(proj_blocks, s ^ k, 0, keepdims=False) for k in range(seq)
-    ]
-    proj_full = join_columns(seq_exchange(proj_blocks), s, 1, group, bf16)
     forward_own = take_feed_forward(fc1_weight[0], fc2_weight[0], s, fsdp, seq)
 
     silu_own = lax.dynamic_slice_in_dim(silu_all, f * rows, rows, 1)
@@ -345,8 +353,13 @@
 
     norm_attn, inv_attn = layer_norm(hidden)
     low_attn = (norm_attn * (1.0 + scale_attn) + shift_attn).astype(bf16)
-    low_attn, forward_own = tie(low_attn, forward_own)
+    low_attn, forward_own, proj_own = tie(low_attn, forward_own, proj_own)
     input_attn = seq_gather(low_attn)
+    proj_blocks = fsdp_gather(proj_own).reshape(seq, group, group)
+    proj_blocks = [
+        lax.dynamic_index_in_dim(proj_blocks, s ^ k, 0, keepdims=False) for k in range(seq)
+    ]
+    proj_full = join_columns(seq_exchange(proj_blocks), s, 1, group, bf16)
     forward_full = lax.all_gather(forward_own, "fsdp", axis=1, tiled=True)
     fc1_full, fc2_full = forward_full[0], forward_full[1]
     d_result = upstream * gate_mlp
@@ -388,7 +401,8 @@
     before = dot(input_mlp, fc1_full) + fc1_offset_own
     activated, pullback = jax.vjp(gelu_tanh, before)
     act_low = activated.astype(bf16)
-    d_before = pullback(dot_back(d_result_low, fc2_full))[0]
+    d_activated = dot_back(d_result_low, fc2_full)
+    d_before = pullback(d_activated)[0]
     d_before_low = d_before.astype(bf16)
     fc2_near = reduce_near(dot_rows(act_low, d_result_low))
     d_input_part = dot_back(d_before_low, fc1_full)
@@ -396,8 +410,6 @@
     d_input_part, act_late = tie(d_input_part, act_low)
     d_input_mlp = seq_reduce(d_input_part)
     result = seq_reduce(dot(act_late, fc2_full)) + fc2_offset
-    output = middle + gate_mlp * result
-    d_gate_mlp = jnp.sum(upstream * result, axis=0, keepdims=True)
     fc2_bias_part = jnp.sum(d_result, axis=0, keepdims=True)
     fc1_bias_part = jnp.sum(d_before, axis=0, keepdims=True)
     d_scale_mlp = jnp.sum(d_input_mlp * norm_mlp, axis=0, keepdims=True)
@@ -408,6 +420,9 @@
     d_gate_attn = jnp.sum(d_middle * branch, axis=0, keepdims=True)
     proj_bias_part = jnp.sum(d_branch, axis=0, keepdims=True)
     low_branch = d_branch.astype(bf16)
+    low_branch, late_upstream, late_middle = tie(low_branch, upstream, middle)
+    output = late_middle + gate_mlp * result
+    d_gate_mlp = jnp.sum(late_upstream * result, axis=0, keepdims=True)
     d_branch_low = seq_gather(low_branch)
     fc2_grad = reduce_far(*fc2_near)
     proj_grad = split_columns(dot_rows(attended_flat, d_branch_low).astype(bf16), s, seq)
@@ -436,21 +451,17 @@
     d_shift_attn = jnp.sum(d_input_attn, axis=0, keepdims=True)
     latents_grad = d_middle + norm_back(d_input_attn * (1.0 + scale_attn), norm_attn, inv_attn)
 
-    sums = seq_sum(
-        jnp.concatenate(
-            [
-                d_shift_attn,
-                d_scale_attn,
-                d_gate_attn,
-                d_shift_mlp,
-                d_scale_mlp,
-                d_gate_mlp,
-                proj_bias_part,
-                fc2_bias_part,
-            ],
-            axis=1,
-        )
-    )
+    parts = [
+        d_shift_attn,
+        d_scale_attn,
+        d_gate_attn,
+        d_shift_mlp,
+        d_scale_mlp,
+        d_gate_mlp,
+        proj_bias_part,
+        fc2_bias_part,
+    ]
+    sums = seq_sum(jnp.concatenate(parts, axis=1))
     own_columns = jnp.concatenate(
         [qkv_sum[:, :group], qkv_sum[:, 2 * group : 3 * group], fc1_bias_part], axis=1
     )
@@ -458,10 +469,10 @@
     query_sum = columns[:, :group].reshape(1, -1)
     value_sum = columns[:, group : 2 * group].reshape(1, -1)
     fc1_sum = jnp.moveaxis(columns[:, 2 * group :].reshape(seq, fsdp, quarter), 0, 1).reshape(1, -1)
-    every = small_gather(
-        jnp.concatenate([sums, query_sum, value_sum, fc1_sum], axis=1), "fsdp"
-    )
+    row = jnp.concatenate([sums, query_sum, value_sum, fc1_sum], axis=1)
+    every = small_gather(row.astype(bf16), "fsdp")
     every, *qkv_near = tie(every, *qkv_near)
+    every = every.astype(f32)
     d_modulation = every[:, : 6 * width]
     weight_grad = lax.dot_general(
         silu_own.astype(f32),
@@ -491,12 +502,12 @@
     cond_sum = lax.dynamic_index_in_dim(cond_all, f, 1, keepdims=False).reshape(1, width)
     conditioning_grad = jax.vjp(jax.nn.silu, conditioning)[1](cond_sum)[0]
 
-    fc2_out = join_rows(seq_blocks(fc2_grad.astype(bf16)), s, f32)
-    fc1_out = join_columns(seq_blocks(fc1_grad.astype(bf16)), s, fsdp, quarter, f32)
+    fc2_out = join_rows(seq_blocks(fc2_grad), s, f32)
+    fc1_out = join_columns(seq_blocks(fc1_grad), s, fsdp, quarter, f32)
     proj_grad = reduce_far(*proj_near)
     qkv_grad = reduce_far(*qkv_near)
-    proj_out = join_columns(seq_blocks(proj_grad.astype(bf16)), s, 1, group, f32)
-    qkv_out = join_columns(seq_blocks(qkv_grad.astype(bf16)), s, 3, group, f32)
+    proj_out = join_columns(seq_blocks(proj_grad), s, 1, group, f32)
+    qkv_out = join_columns(seq_blocks(qkv_grad), s, 3, group, f32)
     return (
         output[None],
         latents_grad[None],

time: 440 us -> 450 us (1.023)
  waiting for transfers between devices: 209 us -> 186 us
  starting transfers between devices: 61.8 us -> 76.2 us
  local copies, waits for them, and re-layouts: 47.5 us -> 60.6 us
    ppermute x68 -> x72, starting transfers between devices: 61.7 us -> 76.1 us  [swap(): return lax.ppermute(value, axis, pairs)]
    all_gather x1, waiting for transfers between devices: 14.1 us -> 0.01 us  [shards(): qkv_full = lax.all_gather(attention_own, 'fsdp', axis=0, tiled=True)]
    unnamed x157 -> x152, local copies, waits for them, and re-layouts: 16.4 us -> 28 us
    ppermute x68 -> x72, waiting for transfers between devices: 173 us -> 168 us  [swap(): return lax.ppermute(value, axis, pairs)]
  transfers between devices with their start and end apart: 70 -> 74, of which waited for: 35 -> 32; matrix products, arithmetic and copies ran while one was open for 21% -> 26% of each run, Pallas kernels for 4% -> 4%
where the time goes in v3:
time: 450 us; the launch traced here: 445 us
  waiting for transfers between devices  186 us (41%)
  starting transfers between devices  76.2 us (17%)
  local copies, waits for them, and re-layouts  60.6 us (13%)
  other arithmetic  41.3 us (9%)
  matrix products  41 us (9%)
  Pallas kernels  24.7 us (5%)
  between operations  15.7 us (3%)
    ppermute x72, waiting for transfers between devices, swap(): return lax.ppermute(value, axis, pairs)  168 us
    ppermute x72, starting transfers between devices, swap(): return lax.ppermute(value, axis, pairs)  76.1 us
    unnamed x152, local copies, waits for them, and re-layouts  28 us
    all_gather x1, waiting for transfers between devices, shards(): forward_full = lax.all_gather(forward_own, 'fsdp', axis=1, tiled=True)  17.9 us
    dot_general x5, matrix products, dot(): return jnp.dot(left, right, preferred_element_type=jnp.float32)  11.9 us
    pallas_call x4, Pallas kernels, join_columns(): pl.pallas_call(kernel, out_shape=jax.ShapeDtypeStruct((rows, parts * grou...  11 us
    dot_general x4, matrix products, dot_rows(): lax.dot_general(left, right, (((0,), (0,)), ((), ())), preferred_element_...  9.13 us
  transfers between devices with their start and end apart: 74, of which 32 were waited for; matrix products, arithmetic and copies ran while one was open for 26% of the time, Pallas kernels for 4%

profile of v3, /device:TPU:0, one launch (start us, length us, event | category | flops | bytes accessed | tf_op | source)
XLA Modules:
  0.0 445.2 jit_solution(11462615032885147960)
XLA Ops:
  7.3 2.3 shard_map.228
  11.1 3.0 collective-permute-start
  19.7 3.1 collective-permute-start.2
  28.1 3.4 shard_map.229
  33.8 2.7 collective-permute-done.4
  36.6 2.7 collective-permute-start.5
  45.0 2.9 collective-permute-start.10
  48.0 6.2 %collective-permute-done.9 = bf16[144,288]{1,0:T(8,128)(2,1)S(1)} collective-permute-done((bf16[144,288]{1,0:T(8,128)(2,1)S(1)}, bf16[144,288]{1,0:T(8,128)(2,1)S(1)}, u32[]{:S(2)}, u32[]{:S(2)}) %collective-permute-start.9) | collective-permute-done | bytes 82976 | tf_op jit(solution)/shard_map/ppermute | solution.py:47
  54.3 6.2 %collective-permute-done.10 = bf16[144,288]{1,0:T(8,128)(2,1)S(1)} collective-permute-done((bf16[144,288]{1,0:T(8,128)(2,1)S(1)}, bf16[144,288]{1,0:T(8,128)(2,1)S(1)}, u32[]{:S(2)}, u32[]{:S(2)}) %collective-permute-start.10) | collective-permute-done | bytes 82976 | tf_op jit(solution)/shard_map/ppermute | solution.py:47
  64.6 4.4 collective-permute-done.12
  77.0 9.8 %collective-permute-done.14 = bf16[2,288,288]{2,1,0:T(8,128)(2,1)S(1)} collective-permute-done((bf16[2,288,288]{2,1,0:T(8,128)(2,1)S(1)}, bf16[2,288,288]{2,1,0:T(8,128)(2,1)S(1)}, u32[]{:S(2)}, u32[]{:S(2)}) %collective-permute-start.14) | collective-permute-done | bytes 331808 | tf_op jit(solution)/shard_map/ppermute | solution.py:47
  87.7 2.4 shard_map.230
  90.1 3.4 fusion.140
  104.1 8.0 %collective-permute-done.18 = bf16[128,1152]{1,0:T(8,128)(2,1)} collective-permute-done((bf16[128,1152]{1,0:T(8,128)(2,1)S(1)}, bf16[128,1152]{1,0:T(8,128)(2,1)}, u32[]{:S(2)}, u32[]{:S(2)}) %collective-permute-start.18) | collective-permute-done | bytes 294944 | tf_op jit(solution)/shard_map/ppermute | solution.py:47
  118.3 2.3 pad_maximum_fusion
  120.6 4.4 collective-permute-done.16
  133.6 4.3 collective-permute-done.21
  142.0 17.9 %all-gather.5.cloned.1.call-done = bf16[2,1152,1152]{2,1,0:T(8,128)(2,1)} async-done(((bf16[2,144,1152]{2,1,0:T(8,128)(2,1)}), bf16[2,1152,1152]{2,1,0:T(8,128)(2,1)}) %all-gather.5.cloned.1.call-update) | async-done | bytes 5308432 | tf_op jit(solution)/shard_map/all_gather | solution.py:363
  159.9 4.2 multiply_convert_fusion.1
  164.1 2.9 fusion.139
  167.0 3.0 convolution_convert_fusion.1
  181.8 7.6 %collective-permute-done.24 = bf16[1,128,1152]{2,1,0:T(8,128)(2,1)S(1)} collective-permute-done((bf16[1,128,1152]{2,1,0:T(8,128)(2,1)S(1)}, bf16[1,128,1152]{2,1,0:T(8,128)(2,1)S(1)}, u32[]{:S(2)}, u32[]{:S(2)}) %collective-permute-start.24) | collective-permute-done | bytes 294944 | tf_op jit(solution)/shard_map/ppermute | solution.py:47
  195.8 5.7 %collective-permute-done.28 = bf16[128,1152]{1,0:T(8,128)(2,1)S(1)} collective-permute-done((bf16[128,1152]{1,0:T(8,128)(2,1)S(1)}, bf16[128,1152]{1,0:T(8,128)(2,1)S(1)}, u32[]{:S(2)}, u32[]{:S(2)}) %collective-permute-start.28) | collective-permute-done | bytes 294944 | tf_op jit(solution)/shard_map/ppermute | solution.py:47
  201.5 5.8 %collective-permute-done.58 = bf16[4,144,1152]{2,1,0:T(8,128)(2,1)S(1)} collective-permute-done((bf16[4,144,1152]{2,1,0:T(8,128)(2,1)S(1)}, bf16[4,144,1152]{2,1,0:T(8,128)(2,1)S(1)}, u32[]{:S(2)}, u32[]{:S(2)}) %collective-permute-start.58) | collective-permute-done | bytes 1327136 | tf_op jit(solution)/shard_map/ppermute | solution.py:47
  212.2 2.3 collective-permute-start.59
  214.5 20.2 %collective-permute-done.65 = bf16[4,144,1152]{2,1,0:T(8,128)(2,1)S(1)} collective-permute-done((bf16[4,144,1152]{2,1,0:T(8,128)(2,1)S(1)}, bf16[4,144,1152]{2,1,0:T(8,128)(2,1)S(1)}, u32[]{:S(2)}, u32[]{:S(2)}) %collective-permute-start.65) | collective-permute-done | bytes 1327136 | tf_op jit(solution)/shard_map/ppermute | solution.py:47
  241.6 2.5 shard_map.231
  246.2 3.2 convolution_convert_fusion.5
  253.2 3.0 convolution_convert_fusion.2
  262.6 3.1 dynamic-slice_bitcast_fusion.2
  270.8 2.3 collective-permute-start.66
  276.7 9.9 %collective-permute-done.67 = bf16[144,1152]{1,0:T(8,128)(2,1)S(1)} collective-permute-done((bf16[144,1152]{1,0:T(8,128)(2,1)S(1)}, bf16[144,1152]{1,0:T(8,128)(2,1)S(1)}, u32[]{:S(2)}, u32[]{:S(2)}) %collective-permute-start.67) | collective-permute-done | bytes 331808 | tf_op jit(solution)/shard_map/ppermute | solution.py:47
  301.7 8.0 %collective-permute-done.50 = bf16[2,288,288]{2,1,0:T(8,128)(2,1)} collective-permute-done((bf16[2,288,288]{2,1,0:T(8,128)(2,1)}, bf16[2,288,288]{2,1,0:T(8,128)(2,1)}, u32[]{:S(2)}, u32[]{:S(2)}) %collective-permute-start.50) | collective-permute-done | bytes 331808 | tf_op jit(solution)/shard_map/ppermute | solution.py:47
  311.6 2.4 shard_map.233
  329.4 3.5 shard_map.235
  333.0 3.1 shard_map.236
  338.5 2.5 collective-permute-done.33
  341.7 21.8 %collective-permute-done.36 = bf16[1,16128]{1,0:T(2,128)(2,1)S(1)} collective-permute-done((bf16[1,16128]{1,0:T(2,128)(2,1)S(1)}, bf16[1,16128]{1,0:T(2,128)(2,1)S(1)}, u32[]{:S(2)}, u32[]{:S(2)}) %collective-permute-start.36) | collective-permute-done | bytes 32288 | tf_op jit(solution)/shard_map/ppermute | solution.py:47
  373.6 8.5 %collective-permute-done.53 = bf16[144,288]{1,0:T(8,128)(2,1)S(1)} collective-permute-done((bf16[144,288]{1,0:T(8,128)(2,1)S(1)}, bf16[144,288]{1,0:T(8,128)(2,1)S(1)}, u32[]{:S(2)}, u32[]{:S(2)}) %collective-permute-start.53) | collective-permute-done | bytes 82976 | tf_op jit(solution)/shard_map/ppermute | solution.py:47
  388.0 3.5 convolution_bitcast_fusion
  398.4 3.1 collective-permute-start.41
  402.1 6.0 %collective-permute-done.41 = f32[2,1152]{1,0:T(2,128)S(1)} collective-permute-done((f32[2,1152]{1,0:T(2,128)S(1)}, f32[2,1152]{1,0:T(2,128)S(1)}, u32[]{:S(2)}, u32[]{:S(2)}) %collective-permute-start.41) | collective-permute-done | bytes 9248 | tf_op jit(solution)/shard_map/ppermute | solution.py:47
  408.1 2.5 collective-permute-start.43
  410.6 4.1 collective-permute-start.42
  414.8 3.7 collective-permute-done.44
  418.5 3.8 collective-permute-done.43
  424.3 5.3 %collective-permute-done.47.refs_2_ = bf16[144,896]{1,0:T(8,128)(2,1)S(1)} collective-permute-done((bf16[144,896]{1,0:T(8,128)(2,1)S(1)}, bf16[144,896]{1,0:T(8,128)(2,1)S(1)}, u32[]{:S(2)}, u32[]{:S(2)}) %collective-permute-start.47) | collective-permute-done | bytes 258080 | tf_op jit(solution)/shard_map/ppermute | solution.py:47
  435.1 3.0 shard_map.232
  (446 shorter events, 179.5 us)
Async XLA Ops:
  7.2 82.8 %all-gather.3.cloned.1.call-start = ((), (), s32[]{:S(2)}) async-start(), calls=%async_computation | async-start | bytes 2322432 | tf_op jit(solution)/shard_map/all_gather | solution.py:337
  14.2 145.7 %all-gather.5.cloned.1.call-start = ((), (), s32[]{:S(2)}) async-start(), calls=%async_computation.1 | async-start | bytes 5971968 | tf_op jit(solution)/shard_map/all_gather | solution.py:363
  43.1 11.1 %collective-permute-start.9 = (bf16[144,288]{1,0:T(8,128)(2,1)S(1)}, bf16[144,288]{1,0:T(8,128)(2,1)S(1)}, u32[]{:S(2)}, u32[]{:S(2)}) collective-permute-start(bf16[144,288]{1,0:T(8,128)(2,1)S(1)} %copy-done.38), channel_id=1, source_target_pairs={{0,2},{1,3},{2,0},{3,1},{4,6},{5,7},{6,4},{7,5},{8,10},{9,11},{10,... | collective-permute-start | bytes 248840 | tf_op jit(solution)/shard_map/ppermute | solution.py:47
  45.0 15.5 %collective-permute-start.10 = (bf16[144,288]{1,0:T(8,128)(2,1)S(1)}, bf16[144,288]{1,0:T(8,128)(2,1)S(1)}, u32[]{:S(2)}, u32[]{:S(2)}) collective-permute-start(bf16[144,288]{1,0:T(8,128)(2,1)S(1)} %copy-done.38), channel_id=1, source_target_pairs={{0,4},{1,5},{2,6},{3,7},{4,0},{5,1},{6,2},{7,3},{8,12},{9,13},{10,... | collective-permute-start | bytes 248840 | tf_op jit(solution)/shard_map/ppermute | solution.py:47
  48.0 12.6 %collective-permute-start.11 = (bf16[144,288]{1,0:T(8,128)(2,1)S(1)}, bf16[144,288]{1,0:T(8,128)(2,1)S(1)}, u32[]{:S(2)}, u32[]{:S(2)}) collective-permute-start(bf16[144,288]{1,0:T(8,128)(2,1)S(1)} %copy-done.38), channel_id=1, source_target_pairs={{0,6},{1,7},{2,4},{3,5},{4,2},{5,3},{6,0},{7,1},{8,14},{9,15},{10,... | collective-permute-start | bytes 248840 | tf_op jit(solution)/shard_map/ppermute | solution.py:47
  61.9 10.9 %collective-permute-start.6 = (bf16[128,1152]{1,0:T(8,128)(2,1)}, bf16[128,1152]{1,0:T(8,128)(2,1)}, u32[]{:S(2)}, u32[]{:S(2)}) collective-permute-start(bf16[128,1152]{1,0:T(8,128)(2,1)} %fusion.45), channel_id=1, source_target_pairs={{0,8},{8,0},{16,24},{24,16},{1,9},{9,1},{17,25},{25,17},{2,10},{10... | collective-permute-start | bytes 884744 | tf_op jit(solution)/shard_map/ppermute | solution.py:47
  62.0 10.3 %collective-permute-start.7 = (bf16[128,1152]{1,0:T(8,128)(2,1)}, bf16[128,1152]{1,0:T(8,128)(2,1)}, u32[]{:S(2)}, u32[]{:S(2)}) collective-permute-start(bf16[128,1152]{1,0:T(8,128)(2,1)} %fusion.45), channel_id=1, source_target_pairs={{0,16},{8,24},{16,0},{24,8},{1,17},{9,25},{17,1},{25,9},{2,18},{10... | collective-permute-start | bytes 884744 | tf_op jit(solution)/shard_map/ppermute | solution.py:47
  74.7 12.2 %collective-permute-start.14 = (bf16[2,288,288]{2,1,0:T(8,128)(2,1)S(1)}, bf16[2,288,288]{2,1,0:T(8,128)(2,1)S(1)}, u32[]{:S(2)}, u32[]{:S(2)}) collective-permute-start(bf16[2,288,288]{2,1,0:T(8,128)(2,1)S(1)} %pad_maximum_fusion.3), channel_id=1, source_target_pairs={{0,16},{8,24},{16,0},{24,8},{1,17},{9,25},{17,1},{25,9},{2,18},{10... | collective-permute-start | bytes 995336 | tf_op jit(solution)/shard_map/ppermute | solution.py:47
  102.5 9.5 %collective-permute-start.15 = (bf16[2,128,1152]{2,1,0:T(8,128)(2,1)}, bf16[2,128,1152]{2,1,0:T(8,128)(2,1)}, u32[]{:S(2)}, u32[]{:S(2)}) collective-permute-start(bf16[2,128,1152]{2,1,0:T(8,128)(2,1)} %fusion.60), channel_id=1, source_target_pairs={{0,8},{8,0},{16,24},{24,16},{1,9},{9,1},{17,25},{25,17},{2,10},{10... | collective-permute-start | bytes 1769480 | tf_op jit(solution)/shard_map/ppermute | solution.py:47
  103.9 14.4 %collective-permute-start.17 = (bf16[128,1152]{1,0:T(8,128)(2,1)S(1)}, bf16[128,1152]{1,0:T(8,128)(2,1)}, u32[]{:S(2)}, u32[]{:S(2)}) collective-permute-start(bf16[128,1152]{1,0:T(8,128)(2,1)S(1)} %copy-done.26), channel_id=1, source_target_pairs={{0,8},{8,0},{16,24},{24,16},{1,9},{9,1},{17,25},{25,17},{2,10},{10... | collective-permute-start | bytes 884744 | tf_op jit(solution)/shard_map/ppermute | solution.py:47
  115.5 9.6 %collective-permute-start.16 = (bf16[1,128,1152]{2,1,0:T(8,128)(2,1)}, bf16[1,128,1152]{2,1,0:T(8,128)(2,1)S(1)}, u32[]{:S(2)}, u32[]{:S(2)}) collective-permute-start(bf16[1,128,1152]{2,1,0:T(8,128)(2,1)} %fusion.80), channel_id=1, source_target_pairs={{0,16},{8,24},{16,0},{24,8},{1,17},{9,25},{17,1},{25,9},{2,18},{10... | collective-permute-start | bytes 884744 | tf_op jit(solution)/shard_map/ppermute | solution.py:47
  128.1 9.7 %collective-permute-start.20 = (bf16[128,1152]{1,0:T(8,128)(2,1)}, bf16[128,1152]{1,0:T(8,128)(2,1)}, u32[]{:S(2)}, u32[]{:S(2)}) collective-permute-start(bf16[128,1152]{1,0:T(8,128)(2,1)} %add_convert_fusion), channel_id=1, source_target_pairs={{0,8},{8,0},{16,24},{24,16},{1,9},{9,1},{17,25},{25,17},{2,10},{10... | collective-permute-start | bytes 884744 | tf_op jit(solution)/shard_map/ppermute | solution.py:47
  128.1 9.7 %collective-permute-start.21 = (bf16[128,1152]{1,0:T(8,128)(2,1)}, bf16[128,1152]{1,0:T(8,128)(2,1)}, u32[]{:S(2)}, u32[]{:S(2)}) collective-permute-start(bf16[128,1152]{1,0:T(8,128)(2,1)} %add_convert_fusion), channel_id=1, source_target_pairs={{0,16},{8,24},{16,0},{24,8},{1,17},{9,25},{17,1},{25,9},{2,18},{10... | collective-permute-start | bytes 884744 | tf_op jit(solution)/shard_map/ppermute | solution.py:47
  175.2 32.1 %collective-permute-start.58 = (bf16[4,144,1152]{2,1,0:T(8,128)(2,1)S(1)}, bf16[4,144,1152]{2,1,0:T(8,128)(2,1)S(1)}, u32[]{:S(2)}, u32[]{:S(2)}) collective-permute-start(bf16[4,144,1152]{2,1,0:T(8,128)(2,1)S(1)} %dynamic-slice_bitcast_fusion.1), channel_id=1, source_target_pairs={{0,1},{1,0},{2,3},{3,2},{4,5},{5,4},{6,7},{7,6},{8,9},{9,8},{10,11... | collective-permute-start | bytes 3981320 | tf_op jit(solution)/shard_map/ppermute | solution.py:47
  177.7 57.1 %collective-permute-start.65 = (bf16[4,144,1152]{2,1,0:T(8,128)(2,1)S(1)}, bf16[4,144,1152]{2,1,0:T(8,128)(2,1)S(1)}, u32[]{:S(2)}, u32[]{:S(2)}) collective-permute-start(bf16[4,144,1152]{2,1,0:T(8,128)(2,1)S(1)} %dynamic-slice_bitcast_fusion), channel_id=1, source_target_pairs={{0,1},{1,0},{2,3},{3,2},{4,5},{5,4},{6,7},{7,6},{8,9},{9,8},{10,11... | collective-permute-start | bytes 3981320 | tf_op jit(solution)/shard_map/ppermute | solution.py:47
  179.4 9.9 %collective-permute-start.24 = (bf16[1,128,1152]{2,1,0:T(8,128)(2,1)S(1)}, bf16[1,128,1152]{2,1,0:T(8,128)(2,1)S(1)}, u32[]{:S(2)}, u32[]{:S(2)}) collective-permute-start(bf16[1,128,1152]{2,1,0:T(8,128)(2,1)S(1)} %fusion.81), channel_id=1, source_target_pairs={{0,16},{8,24},{16,0},{24,8},{1,17},{9,25},{17,1},{25,9},{2,18},{10... | collective-permute-start | bytes 884744 | tf_op jit(solution)/shard_map/ppermute | solution.py:47
  181.1 13.0 %collective-permute-start.26 = (bf16[1,128,1152]{2,1,0:T(8,128)(2,1)S(1)}, bf16[1,128,1152]{2,1,0:T(8,128)(2,1)S(1)}, u32[]{:S(2)}, u32[]{:S(2)}) collective-permute-start(bf16[1,128,1152]{2,1,0:T(8,128)(2,1)S(1)} %fusion.82), channel_id=1, source_target_pairs={{0,16},{8,24},{16,0},{24,8},{1,17},{9,25},{17,1},{25,9},{2,18},{10... | collective-permute-start | bytes 884744 | tf_op jit(solution)/shard_map/ppermute | solution.py:47
  201.4 37.6 %collective-permute-start.29 = (bf16[128,1152]{1,0:T(8,128)(2,1)S(1)}, bf16[128,1152]{1,0:T(8,128)(2,1)S(1)}, u32[]{:S(2)}, u32[]{:S(2)}) collective-permute-start(bf16[128,1152]{1,0:T(8,128)(2,1)S(1)} %collective-permute-done.28), channel_id=1, source_target_pairs={{0,8},{8,0},{16,24},{24,16},{1,9},{9,1},{17,25},{25,17},{2,10},{10... | collective-permute-start | bytes 884744 | tf_op jit(solution)/shard_map/ppermute | solution.py:47
  210.1 60.6 %collective-permute-start.61 = (bf16[144,1152]{1,0:T(8,128)(2,1)}, bf16[144,1152]{1,0:T(8,128)(2,1)S(1)}, u32[]{:S(2)}, u32[]{:S(2)}) collective-permute-start(bf16[144,1152]{1,0:T(8,128)(2,1)} %get-tuple-element.90), channel_id=1, source_target_pairs={{0,6},{1,7},{2,4},{3,5},{4,2},{5,3},{6,0},{7,1},{8,14},{9,15},{10,... | collective-permute-start | bytes 995336 | tf_op jit(solution)/shard_map/ppermute | solution.py:47
  211.6 61.5 %collective-permute-start.60 = (bf16[144,1152]{1,0:T(8,128)(2,1)}, bf16[144,1152]{1,0:T(8,128)(2,1)}, u32[]{:S(2)}, u32[]{:S(2)}) collective-permute-start(bf16[144,1152]{1,0:T(8,128)(2,1)} %get-tuple-element.91), channel_id=1, source_target_pairs={{0,4},{1,5},{2,6},{3,7},{4,0},{5,1},{6,2},{7,3},{8,12},{9,13},{10,... | collective-permute-start | bytes 995336 | tf_op jit(solution)/shard_map/ppermute | solution.py:47
  212.2 60.9 %collective-permute-start.59 = (bf16[144,1152]{1,0:T(8,128)(2,1)}, bf16[144,1152]{1,0:T(8,128)(2,1)}, u32[]{:S(2)}, u32[]{:S(2)}) collective-permute-start(bf16[144,1152]{1,0:T(8,128)(2,1)} %get-tuple-element.89), channel_id=1, source_target_pairs={{0,2},{1,3},{2,0},{3,1},{4,6},{5,7},{6,4},{7,5},{8,10},{9,11},{10,... | collective-permute-start | bytes 995336 | tf_op jit(solution)/shard_map/ppermute | solution.py:47
  237.6 37.6 %collective-permute-start.68 = (bf16[144,1152]{1,0:T(8,128)(2,1)}, bf16[144,1152]{1,0:T(8,128)(2,1)}, u32[]{:S(2)}, u32[]{:S(2)}) collective-permute-start(bf16[144,1152]{1,0:T(8,128)(2,1)} %get-tuple-element.87), channel_id=1, source_target_pairs={{0,6},{1,7},{2,4},{3,5},{4,2},{5,3},{6,0},{7,1},{8,14},{9,15},{10,... | collective-permute-start | bytes 995336 | tf_op jit(solution)/shard_map/ppermute | solution.py:47
  269.5 17.2 %collective-permute-start.67 = (bf16[144,1152]{1,0:T(8,128)(2,1)S(1)}, bf16[144,1152]{1,0:T(8,128)(2,1)S(1)}, u32[]{:S(2)}, u32[]{:S(2)}) collective-permute-start(bf16[144,1152]{1,0:T(8,128)(2,1)S(1)} %copy-done.32), channel_id=1, source_target_pairs={{0,4},{1,5},{2,6},{3,7},{4,0},{5,1},{6,2},{7,3},{8,12},{9,13},{10,... | collective-permute-start | bytes 995336 | tf_op jit(solution)/shard_map/ppermute | solution.py:47
  270.8 16.4 %collective-permute-start.66 = (bf16[144,1152]{1,0:T(8,128)(2,1)S(1)}, bf16[144,1152]{1,0:T(8,128)(2,1)S(1)}, u32[]{:S(2)}, u32[]{:S(2)}) collective-permute-start(bf16[144,1152]{1,0:T(8,128)(2,1)S(1)} %copy-done.31), channel_id=1, source_target_pairs={{0,2},{1,3},{2,0},{3,1},{4,6},{5,7},{6,4},{7,5},{8,10},{9,11},{10,... | collective-permute-start | bytes 995336 | tf_op jit(solution)/shard_map/ppermute | solution.py:47
  273.1 19.8 %collective-permute-start.30 = (bf16[2,128,1152]{2,1,0:T(8,128)(2,1)}, bf16[2,128,1152]{2,1,0:T(8,128)(2,1)S(1)}, u32[]{:S(2)}, u32[]{:S(2)}) collective-permute-start(bf16[2,128,1152]{2,1,0:T(8,128)(2,1)} %fusion.63), channel_id=1, source_target_pairs={{0,8},{8,0},{16,24},{24,16},{1,9},{9,1},{17,25},{25,17},{2,10},{10... | collective-permute-start | bytes 1769480 | tf_op jit(solution)/shard_map/ppermute | solution.py:47
  273.1 17.6 %collective-permute-start.49 = (bf16[2,288,288]{2,1,0:T(8,128)(2,1)S(1)}, bf16[2,288,288]{2,1,0:T(8,128)(2,1)S(1)}, u32[]{:S(2)}, u32[]{:S(2)}) collective-permute-start(bf16[2,288,288]{2,1,0:T(8,128)(2,1)S(1)} %pad_maximum_fusion.4), channel_id=1, source_target_pairs={{0,8},{8,0},{16,24},{24,16},{1,9},{9,1},{17,25},{25,17},{2,10},{10... | collective-permute-start | bytes 995336 | tf_op jit(solution)/shard_map/ppermute | solution.py:47
  275.2 25.9 %collective-permute-start.63 = (bf16[144,1152]{1,0:T(8,128)(2,1)S(1)}, bf16[144,1152]{1,0:T(8,128)(2,1)}, u32[]{:S(2)}, u32[]{:S(2)}) collective-permute-start(bf16[144,1152]{1,0:T(8,128)(2,1)S(1)} %fusion.43.refs_0_), channel_id=1, source_target_pairs={{0,16},{8,24},{16,0},{24,8},{1,17},{9,25},{17,1},{25,9},{2,18},{10... | collective-permute-start | bytes 995336 | tf_op jit(solution)/shard_map/ppermute | solution.py:47
  289.3 12.4 %collective-permute-start.70 = (bf16[144,1152]{1,0:T(8,128)(2,1)}, bf16[144,1152]{1,0:T(8,128)(2,1)}, u32[]{:S(2)}, u32[]{:S(2)}) collective-permute-start(bf16[144,1152]{1,0:T(8,128)(2,1)} %fusion.40.refs_0_), channel_id=1, source_target_pairs={{0,16},{8,24},{16,0},{24,8},{1,17},{9,25},{17,1},{25,9},{2,18},{10... | collective-permute-start | bytes 995336 | tf_op jit(solution)/shard_map/ppermute | solution.py:47
  292.3 17.4 %collective-permute-start.50 = (bf16[2,288,288]{2,1,0:T(8,128)(2,1)}, bf16[2,288,288]{2,1,0:T(8,128)(2,1)}, u32[]{:S(2)}, u32[]{:S(2)}) collective-permute-start(bf16[2,288,288]{2,1,0:T(8,128)(2,1)} %pad_maximum_fusion.5), channel_id=1, source_target_pairs={{0,16},{8,24},{16,0},{24,8},{1,17},{9,25},{17,1},{25,9},{2,18},{10... | collective-permute-start | bytes 995336 | tf_op jit(solution)/shard_map/ppermute | solution.py:47
  294.8 19.7 %collective-permute-start.31 = (bf16[1,128,1152]{2,1,0:T(8,128)(2,1)}, bf16[1,128,1152]{2,1,0:T(8,128)(2,1)S(1)}, u32[]{:S(2)}, u32[]{:S(2)}) collective-permute-start(bf16[1,128,1152]{2,1,0:T(8,128)(2,1)} %fusion.83), channel_id=1, source_target_pairs={{0,16},{8,24},{16,0},{24,8},{1,17},{9,25},{17,1},{25,9},{2,18},{10... | collective-permute-start | bytes 884744 | tf_op jit(solution)/shard_map/ppermute | solution.py:47
  301.2 26.3 %collective-permute-start.62 = (bf16[144,1152]{1,0:T(8,128)(2,1)S(1)}, bf16[144,1152]{1,0:T(8,128)(2,1)}, u32[]{:S(2)}, u32[]{:S(2)}) collective-permute-start(bf16[144,1152]{1,0:T(8,128)(2,1)S(1)} %fusion.43.refs_0_), channel_id=1, source_target_pairs={{0,8},{8,0},{16,24},{24,16},{1,9},{9,1},{17,25},{25,17},{2,10},{10... | collective-permute-start | bytes 995336 | tf_op jit(solution)/shard_map/ppermute | solution.py:47
  301.2 31.8 %collective-permute-start.69 = (bf16[144,1152]{1,0:T(8,128)(2,1)}, bf16[144,1152]{1,0:T(8,128)(2,1)}, u32[]{:S(2)}, u32[]{:S(2)}) collective-permute-start(bf16[144,1152]{1,0:T(8,128)(2,1)} %fusion.40.refs_0_), channel_id=1, source_target_pairs={{0,8},{8,0},{16,24},{24,16},{1,9},{9,1},{17,25},{25,17},{2,10},{10... | collective-permute-start | bytes 995336 | tf_op jit(solution)/shard_map/ppermute | solution.py:47
  301.7 26.3 %collective-permute-start.64 = (bf16[144,1152]{1,0:T(8,128)(2,1)}, bf16[144,1152]{1,0:T(8,128)(2,1)}, u32[]{:S(2)}, u32[]{:S(2)}) collective-permute-start(bf16[144,1152]{1,0:T(8,128)(2,1)} %collective-permute-done.63.refs_2_), channel_id=1, source_target_pairs={{0,8},{8,0},{16,24},{24,16},{1,9},{9,1},{17,25},{25,17},{2,10},{10... | collective-permute-start | bytes 995336 | tf_op jit(solution)/shard_map/ppermute | solution.py:47
  309.8 23.2 %collective-permute-start.71 = (bf16[144,1152]{1,0:T(8,128)(2,1)}, bf16[144,1152]{1,0:T(8,128)(2,1)}, u32[]{:S(2)}, u32[]{:S(2)}) collective-permute-start(bf16[144,1152]{1,0:T(8,128)(2,1)} %collective-permute-done.70.refs_2_), channel_id=1, source_target_pairs={{0,8},{8,0},{16,24},{24,16},{1,9},{9,1},{17,25},{25,17},{2,10},{10... | collective-permute-start | bytes 995336 | tf_op jit(solution)/shard_map/ppermute | solution.py:47
  326.4 9.7 %collective-permute-start.32 = (f32[1,9216]{1,0:T(1,128)}, f32[1,9216]{1,0:T(1,128)}, u32[]{:S(2)}, u32[]{:S(2)}) collective-permute-start(f32[1,9216]{1,0:T(1,128)} %constant_dynamic-update-slice_fusion.12), channel_id=1, source_target_pairs={{0,8},{8,0},{16,24},{24,16},{1,9},{9,1},{17,25},{25,17},{2,10},{10... | collective-permute-start | bytes 110600 | tf_op jit(solution)/shard_map/ppermute | solution.py:47
  327.4 60.0 %collective-permute-start.39 = (bf16[4,144,896]{2,1,0:T(8,128)(2,1)}, bf16[4,144,896]{2,1,0:T(8,128)(2,1)}, u32[]{:S(2)}, u32[]{:S(2)}) collective-permute-start(bf16[4,144,896]{2,1,0:T(8,128)(2,1)} %get-tuple-element.82), channel_id=1, source_target_pairs={{0,1},{1,0},{2,3},{3,2},{4,5},{5,4},{6,7},{7,6},{8,9},{9,8},{10,11... | collective-permute-start | bytes 3096584 | tf_op jit(solution)/shard_map/ppermute | solution.py:47
  328.0 36.3 %collective-permute-start.51 = (bf16[4,144,288]{2,1,0:T(8,128)(2,1)}, bf16[4,144,288]{2,1,0:T(8,128)(2,1)}, u32[]{:S(2)}, u32[]{:S(2)}) collective-permute-start(bf16[4,144,288]{2,1,0:T(8,128)(2,1)} %dynamic-slice_bitcast_fusion.4), channel_id=1, source_target_pairs={{0,1},{1,0},{2,3},{3,2},{4,5},{5,4},{6,7},{7,6},{8,9},{9,8},{10,11... | collective-permute-start | bytes 995336 | tf_op jit(solution)/shard_map/ppermute | solution.py:47
  341.1 22.4 %collective-permute-start.36 = (bf16[1,16128]{1,0:T(2,128)(2,1)S(1)}, bf16[1,16128]{1,0:T(2,128)(2,1)S(1)}, u32[]{:S(2)}, u32[]{:S(2)}) collective-permute-start(bf16[1,16128]{1,0:T(2,128)(2,1)S(1)} %pad_maximum_fusion.8), channel_id=1, source_target_pairs={{0,1},{1,0},{2,3},{3,2},{4,5},{5,4},{6,7},{7,6},{8,9},{9,8},{10,11... | collective-permute-start | bytes 96776 | tf_op jit(solution)/shard_map/ppermute | solution.py:47
  367.4 14.6 %collective-permute-start.53 = (bf16[144,288]{1,0:T(8,128)(2,1)S(1)}, bf16[144,288]{1,0:T(8,128)(2,1)S(1)}, u32[]{:S(2)}, u32[]{:S(2)}) collective-permute-start(bf16[144,288]{1,0:T(8,128)(2,1)S(1)} %get-tuple-element.109), channel_id=1, source_target_pairs={{0,4},{1,5},{2,6},{3,7},{4,0},{5,1},{6,2},{7,3},{8,12},{9,13},{10,... | collective-permute-start | bytes 248840 | tf_op jit(solution)/shard_map/ppermute | solution.py:47
  369.1 12.9 %collective-permute-start.52 = (bf16[144,288]{1,0:T(8,128)(2,1)S(1)}, bf16[144,288]{1,0:T(8,128)(2,1)S(1)}, u32[]{:S(2)}, u32[]{:S(2)}) collective-permute-start(bf16[144,288]{1,0:T(8,128)(2,1)S(1)} %get-tuple-element.107), channel_id=1, source_target_pairs={{0,2},{1,3},{2,0},{3,1},{4,6},{5,7},{6,4},{7,5},{8,10},{9,11},{10,... | collective-permute-start | bytes 248840 | tf_op jit(solution)/shard_map/ppermute | solution.py:47
  370.6 16.5 %collective-permute-start.38 = (bf16[4,16128]{1,0:T(4,128)(2,1)S(1)}, bf16[4,16128]{1,0:T(4,128)(2,1)S(1)}, u32[]{:S(2)}, u32[]{:S(2)}) collective-permute-start(bf16[4,16128]{1,0:T(4,128)(2,1)S(1)} %pad_maximum_fusion.7), channel_id=1, source_target_pairs={{0,4},{1,5},{2,6},{3,7},{4,0},{5,1},{6,2},{7,3},{8,12},{9,13},{10,... | collective-permute-start | bytes 387080 | tf_op jit(solution)/shard_map/ppermute | solution.py:47
  385.1 45.2 %collective-permute-start.55 = (bf16[144,288]{1,0:T(8,128)(2,1)S(1)}, bf16[144,288]{1,0:T(8,128)(2,1)S(1)}, u32[]{:S(2)}, u32[]{:S(2)}) collective-permute-start(bf16[144,288]{1,0:T(8,128)(2,1)S(1)} %fusion.88.refs_0_), channel_id=1, source_target_pairs={{0,8},{8,0},{16,24},{24,16},{1,9},{9,1},{17,25},{25,17},{2,10},{10... | collective-permute-start | bytes 248840 | tf_op jit(solution)/shard_map/ppermute | solution.py:47
  387.1 43.2 %collective-permute-start.57 = (bf16[144,288]{1,0:T(8,128)(2,1)}, bf16[144,288]{1,0:T(8,128)(2,1)S(1)}, u32[]{:S(2)}, u32[]{:S(2)}) collective-permute-start(bf16[144,288]{1,0:T(8,128)(2,1)} %collective-permute-done.56.refs_2_), channel_id=1, source_target_pairs={{0,8},{8,0},{16,24},{24,16},{1,9},{9,1},{17,25},{25,17},{2,10},{10... | collective-permute-start | bytes 248840 | tf_op jit(solution)/shard_map/ppermute | solution.py:47
  395.0 15.6 %collective-permute-start.45 = (bf16[144,896]{1,0:T(8,128)(2,1)S(1)}, bf16[144,896]{1,0:T(8,128)(2,1)S(1)}, u32[]{:S(2)}, u32[]{:S(2)}) collective-permute-start(bf16[144,896]{1,0:T(8,128)(2,1)S(1)} %get-tuple-element.93), channel_id=1, source_target_pairs={{0,6},{1,7},{2,4},{3,5},{4,2},{5,3},{6,0},{7,1},{8,14},{9,15},{10,... | collective-permute-start | bytes 774152 | tf_op jit(solution)/shard_map/ppermute | solution.py:47
  396.4 22.0 %collective-permute-start.44 = (bf16[144,896]{1,0:T(8,128)(2,1)S(1)}, bf16[144,896]{1,0:T(8,128)(2,1)S(1)}, u32[]{:S(2)}, u32[]{:S(2)}) collective-permute-start(bf16[144,896]{1,0:T(8,128)(2,1)S(1)} %get-tuple-element.94), channel_id=1, source_target_pairs={{0,4},{1,5},{2,6},{3,7},{4,0},{5,1},{6,2},{7,3},{8,12},{9,13},{10,... | collective-permute-start | bytes 774152 | tf_op jit(solution)/shard_map/ppermute | solution.py:47
  398.4 9.7 %collective-permute-start.41 = (f32[2,1152]{1,0:T(2,128)S(1)}, f32[2,1152]{1,0:T(2,128)S(1)}, u32[]{:S(2)}, u32[]{:S(2)}) collective-permute-start(f32[2,1152]{1,0:T(2,128)S(1)} %pad_maximum_fusion.16), channel_id=1, source_target_pairs={{0,2},{1,3},{2,0},{3,1},{4,6},{5,7},{6,4},{7,5},{8,10},{9,11},{10,... | collective-permute-start | bytes 27656 | tf_op jit(solution)/shard_map/ppermute | solution.py:47
  408.1 14.2 %collective-permute-start.43 = (bf16[144,896]{1,0:T(8,128)(2,1)S(1)}, bf16[144,896]{1,0:T(8,128)(2,1)S(1)}, u32[]{:S(2)}, u32[]{:S(2)}) collective-permute-start(bf16[144,896]{1,0:T(8,128)(2,1)S(1)} %get-tuple-element.92), channel_id=1, source_target_pairs={{0,2},{1,3},{2,0},{3,1},{4,6},{5,7},{6,4},{7,5},{8,10},{9,11},{10,... | collective-permute-start | bytes 774152 | tf_op jit(solution)/shard_map/ppermute | solution.py:47
  410.6 13.3 %collective-permute-start.42 = (f32[4,1152]{1,0:T(4,128)S(1)}, f32[4,1152]{1,0:T(4,128)S(1)}, u32[]{:S(2)}, u32[]{:S(2)}) collective-permute-start(f32[4,1152]{1,0:T(4,128)S(1)} %pad_maximum_fusion.13), channel_id=1, source_target_pairs={{0,4},{1,5},{2,6},{3,7},{4,0},{5,1},{6,2},{7,3},{8,12},{9,13},{10,... | collective-permute-start | bytes 55304 | tf_op jit(solution)/shard_map/ppermute | solution.py:47
  (93 other events, 826.5 us)
Sparse Core Ops, SparseCore 0:
  14.3 56.6 all-gather.2
  73.8 86.0 all-gather.4
